TPU v7x, 32 devices: a whole 2x2x4 slice. The times are simulated.
32 devices in a mesh: dp: 8 (over y, x, core), blk: 4 (over z).
Axes of the slice: x: 2, y: 2, z: 4, core: 2. Of those that a mesh axis runs over, the one named last changes fastest.
Arguments:
- tokens: bfloat16 [24, 1024, 1024], P('dp', 'blk'), may hold values from -6 to 6
- cotangent: bfloat16 [24, 1024, 1024], P('dp', 'blk'), may hold values from -6 to 6
- domain_ids: int32 [24, 1024], P('dp', 'blk'), may hold values from 0 to 21
- domain_weight: float32 [22], replicated, may hold values from 0.3 to 3
- frozen_input_weights: bfloat16 [1024, 8192], P('dp'), may hold values from -0.1875 to 0.1875
- bias_in: bfloat16 [8192], replicated, may hold values from -1.25 to 1.25
- frozen_down_weight: bfloat16 [4096, 1024], P('dp'), may hold values from -0.09375 to 0.09375
- bias_ff: bfloat16 [1024], replicated, may hold values from -1.25 to 1.25
- norm_gain: float32 [2, 1024], replicated, may hold values from 0.5 to 1.5
- norm_shift: float32 [2, 1024], replicated, may hold values from -1.25 to 1.25
- adapt_a: float32 [1024, 384], P('dp'), may hold values from -0.1875 to 0.1875
- adapt_a_ff: float32 [4096, 128], P('dp'), may hold values from -0.09375 to 0.09375
- adapt_b: float32 [128, 8192], P(None, 'dp'), may hold values from -0.5 to 0.5
- adapt_b_ff: float32 [128, 1024], P(None, 'dp'), may hold values from -0.5 to 0.5
- mean_a: float32 [1024, 384], P('dp'), may hold values from -192 to 192
- mean_a_ff: float32 [4096, 128], P('dp'), may hold values from -192 to 192
- mean_b: float32 [128, 8192], P(None, 'dp'), may hold values from -192 to 192
- mean_b_ff: float32 [128, 1024], P(None, 'dp'), may hold values from -192 to 192
- square_a: float32 [1024, 384], P('dp'), may hold values from 100 to 100000
- square_a_ff: float32 [4096, 128], P('dp'), may hold values from 100 to 100000
- square_b: float32 [128, 8192], P(None, 'dp'), may hold values from 100 to 100000
- square_b_ff: float32 [128, 1024], P(None, 'dp'), may hold values from 100 to 100000
- keep_a: int32 [1024, 384], P('dp'), may hold values 0 or 1
- keep_a_ff: int32 [4096, 128], P('dp'), may hold values 0 or 1
- keep_b: int32 [128, 8192], P(None, 'dp'), may hold values 0 or 1
- keep_b_ff: int32 [128, 1024], P(None, 'dp'), may hold values 0 or 1
Outputs:
- mixed: bfloat16 [24, 1024, 1024], P('dp', 'blk')
- grad_tokens: bfloat16 [24, 1024, 1024], P('dp', 'blk')
- grad_gain: float32 [2, 1024], replicated
- grad_shift: float32 [2, 1024], replicated
- grad_a: float32 [1024, 384], P('dp')
- grad_a_ff: float32 [4096, 128], P('dp')
- grad_b: float32 [128, 8192], P(None, 'dp')
- grad_b_ff: float32 [128, 1024], P(None, 'dp')
- new_mean_a: float32 [1024, 384], P('dp')
- new_square_a: float32 [1024, 384], P('dp')
- new_mean_a_ff: float32 [4096, 128], P('dp')
- new_square_a_ff: float32 [4096, 128], P('dp')
- new_mean_b: float32 [128, 8192], P(None, 'dp')
- new_square_b: float32 [128, 8192], P(None, 'dp')
- new_mean_b_ff: float32 [128, 1024], P(None, 'dp')
- new_square_b_ff: float32 [128, 1024], P(None, 'dp')
- folded_input_weights: bfloat16 [1024, 8192], P('dp')
- folded_down_weight: bfloat16 [4096, 1024], P('dp')
All inputs are finite; a program needn't handle non-finite values. No bound on the sum of `keep_a` or of `keep_a_ff` or of `keep_b` or of `keep_b_ff` on one device may be relied on, other than what follows from the above.
Results may differ from a plain program's by a relative error of at most 0.025.
Values may be sent and summed in bfloat16 or wider, within the bound.
A program may use at most 320 MiB of HBM per device.

v0:
```python
import math

import jax
import jax.numpy as jnp
from jax import lax
from jax.sharding import PartitionSpec as P

HEADS = 16
ROTARY = 16
DOMAINS = 22


highest = lax.Precision.HIGHEST
adapter_scale = 0.25
rope_base = 10000.0
norm_eps = 1e-05
masked_score = -1e30
first_fix = 1.0 - (0.9**10) ** 10
second_fix = 1.0 - (0.999**10) ** 10


def matrix_product(left, right):
    return jnp.dot(left, right, preferred_element_type=jnp.float32)


def product_right_transposed(left, right):
    return lax.dot_general(
        left, right, (((1,), (1,)), ((), ())), preferred_element_type=jnp.float32
    )


def product_left_transposed(left, right):
    return lax.dot_general(
        left, right, (((0,), (0,)), ((), ())), preferred_element_type=jnp.float32
    )


def precise_product(left, right):
    return jnp.dot(left, right, precision=highest)


def layer_norm(values, gain, shift):
    centre = values - jnp.mean(values, axis=-1, keepdims=True)
    spread = jnp.mean(centre * centre, axis=-1, keepdims=True)
    return centre * lax.rsqrt(spread + norm_eps) * gain + shift


def exact_gelu(values):
    return jax.nn.gelu(values, approximate=False)


def rope_tables(positions, rotary):
    half = rotary // 2
    freqs = rope_base ** (-(jnp.arange(half, dtype=jnp.float32) * 2.0) / rotary)
    angles = positions.astype(jnp.float32)[:, None] * freqs[None, :]
    return (jnp.cos(angles), jnp.sin(angles))


def rotate(values, cosine, sine, rotary):
    half = rotary // 2
    front = values[..., :half]
    back = values[..., half:rotary]
    rest = values[..., rotary:]
    cos_b = cosine[:, None, :]
    sin_b = sine[:, None, :]
    return jnp.concatenate(
        [front * cos_b - back * sin_b, back * cos_b + front * sin_b, rest], axis=-1
    )


def project(input_rows, weight_matrix, bias_vector, down, upper_factor):
    middle_rows = matrix_product(input_rows, down).astype(jnp.bfloat16)
    return (
        matrix_product(input_rows, weight_matrix)
        + bias_vector.astype(jnp.float32)
        + adapter_scale * matrix_product(middle_rows, upper_factor),
        middle_rows,
    )


def project_back(
    output_gradient, input_rows, middle_rows, weight_matrix, bias_vector, down, upper_factor
):
    middle_gradient = (
        adapter_scale * product_right_transposed(output_gradient, upper_factor)
    ).astype(jnp.bfloat16)
    upper_gradient = adapter_scale * product_left_transposed(middle_rows, output_gradient)
    grad_down = product_left_transposed(input_rows, middle_gradient)
    grad_in = product_right_transposed(output_gradient, weight_matrix) + product_right_transposed(
        middle_gradient, down
    )
    return (grad_in, grad_down, upper_gradient)


def split_blocks(full, bias_in, bias_ff, width, rank):
    w_all, w_ff, a_all, a_ff, b_all, b_ff = full
    part_qkv = (w_all[:, : 3 * width], bias_in[: 3 * width], a_all[:, :rank], b_all[:, : 3 * width])
    part_att = (
        w_all[:, 3 * width : 4 * width],
        bias_in[3 * width : 4 * width],
        a_all[:, rank : 2 * rank],
        b_all[:, 3 * width : 4 * width],
    )
    part_up = (
        w_all[:, 4 * width :],
        bias_in[4 * width :],
        a_all[:, 2 * rank :],
        b_all[:, 4 * width :],
    )
    part_ff = (w_ff, bias_ff, a_ff, b_ff)
    return (part_qkv, part_att, part_up, part_ff)


def adam_update(param, grad, mean, square, keep):
    mean_new = 0.9 * mean + 0.1 * grad
    square_new = 0.999 * square + 0.001 * grad * grad
    fresh = param - 0.01 * (mean_new / first_fix) / (jnp.sqrt(square_new / second_fix) + 1e-08)
    kept = keep.astype(jnp.float32)
    return (fresh, mean_new * kept, square_new * kept)


def body(
    tokens,
    cotangent,
    domain_ids,
    domain_weight,
    frozen_input_weights,
    bias_in,
    frozen_down_weight,
    bias_ff,
    norm_gain,
    norm_shift,
    adapt_a,
    adapt_a_ff,
    adapt_b,
    adapt_b_ff,
    mean_a,
    mean_a_ff,
    mean_b,
    mean_b_ff,
    square_a,
    square_a_ff,
    square_b,
    square_b_ff,
    keep_a,
    keep_a_ff,
    keep_b,
    keep_b_ff,
):
    seqs, span, width = tokens.shape
    rows = seqs * span
    rank = adapt_b.shape[0]
    depth = width // HEADS
    att_scale = 1.0 / math.sqrt(depth)
    shards = (
        frozen_input_weights,
        frozen_down_weight,
        adapt_a.astype(jnp.bfloat16),
        adapt_a_ff.astype(jnp.bfloat16),
        adapt_b.astype(jnp.bfloat16),
        adapt_b_ff.astype(jnp.bfloat16),
    )
    whole = (
        lax.all_gather(shards[0], "dp", axis=0, tiled=True),
        lax.all_gather(shards[1], "dp", axis=0, tiled=True),
        lax.all_gather(shards[2], "dp", axis=0, tiled=True),
        lax.all_gather(shards[3], "dp", axis=0, tiled=True),
        lax.all_gather(shards[4], "dp", axis=1, tiled=True),
        lax.all_gather(shards[5], "dp", axis=1, tiled=True),
    )
    part_qkv, part_att, part_up, part_ff = split_blocks(whole, bias_in, bias_ff, width, rank)
    input_rows = tokens.astype(jnp.float32).reshape(rows, width)
    first_f, first_pull = jax.vjp(layer_norm, input_rows, norm_gain[0], norm_shift[0])
    second_f, second_pull = jax.vjp(layer_norm, input_rows, norm_gain[1], norm_shift[1])
    first = first_f.astype(jnp.bfloat16)
    second = second_f.astype(jnp.bfloat16)
    joint, middle_qkv = project(first, *part_qkv)
    joint3 = joint.reshape(seqs, span, 3 * width)
    positions = lax.axis_index("blk") * span + jnp.arange(span, dtype=jnp.int32)
    cosine, sine = rope_tables(positions, ROTARY)

    def turn(query_raw, key_raw):
        return (rotate(query_raw, cosine, sine, ROTARY), rotate(key_raw, cosine, sine, ROTARY))

    (query_r, key_r), rope_pull = jax.vjp(
        turn,
        joint3[..., :width].reshape(seqs, span, HEADS, depth),
        joint3[..., width : 2 * width].reshape(seqs, span, HEADS, depth),
    )
    query_b = query_r.astype(jnp.bfloat16)
    key_local = key_r.astype(jnp.bfloat16)
    value_local = joint3[..., 2 * width :].reshape(seqs, span, HEADS, depth).astype(jnp.bfloat16)
    key_send = key_local.reshape(seqs, span, width)
    value_send = value_local.reshape(seqs, span, width)
    top = jnp.full((seqs, HEADS, span), masked_score, jnp.float32)
    key_piece = lax.all_gather(key_send, "blk", axis=1, tiled=True)
    value_piece = lax.all_gather(value_send, "blk", axis=1, tiled=True)
    count = key_piece.shape[1]
    key_h = key_piece.reshape(seqs, count, HEADS, depth)
    value_h = value_piece.reshape(seqs, count, HEADS, depth)
    scores = (
        jnp.einsum("sqhe,skhe->shqk", query_b, key_h, preferred_element_type=jnp.float32)
        * att_scale
    )
    allowed = positions[:, None] >= jnp.arange(count, dtype=jnp.int32)[None, :]
    scores = jnp.where(allowed, scores, masked_score)
    new_top = jnp.maximum(top, jnp.max(scores, axis=-1))
    weights = jnp.where(allowed, jnp.exp(scores - new_top[..., None]), 0.0)
    total = jnp.sum(weights, axis=-1)
    update = jnp.einsum(
        "shqk,skhe->sqhe", weights.astype(jnp.bfloat16), value_h, preferred_element_type=jnp.float32
    )
    accum = update
    top, total, accum = (new_top, total, accum)
    attended_f = (accum / jnp.transpose(total, (0, 2, 1))[..., None]).reshape(rows, width)
    log_total = top + jnp.log(total)
    attended = attended_f.astype(jnp.bfloat16)
    branch_att, middle_att = project(attended, *part_att)
    up_pre, middle_up = project(second, *part_up)
    hidden_f, gelu_pull = jax.vjp(exact_gelu, up_pre)
    hidden = hidden_f.astype(jnp.bfloat16)
    branch_ff, middle_ff = project(hidden, *part_ff)
    mixed = (input_rows + branch_att + branch_ff).astype(jnp.bfloat16).reshape(seqs, span, width)
    lookup = (domain_ids[..., None] == jnp.arange(DOMAINS, dtype=jnp.int32)).astype(jnp.float32)
    row_weight = jnp.sum(lookup * domain_weight, axis=-1).reshape(rows, 1)
    row_grad = cotangent.astype(jnp.float32).reshape(rows, width) * row_weight
    grad_low = row_grad.astype(jnp.bfloat16)
    grad_hidden, grad_a_ffp, grad_b_ffp = project_back(grad_low, hidden, middle_ff, *part_ff)
    upper_gradient = gelu_pull(grad_hidden)[0].astype(jnp.bfloat16)
    grad_second, grad_a_up, grad_b_up = project_back(upper_gradient, second, middle_up, *part_up)
    grad_att_f, grad_a_att, grad_b_att = project_back(grad_low, attended, middle_att, *part_att)
    grad_att = grad_att_f.astype(jnp.bfloat16)
    grad_heads = grad_att.reshape(seqs, span, HEADS, depth)
    delta = jnp.transpose(
        jnp.sum(
            grad_heads.astype(jnp.float32) * attended_f.reshape(seqs, span, HEADS, depth), axis=-1
        ),
        (0, 2, 1),
    )
    key_piece = lax.all_gather(key_send, "blk", axis=1, tiled=True)
    value_piece = lax.all_gather(value_send, "blk", axis=1, tiled=True)
    count = key_piece.shape[1]
    key_h = key_piece.reshape(seqs, count, HEADS, depth)
    value_h = value_piece.reshape(seqs, count, HEADS, depth)
    scores = (
        jnp.einsum("sqhe,skhe->shqk", query_b, key_h, preferred_element_type=jnp.float32)
        * att_scale
    )
    allowed = positions[:, None] >= jnp.arange(count, dtype=jnp.int32)[None, :]
    weights = jnp.where(allowed, jnp.exp(scores - log_total[..., None]), 0.0)
    grad_w = jnp.einsum("sqhe,skhe->shqk", grad_heads, value_h, preferred_element_type=jnp.float32)
    grad_s = (weights * (grad_w - delta[..., None])).astype(jnp.bfloat16)
    grad_query = (
        jnp.einsum("shqk,skhe->sqhe", grad_s, key_h, preferred_element_type=jnp.float32) * att_scale
    )
    stats_lse, stats_delta = (
        lax.all_gather(log_total.astype(jnp.bfloat16), "blk", axis=2, tiled=True).astype(
            log_total.dtype
        ),
        lax.all_gather(delta.astype(jnp.bfloat16), "blk", axis=2, tiled=True).astype(delta.dtype),
    )
    query_piece = lax.all_gather(query_b.reshape(seqs, span, width), "blk", axis=1, tiled=True)
    grad_piece = lax.all_gather(grad_att.reshape(seqs, span, width), "blk", axis=1, tiled=True)
    count = query_piece.shape[1]
    query_h = query_piece.reshape(seqs, count, HEADS, depth)
    grad_h = grad_piece.reshape(seqs, count, HEADS, depth)
    scores = (
        jnp.einsum("sqhe,skhe->shqk", query_h, key_local, preferred_element_type=jnp.float32)
        * att_scale
    )
    allowed = jnp.arange(count, dtype=jnp.int32)[:, None] >= positions[None, :]
    weights = jnp.where(allowed, jnp.exp(scores - stats_lse[..., None]), 0.0)
    grad_v = jnp.einsum(
        "shqk,sqhe->skhe", weights.astype(jnp.bfloat16), grad_h, preferred_element_type=jnp.float32
    )
    grad_w = jnp.einsum("sqhe,skhe->shqk", grad_h, value_local, preferred_element_type=jnp.float32)
    grad_s = (weights * (grad_w - stats_delta[..., None])).astype(jnp.bfloat16)
    grad_k = (
        jnp.einsum("shqk,sqhe->skhe", grad_s, query_h, preferred_element_type=jnp.float32)
        * att_scale
    )
    grad_query_raw, grad_key_raw = rope_pull((grad_query, grad_k))
    grad_joint = jnp.concatenate(
        [
            grad_query_raw.reshape(rows, width),
            grad_key_raw.reshape(rows, width),
            grad_v.reshape(rows, width),
        ],
        axis=1,
    ).astype(jnp.bfloat16)
    grad_first, grad_a_qkv, grad_b_qkv = project_back(grad_joint, first, middle_qkv, *part_qkv)
    back_one = first_pull(grad_first)
    back_two = second_pull(grad_second)
    grad_tokens = (
        (row_grad + back_one[0] + back_two[0]).astype(jnp.bfloat16).reshape(seqs, span, width)
    )
    gain_part = jnp.stack([back_one[1], back_two[1]])
    shift_part = jnp.stack([back_one[2], back_two[2]])
    grad_a_part = jnp.concatenate([grad_a_qkv, grad_a_att, grad_a_up], axis=1)
    grad_b_part = jnp.concatenate([grad_b_qkv, grad_b_att, grad_b_up], axis=1)
    summed = lax.psum(
        (grad_a_part, grad_a_ffp, grad_b_part, grad_b_ffp, gain_part, shift_part), ("dp", "blk")
    )
    owner = lax.axis_index("dp")
    grad_a = lax.dynamic_slice_in_dim(summed[0], owner * adapt_a.shape[0], adapt_a.shape[0], 0)
    grad_a_ff = lax.dynamic_slice_in_dim(
        summed[1], owner * adapt_a_ff.shape[0], adapt_a_ff.shape[0], 0
    )
    grad_b = lax.dynamic_slice_in_dim(summed[2], owner * adapt_b.shape[1], adapt_b.shape[1], 1)
    grad_b_ff = lax.dynamic_slice_in_dim(
        summed[3], owner * adapt_b_ff.shape[1], adapt_b_ff.shape[1], 1
    )
    grad_gain = summed[4]
    grad_shift = summed[5]
    fresh_a, new_mean_a, new_square_a = adam_update(adapt_a, grad_a, mean_a, square_a, keep_a)
    reset_down_adapter_left, new_mean_a_ff, new_square_a_ff = adam_update(
        adapt_a_ff, grad_a_ff, mean_a_ff, square_a_ff, keep_a_ff
    )
    fresh_b, new_mean_b, new_square_b = adam_update(adapt_b, grad_b, mean_b, square_b, keep_b)
    reset_down_adapter_right, new_mean_b_ff, new_square_b_ff = adam_update(
        adapt_b_ff, grad_b_ff, mean_b_ff, square_b_ff, keep_b_ff
    )
    fresh_b_all, reset_down_right_stacked = (
        lax.all_gather(fresh_b.astype(jnp.bfloat16), "dp", axis=1, tiled=True).astype(
            fresh_b.dtype
        ),
        lax.all_gather(
            reset_down_adapter_right.astype(jnp.bfloat16), "dp", axis=1, tiled=True
        ).astype(reset_down_adapter_right.dtype),
    )
    input_weight_update = jnp.concatenate(
        [
            precise_product(fresh_a[:, :rank], fresh_b_all[:, : 3 * width]),
            precise_product(fresh_a[:, rank : 2 * rank], fresh_b_all[:, 3 * width : 4 * width]),
            precise_product(fresh_a[:, 2 * rank :], fresh_b_all[:, 4 * width :]),
        ],
        axis=1,
    )
    folded_input_weights = (
        frozen_input_weights.astype(jnp.float32) + adapter_scale * input_weight_update
    ).astype(jnp.bfloat16)
    folded_down_weight = (
        frozen_down_weight.astype(jnp.float32)
        + adapter_scale * precise_product(reset_down_adapter_left, reset_down_right_stacked)
    ).astype(jnp.bfloat16)
    return (
        mixed,
        grad_tokens,
        grad_gain,
        grad_shift,
        grad_a,
        grad_a_ff,
        grad_b,
        grad_b_ff,
        new_mean_a,
        new_square_a,
        new_mean_a_ff,
        new_square_a_ff,
        new_mean_b,
        new_square_b,
        new_mean_b_ff,
        new_square_b_ff,
        folded_input_weights,
        folded_down_weight,
    )


def solution(mesh):
    in_specs = (
        P("dp", "blk", None),
        P("dp", "blk", None),
        P("dp", "blk"),
        P(),
        P("dp", None),
        P(),
        P("dp", None),
        P(),
        P(),
        P(),
        P("dp", None),
        P("dp", None),
        P(None, "dp"),
        P(None, "dp"),
        P("dp", None),
        P("dp", None),
        P(None, "dp"),
        P(None, "dp"),
        P("dp", None),
        P("dp", None),
        P(None, "dp"),
        P(None, "dp"),
        P("dp", None),
        P("dp", None),
        P(None, "dp"),
        P(None, "dp"),
    )
    out_specs = (
        P("dp", "blk", None),
        P("dp", "blk", None),
        P(),
        P(),
        P("dp", None),
        P("dp", None),
        P(None, "dp"),
        P(None, "dp"),
        P("dp", None),
        P("dp", None),
        P("dp", None),
        P("dp", None),
        P(None, "dp"),
        P(None, "dp"),
        P(None, "dp"),
        P(None, "dp"),
        P("dp", None),
        P("dp", None),
    )
    return jax.shard_map(body, mesh=mesh, in_specs=in_specs, out_specs=out_specs, check_vma=False)
```

profile of v0, /device:TPU:0, one launch (start us, length us, event | category | flops | bytes accessed | tf_op | source)
XLA Modules:
  0.0 990.2 jit_solution(3469510999970349865)
XLA Ops:
  12.5 12.9 %all_gather.45 = bf16[1024,384]{1,0:T(8,128)(2,1)} all-gather(bf16[128,384]{1,0:T(8,128)(2,1)S(1)} %convert_element_type.174), channel_id=1, replica_groups=mesh['dp'=8,'blk'=4] {'dp'}, dimensions={0}, use_global_device_ids=true | all-gather | bytes 884736 | tf_op jit(solution)/shard_map/all_gather | solution.py:166
  30.0 72.5 %all-gather.10.cloned.1.call-done = bf16[1024,8192]{1,0:T(8,128)(2,1)} async-done(((bf16[128,8192]{1,0:T(8,128)(2,1)}), bf16[1024,8192]{1,0:T(8,128)(2,1)}) %all-gather.10.cloned.1.call-update) | async-done | bytes 16777232 | tf_op jit(solution)/shard_map/all_gather | solution.py:164
  102.5 10.2 %fusion.23 = f32[768,3072]{1,0:T(8,128)} fusion(bf16[768,1024]{1,0:T(8,128)(2,1)S(1)} %get-tuple-element.112, bf16[1024,8192]{1,0:T(8,128)(2,1)} %all-gather.10.cloned.1.call-done), kind=kOutput, calls=%fused_computation.39 | convolution fusion | flops 4831838208 | bytes 17301504 | tf_op jit(solution)/shard_map/dot_general | solution.py:23
  112.8 20.2 %all-gather.12.cloned.1.call-done = bf16[128,8192]{1,0:T(8,128)(2,1)} async-done(((bf16[128,1024]{1,0:T(8,128)(2,1)}), bf16[128,8192]{1,0:T(8,128)(2,1)}) %all-gather.12.cloned.1.call-update) | async-done | bytes 2097168 | tf_op jit(solution)/shard_map/all_gather | solution.py:168
  132.9 5.3 multiply_add_fusion.1
  138.3 2.7 fusion.131
  143.1 3.9 copy.73
  147.0 2.4 copy.74
  168.0 10.3 %all_gather.51 = bf16[128,1024]{1,0:T(8,128)(2,1)S(1)} all-gather(bf16[128,128]{1,0:T(8,128)(2,1)} %convert_element_type.194), channel_id=1, replica_groups=mesh['dp'=8,'blk'=4] {'dp'}, dimensions={1}, use_global_device_ids=true | all-gather | bytes 294912 | tf_op jit(solution)/shard_map/all_gather | solution.py:169
  190.3 12.6 %fusion.136 = f32[768,4096]{1,0:T(8,128)} fusion(bf16[768,1024]{1,0:T(8,128)(2,1)S(1)} %fusion.28, bf16[4096,1024]{1,0:T(8,128)(2,1)} %all-gather.18.cloned.1.call-done), kind=kOutput, calls=%fused_computation.232 | convolution fusion | flops 6442450944 | bytes 22544384 | tf_op jit(solution)/shard_map/dot_general | solution.py:27
  202.9 2.8 slice.131
  205.7 3.4 fusion.57
  210.7 3.3 reshape.291
  214.0 5.0 copy.77
  219.0 2.8 maximum_convert_fusion
  222.1 9.4 fusion.19
  231.5 31.8 %multiply_convert_fusion.2 = (bf16[768,4096]{1,0:T(8,128)(2,1)}, f32[768,4096]{1,0:T(8,128)}, f32[768,4096]{1,0:T(8,128)}) fusion(bf16[768,128]{1,0:T(8,128)(2,1)S(1)} %copy-done.54, bf16[128,8192]{1,0:T(8,128)(2,1)S(1)} %copy-done.56, f32[768,4096]{1,0:T(8,128)S(1)} %fusion.19, f32[4096]{0:T(1024)S(1)} %copy-done.84), kind=kOutput, calls=%fused_computation.15 | convolution fusion | flops 1019215872 | bytes 45301760 | tf_op jit(solution)/shard_map/dot_general | solution.py:23
  263.4 17.3 %add_convert_fusion = bf16[768,4096]{1,0:T(8,128)(2,1)} fusion(f32[768,4096]{1,0:T(8,128)} %get-tuple-element.99, f32[768,4096]{1,0:T(8,128)} %fusion.136, f32[768,4096]{1,0:T(8,128)} %get-tuple-element.136, bf16[768,128]{1,0:T(8,128)(2,1)} %fusion.69, bf16[4096,128]{1,0:T(8,128)(2,1)} %all-gather.20.cloned.1.call-done), kind=kOutput, calls=%fused_computation.14 | convolution fusion | flops 852492288 | bytes 45285376 | tf_op jit(solution)/shard_map/dot_general | solution.py:27
  280.7 5.0 fusion.70
  290.0 3.1 fusion.89
  295.5 3.2 fusion.140
  298.8 12.6 %fusion.135 = f32[768,1024]{1,0:T(8,128)} fusion(bf16[768,4096]{1,0:T(8,128)(2,1)} %get-tuple-element.98, bf16[4096,1024]{1,0:T(8,128)(2,1)} %all-gather.18.cloned.1.call-done), kind=kOutput, calls=%fused_computation.231 | convolution fusion | flops 6442450944 | bytes 17825792 | tf_op jit(solution)/shard_map/dot_general | solution.py:23
  311.4 21.1 %all-gather.16.cloned.1.call-done = bf16[3,1024,1024]{1,2,0:T(8,128)(2,1)} async-done(((bf16[3,256,1024]{1,2,0:T(8,128)(2,1)}), bf16[3,1024,1024]{1,2,0:T(8,128)(2,1)}) %all-gather.16.cloned.1.call-update) | async-done | bytes 6291472 | tf_op jit(solution)/shard_map/all_gather | solution.py:196
  332.5 21.8 %select_reduce_fusion = (f32[3,16,256]{2,1,0:T(8,128)S(1)}, f32[3,16,256,1024]{3,2,1,0:T(8,128)}) fusion(pred[256,1024]{1,0:T(8,128)(4,1)S(1)} %copy-done.5, bf16[3,1024,16,64]{1,3,2,0:T(8,128)(2,1)} %bitcast.174, bf16[3,256,16,48]{1,3,2,0:T(8,128)(2,1)S(1)} %copy-done.14, bf16[3,256,16,8]{1,3,2,0:T(8,128)(2,1)S(1)} %get-tuple-element.124, ...), kind=kOutput, calls=%fused_computation.4 | convolution fusion | flops 1653067776 | bytes 58507264 | tf_op jit(solution)/shard_map/sqhe,skhe->shqk/dot_general | solution.py:202
  354.3 23.0 %fusion.1 = f32[3,16,256]{2,1,0:T(8,128)S(1)} fusion(f32[3,16,256,1024]{3,2,1,0:T(8,128)} %get-tuple-element.135, f32[3,16,256]{2,1,0:T(8,128)S(1)} %broadcast_maximum_fusion, pred[256,1024]{1,0:T(8,128)(4,1)S(1)} %copy-done.5), kind=kLoop, calls=%fused_computation.6 | loop fusion | flops 62902272 | bytes 50692096 | tf_op jit(solution)/shard_map/reduce_sum | solution.py:209
  377.3 20.7 %all_gather.53 = bf16[3,16,1024]{2,1,0:T(8,128)(2,1)S(1)} all-gather(bf16[3,16,256]{2,1,0:T(8,128)(2,1)S(1)} %get-tuple-element.96), channel_id=1, replica_groups=mesh['dp'=8,'blk'=4] {'blk'}, dimensions={2}, use_global_device_ids=true | all-gather | bytes 122880 | tf_op jit(solution)/shard_map/all_gather | solution.py:257
  398.0 50.5 %all-gather.14.cloned.1.call-done = bf16[3,1024,1024]{1,2,0:T(8,128)(2,1)} async-done(((bf16[3,256,1024]{1,2,0:T(8,128)(2,1)}), bf16[3,1024,1024]{1,2,0:T(8,128)(2,1)}) %all-gather.14.cloned.1.call-update) | async-done | bytes 6291472 | tf_op jit(solution)/shard_map/all_gather | solution.py:197
  448.5 23.5 %multiply_reduce_fusion = (f32[3,256,16]{1,2,0:T(8,128)S(1)}, bf16[3,256,16,64]{1,3,2,0:T(8,128)(2,1)}) fusion(bf16[3,256,16,64]{1,3,2,0:T(8,128)(2,1)S(1)} %copy-done.39, f32[3,256,16]{1,2,0:T(8,128)S(1)} %bitcast.202, bf16[3,1024,16,64]{1,3,2,0:T(8,128)(2,1)} %bitcast.218, f32[3,16,256,1024]{3,2,1,0:T(8,128)} %get-tuple-element.135, ...), kind=kOutput, calls=%fused_computation.86 | convolution fusion | flops 1677447168 | bytes 60178432 | tf_op jit(solution)/shard_map/shqk,skhe->sqhe/dot_general | solution.py:210
  472.1 28.8 %multiply_bitcast_fusion.1 = f32[3,256,16,64]{1,3,2,0:T(8,128)} fusion(bf16[3,1024,16,64]{1,3,2,0:T(8,128)(2,1)} %bitcast.175, f32[3,16,256,1024]{3,2,1,0:T(8,128)} %get-tuple-element.135, bf16[3,256,16,64]{1,3,2,0:T(8,128)(2,1)S(1)} %copy-done.39, bf16[3,1024,16,64]{1,3,2,0:T(8,128)(2,1)} %bitcast.219, f32[3,16,256]{2,1,0:T(8,128)S(1)} %bitcast.211, ...), kind=kOutput, calls=%fused_computation.85 | convolution fusion | flops 3297509376 | bytes 67993600 | tf_op jit(solution)/shard_map/shqk,skhe->sqhe/dot_general | solution.py:254
  500.9 27.6 %all_gather.55 = bf16[3,16,1024]{2,1,0:T(8,128)(2,1)S(1)} all-gather(bf16[3,16,256]{2,1,0:T(8,128)(2,1)S(1)} %bitcast_convert_fusion), channel_id=1, replica_groups=mesh['dp'=8,'blk'=4] {'blk'}, dimensions={2}, use_global_device_ids=true | all-gather | bytes 122880 | tf_op jit(solution)/shard_map/all_gather | solution.py:260
  529.2 35.5 %all-gather.22.cloned.1.call-done = bf16[3,1024,1024]{1,2,0:T(8,128)(2,1)} async-done(((bf16[3,256,1024]{1,2,0:T(8,128)(2,1)}), bf16[3,1024,1024]{1,2,0:T(8,128)(2,1)}) %all-gather.22.cloned.1.call-update) | async-done | bytes 6291472 | tf_op jit(solution)/shard_map/all_gather | solution.py:262
  564.7 22.0 %fusion.134 = f32[3,16,1024,256]{3,2,1,0:T(8,128)} fusion(bf16[3,1024,16,64]{1,3,2,0:T(8,128)(2,1)} %bitcast.179, bf16[3,256,16,48]{1,3,2,0:T(8,128)(2,1)S(1)} %copy-done.13, bf16[3,256,16,8]{1,3,2,0:T(8,128)(2,1)S(1)} %copy-done.36, bf16[3,256,16,8]{1,3,2,0:T(8,128)(2,1)S(1)} %copy-done.34), kind=kOutput, calls=%fused_computation.230 | convolution fusion | flops 1615331328 | bytes 58195968 | tf_op jit(solution)/shard_map/sqhe,skhe->shqk/dot_general | solution.py:268
  586.7 93.3 %all-gather.24.cloned.1.call-done = bf16[3,1024,1024]{2,1,0:T(8,128)(2,1)} async-done(((bf16[3,256,1024]{2,1,0:T(8,128)(2,1)}), bf16[3,1024,1024]{2,1,0:T(8,128)(2,1)}) %all-gather.24.cloned.1.call-update) | async-done | bytes 6291472 | tf_op jit(solution)/shard_map/all_gather | solution.py:263
  680.1 8.7 copy.80
  688.7 20.5 %fusion.64 = bf16[3,256,16,64]{1,3,2,0:T(8,128)(2,1)} fusion(bf16[3,1024,16,64]{1,3,2,0:T(8,128)(2,1)} %bitcast.189, f32[3,16,1024,256]{3,2,1,0:T(8,128)} %fusion.134, f32[3,16,1024]{2,1,0:T(8,128)S(1)} %convert_element_type.203, pred[1024,256]{1,0:T(8,128)(4,1)S(1)} %copy-done.60), kind=kOutput, calls=%fused_computation.97 | convolution fusion | flops 1661730816 | bytes 58654720 | tf_op jit(solution)/shard_map/shqk,sqhe->skhe/dot_general | solution.py:273
  709.2 28.0 %multiply_bitcast_fusion = f32[3,256,16,64]{1,3,2,0:T(8,128)} fusion(bf16[3,1024,16,64]{1,3,2,0:T(8,128)(2,1)} %bitcast.180, f32[3,16,1024,256]{3,2,1,0:T(8,128)} %fusion.134, bf16[3,1024,16,64]{1,3,2,0:T(8,128)(2,1)} %bitcast.190, bf16[3,256,16,64]{1,3,2,0:T(8,128)(2,1)} %bitcast.191, f32[3,16,1024]{2,1,0:T(8,128)} %convert_element_type.206, ...), kind=kOutput, calls=%fused_computation.83 | convolution fusion | flops 3297509376 | bytes 68288512 | tf_op jit(solution)/shard_map/shqk,sqhe->skhe/dot_general | solution.py:279
  754.6 2.7 fusion.67
  761.6 8.6 fusion.21
  772.9 13.2 %fusion.128 = (f32[1024]{0:T(1024)S(1)}, f32[768]{0:T(1024)S(1)}, f32[768]{0:T(1024)S(1)}, f32[1024]{0:T(1024)S(1)}, f32[768,1024]{1,0:T(8,128)S(1)}) fusion(f32[1024]{0:T(1024)S(1)} %bitcast.208, f32[768]{0:T(1024)S(1)} %copy-done.71, bf16[3,256,1024]{2,1,0:T(8,128)(2,1)S(1)} %copy-done.1, f32[768,1024]{1,0:T(8,128)S(1)} %convolution_add_fusion, ...), kind=kOutput, calls=%fused_computation.225 | convolution fusion | flops 6451097600 | bytes 25715712 | tf_op jit(solution)/shard_map/dot_general | solution.py:27
  786.1 2.9 fusion.44
  789.1 39.3 %all-reduce.6 = (f32[2,1024]{1,0:T(2,128)}, f32[2,1024]{1,0:T(2,128)}) all-reduce(f32[2,1024]{1,0:T(2,128)S(1)} %pad_maximum_fusion.2, f32[2,1024]{1,0:T(2,128)S(1)} %pad_maximum_fusion.3), channel_id=1, replica_groups=mesh['dp'=8,'blk'=4] {'dp','blk'}, use_global_device_ids=true, to_apply=%region_12.13 | all-reduce | flops 4096 | bytes 32768 | tf_op jit(solution)/shard_map/psum | solution.py:301
  828.4 3.1 fusion.93
  831.5 5.1 fusion.59
  836.6 103.6 %all-reduce.10.cloned.1.call-done = (f32[1024,384]{0,1:T(8,128)}, f32[4096,128]{1,0:T(8,128)}, f32[128,8192]{1,0:T(8,128)}, f32[128,1024]{1,0:T(8,128)}) async-done(((f32[1024,384]{0,1:T(8,128)}, f32[4096,128]{1,0:T(8,128)}, f32[128,8192]{1,0:T(8,128)}, f32[128,1024]{1,0:T(8,128)}), (f32[1024,384]{0,1:T(8,128)}, f32[4096,128]{1,0:T(8,128)}, f32[128,8192]{1,0:T(8,128)}, ...) | async-done | bytes 8388624 | tf_op jit(solution)/shard_map/psum | solution.py:301
  940.2 2.6 subtract_convert_fusion
  942.9 6.1 fusion.51
  949.3 3.2 fusion.30
  957.2 10.1 %all_gather.57 = bf16[128,1024]{1,0:T(8,128)(2,1)S(1)} all-gather(bf16[128,128]{1,0:T(8,128)(2,1)S(1)} %get-tuple-element.88), channel_id=1, replica_groups=mesh['dp'=8,'blk'=4] {'dp'}, dimensions={1}, use_global_device_ids=true | all-gather | bytes 294912 | tf_op jit(solution)/shard_map/all_gather | solution.py:327
  (305 shorter events, 96.1 us)
Async XLA Ops:
  7.2 95.3 %all-gather.10.cloned.1.call-start = ((), (), s32[]{:S(2)}) async-start(), calls=%async_computation | async-start | bytes 18874368 | tf_op jit(solution)/shard_map/all_gather | solution.py:164
  8.0 125.0 %all-gather.12.cloned.1.call-start = ((), (), s32[]{:S(2)}) async-start(), calls=%async_computation.1 | async-start | bytes 2359296 | tf_op jit(solution)/shard_map/all_gather | solution.py:168
  9.9 180.5 %all-gather.18.cloned.1.call-start = ((), (), s32[]{:S(2)}) async-start(), calls=%async_computation.4 | async-start | bytes 9437184 | tf_op jit(solution)/shard_map/all_gather | solution.py:165
  10.6 252.8 %all-gather.20.cloned.1.call-start = ((), (), s32[]{:S(2)}) async-start(), calls=%async_computation.5 | async-start | bytes 1179648 | tf_op jit(solution)/shard_map/all_gather | solution.py:167
  11.4 321.1 %all-gather.16.cloned.1.call-start = ((), (), s32[]{:S(2)}) async-start(), calls=%async_computation.3 | async-start | bytes 7864320 | tf_op jit(solution)/shard_map/all_gather | solution.py:196
  12.3 17.6 %copy-start.70 = (f32[768]{0:T(1024)}, f32[768]{0:T(1024)S(1)}, u32[]{:S(2)}) copy-start(f32[768]{0:T(1024)S(1)} %div.87) | copy-start | bytes 9220
  12.3 13.8 %copy-start.80 = (f32[768]{0:T(1024)}, f32[768]{0:T(1024)S(1)}, u32[]{:S(2)}) copy-start(f32[768]{0:T(1024)S(1)} %add.223) | copy-start | bytes 9220
  12.4 17.5 %copy-start.72 = (f32[768]{0:T(1024)}, f32[768]{0:T(1024)S(1)}, u32[]{:S(2)}) copy-start(f32[768]{0:T(1024)S(1)} %rsqrt.13) | copy-start | bytes 9220
  12.4 17.5 %copy-start.74 = (f32[1,1024]{1,0:T(1,128)}, f32[1,1024]{1,0:T(1,128)S(1)}, u32[]{:S(2)}) copy-start(f32[1,1024]{1,0:T(1,128)S(1)} %get-tuple-element.126) | copy-start | bytes 12292
  12.4 17.5 %copy-start.76 = (f32[1,1024]{1,0:T(1,128)}, f32[1,1024]{1,0:T(1,128)S(1)}, u32[]{:S(2)}) copy-start(f32[1,1024]{1,0:T(1,128)S(1)} %get-tuple-element.127) | copy-start | bytes 12292
  28.1 84.6 %copy-start.21 = (bf16[768,1024]{1,0:T(8,128)(2,1)}, bf16[768,1024]{1,0:T(8,128)(2,1)S(1)}, u32[]{:S(2)}) copy-start(bf16[768,1024]{1,0:T(8,128)(2,1)S(1)} %get-tuple-element.112) | copy-start | bytes 4718596
  29.9 103.1 %copy-start.45 = (bf16[768,128]{1,0:T(8,128)(2,1)}, bf16[768,128]{1,0:T(8,128)(2,1)S(1)}, u32[]{:S(2)}) copy-start(bf16[768,128]{1,0:T(8,128)(2,1)S(1)} %convolution_convert_fusion.3) | copy-start | bytes 589828
  30.0 121.2 %copy-start.66 = (f32[256,8]{0,1:T(8,128)}, f32[256,8]{0,1:T(8,128)S(1)}, u32[]{:S(2)}) copy-start(f32[256,8]{0,1:T(8,128)S(1)} %get-tuple-element.132) | copy-start | bytes 24580
  30.0 121.2 %copy-start.68 = (f32[256,8]{0,1:T(8,128)}, f32[256,8]{0,1:T(8,128)S(1)}, u32[]{:S(2)}) copy-start(f32[256,8]{0,1:T(8,128)S(1)} %get-tuple-element.133) | copy-start | bytes 24580
  154.7 293.8 %all-gather.14.cloned.1.call-start = ((), (), s32[]{:S(2)}) async-start(), calls=%async_computation.2 | async-start | bytes 7864320 | tf_op jit(solution)/shard_map/all_gather | solution.py:197
  158.5 24.2 %copy-start.23 = (bf16[768,1024]{1,0:T(8,128)(2,1)S(1)}, bf16[768,1024]{1,0:T(8,128)(2,1)}, u32[]{:S(2)}) copy-start(bf16[768,1024]{1,0:T(8,128)(2,1)} %get-tuple-element.113) | copy-start | bytes 4718596
  158.5 26.3 %copy-start.19 = (bf16[3,256,1024]{2,1,0:T(8,128)(2,1)S(1)}, bf16[3,256,1024]{2,1,0:T(8,128)(2,1)}, u32[]{:S(2)}) copy-start(bf16[3,256,1024]{2,1,0:T(8,128)(2,1)} %param.27) | copy-start | bytes 4718596
  158.6 406.2 %all-gather.22.cloned.1.call-start = ((), (), s32[]{:S(2)}) async-start(), calls=%async_computation.6 | async-start | bytes 7864320 | tf_op jit(solution)/shard_map/all_gather | solution.py:262
  160.6 24.6 %copy-start.78 = (f32[768]{0:T(1024)}, f32[768]{0:T(1024)S(1)}, u32[]{:S(2)}) copy-start(f32[768]{0:T(1024)S(1)} %mul.573) | copy-start | bytes 9220
  185.2 103.5 %copy-start.6 = (bf16[768,1024]{1,0:T(8,128)(2,1)}, bf16[768,1024]{1,0:T(8,128)(2,1)S(1)}, u32[]{:S(2)}) copy-start(bf16[768,1024]{1,0:T(8,128)(2,1)S(1)} %fusion.28) | copy-start | bytes 4718596
  221.8 458.3 %all-gather.24.cloned.1.call-start = ((), (), s32[]{:S(2)}) async-start(), calls=%async_computation.7 | async-start | bytes 7864320 | tf_op jit(solution)/shard_map/all_gather | solution.py:263
  298.7 33.7 %copy-start.5 = (pred[256,1024]{1,0:T(8,128)(4,1)S(1)}, pred[256,1024]{1,0:T(8,128)(4,1)}, u32[]{:S(2)}) copy-start(pred[256,1024]{1,0:T(8,128)(4,1)} %iota_compare_fusion.1) | copy-start | bytes 786436
  298.7 33.7 %copy-start.14 = (bf16[3,256,16,48]{1,3,2,0:T(8,128)(2,1)S(1)}, bf16[3,256,16,48]{1,3,2,0:T(8,128)(2,1)}, u32[]{:S(2)}) copy-start(bf16[3,256,16,48]{1,3,2,0:T(8,128)(2,1)} %slice.131) | copy-start | bytes 3538948
  298.7 641.4 %all-reduce.10.cloned.1.call-start = ((), (), s32[]{:S(2)}) async-start(), calls=%async_computation.9 | async-start | bytes 16777216 | tf_op jit(solution)/shard_map/psum | solution.py:301
  354.3 94.2 %copy-start.39 = (bf16[3,256,16,64]{1,3,2,0:T(8,128)(2,1)S(1)}, bf16[3,256,16,64]{1,3,2,0:T(8,128)(2,1)}, u32[]{:S(2)}) copy-start(bf16[3,256,16,64]{1,3,2,0:T(8,128)(2,1)} %copy.77) | copy-start | bytes 4718596
  398.0 290.7 %copy-start.64 = (f32[3,16,1024]{2,1,0:T(8,128)}, f32[3,16,1024]{2,1,0:T(8,128)S(1)}, u32[]{:S(2)}) copy-start(f32[3,16,1024]{2,1,0:T(8,128)S(1)} %convert_element_type.203) | copy-start | bytes 589828
  500.9 63.8 %copy-start.13 = (bf16[3,256,16,48]{1,3,2,0:T(8,128)(2,1)S(1)}, bf16[3,256,16,48]{1,3,2,0:T(8,128)(2,1)}, u32[]{:S(2)}) copy-start(bf16[3,256,16,48]{1,3,2,0:T(8,128)(2,1)} %copy-done.12) | copy-start | bytes 3538948
  500.9 63.8 %copy-start.34 = (bf16[3,256,16,8]{1,3,2,0:T(8,128)(2,1)S(1)}, bf16[3,256,16,8]{1,3,2,0:T(8,128)(2,1)}, u32[]{:S(2)}) copy-start(bf16[3,256,16,8]{1,3,2,0:T(8,128)(2,1)} %copy-done.33) | copy-start | bytes 589828
  500.9 63.8 %copy-start.36 = (bf16[3,256,16,8]{1,3,2,0:T(8,128)(2,1)S(1)}, bf16[3,256,16,8]{1,3,2,0:T(8,128)(2,1)}, u32[]{:S(2)}) copy-start(bf16[3,256,16,8]{1,3,2,0:T(8,128)(2,1)} %copy-done.35) | copy-start | bytes 589828
  586.7 102.0 %copy-start.60 = (pred[1024,256]{1,0:T(8,128)(4,1)S(1)}, pred[1024,256]{1,0:T(8,128)(4,1)}, u32[]{:S(2)}) copy-start(pred[1024,256]{1,0:T(8,128)(4,1)} %iota_compare_fusion) | copy-start | bytes 786436
  709.2 28.0 %copy-start.15 = (f32[3,256,16,64]{1,3,2,0:T(8,128)S(1)}, f32[3,256,16,64]{1,3,2,0:T(8,128)}, u32[]{:S(2)}) copy-start(f32[3,256,16,64]{1,3,2,0:T(8,128)} %multiply_bitcast_fusion.1) | copy-start | bytes 9437188
  709.2 28.0 %copy-start.67 = (f32[256,8]{0,1:T(8,128)S(1)}, f32[256,8]{0,1:T(8,128)}, u32[]{:S(2)}) copy-start(f32[256,8]{0,1:T(8,128)} %copy-done.66) | copy-start | bytes 24580
  709.2 28.0 %copy-start.69 = (f32[256,8]{0,1:T(8,128)S(1)}, f32[256,8]{0,1:T(8,128)}, u32[]{:S(2)}) copy-start(f32[256,8]{0,1:T(8,128)} %copy-done.68) | copy-start | bytes 24580
  761.6 215.2 %all-gather.26.cloned.1.call-start = ((), (), s32[]{:S(2)}) async-start(), calls=%async_computation.8 | async-start | bytes 2359296 | tf_op jit(solution)/shard_map/all_gather | solution.py:324
  772.8 13.2 %copy-start.3 = (f32[768,1024]{1,0:T(8,128)}, f32[768,1024]{1,0:T(8,128)S(1)}, u32[]{:S(2)}) copy-start(f32[768,1024]{1,0:T(8,128)S(1)} %convolution_add_fusion) | copy-start | bytes 9437188
  836.6 106.2 %copy-start.41 = (bf16[128,1024]{1,0:T(8,128)(2,1)S(1)}, bf16[128,1024]{1,0:T(8,128)(2,1)}, u32[]{:S(2)}) copy-start(bf16[128,1024]{1,0:T(8,128)(2,1)} %copy-done.40) | copy-start | bytes 786436
  836.6 106.2 %copy-start.53 = (bf16[768,128]{1,0:T(8,128)(2,1)S(1)}, bf16[768,128]{1,0:T(8,128)(2,1)}, u32[]{:S(2)}) copy-start(bf16[768,128]{1,0:T(8,128)(2,1)} %copy-done.52) | copy-start | bytes 589828
  836.6 106.2 %copy-start.82 = (f32[1024]{0:T(1024)S(1)}, f32[1024]{0:T(1024)}, u32[]{:S(2)}) copy-start(f32[1024]{0:T(1024)} %convert_element_type.191) | copy-start | bytes 12292
  836.6 106.2 %copy-start.83 = (f32[1024]{0:T(1024)S(1)}, f32[1024]{0:T(1024)}, u32[]{:S(2)}) copy-start(f32[1024]{0:T(1024)} %slice_convert_fusion.2) | copy-start | bytes 12292
  942.8 29.6 %copy-start.30 = (f32[128,1024]{1,0:T(8,128)}, f32[128,1024]{1,0:T(8,128)S(1)}, u32[]{:S(2)}) copy-start(f32[128,1024]{1,0:T(8,128)S(1)} %get-tuple-element.93) | copy-start | bytes 1572868
  952.5 16.4 %copy-start.43 = (s32[512,128]{1,0:T(8,128)S(1)}, s32[512,128]{1,0:T(8,128)}, u32[]{:S(2)}) copy-start(s32[512,128]{1,0:T(8,128)} %param.49) | copy-start | bytes 786436
  952.5 16.4 %copy-start.57 = (f32[512,128]{1,0:T(8,128)S(1)}, f32[512,128]{1,0:T(8,128)}, u32[]{:S(2)}) copy-start(f32[512,128]{1,0:T(8,128)} %param.45) | copy-start | bytes 786436
  953.7 18.7 %copy-start.27 = (f32[128,1024]{1,0:T(8,128)S(1)}, f32[128,1024]{1,0:T(8,128)}, u32[]{:S(2)}) copy-start(f32[128,1024]{1,0:T(8,128)} %param.42) | copy-start | bytes 1572868
  953.7 18.7 %copy-start.28 = (f32[128,1024]{1,0:T(8,128)S(1)}, f32[128,1024]{1,0:T(8,128)}, u32[]{:S(2)}) copy-start(f32[128,1024]{1,0:T(8,128)} %param.46) | copy-start | bytes 1572868
  957.2 19.6 %copy-start.63 = (f32[128,128]{1,0:T(8,128)}, f32[128,128]{1,0:T(8,128)S(1)}, u32[]{:S(2)}) copy-start(f32[128,128]{1,0:T(8,128)S(1)} %get-tuple-element.89) | copy-start | bytes 196612
  957.2 17.4 %copy-start.42 = (bf16[512,1024]{1,0:T(8,128)(2,1)S(1)}, bf16[512,1024]{1,0:T(8,128)(2,1)}, u32[]{:S(2)}) copy-start(bf16[512,1024]{1,0:T(8,128)(2,1)} %param.32) | copy-start | bytes 3145732
  957.2 17.4 %copy-start.59 = (f32[512,128]{1,0:T(8,128)S(1)}, f32[512,128]{1,0:T(8,128)}, u32[]{:S(2)}) copy-start(f32[512,128]{1,0:T(8,128)} %param.37) | copy-start | bytes 786436
  957.2 17.4 %copy-start.62 = (f32[512,128]{1,0:T(8,128)S(1)}, f32[512,128]{1,0:T(8,128)}, u32[]{:S(2)}) copy-start(f32[512,128]{1,0:T(8,128)} %param.41) | copy-start | bytes 786436
  (57 other events, 264.2 us)
Sparse Core Ops, SparseCore 0:
  9.9 92.5 all-gather.9
  105.0 27.8 all-gather.11
  134.8 55.4 all-gather.17
  192.6 23.4 all-gather.19
  217.6 114.8 all-gather.15
  333.9 114.6 all-gather.13
  450.1 114.6 all-gather.21
  566.3 113.7 all-gather.23
  761.7 178.4 all-reduce.9
  942.9 28.6 all-gather.25
where the time goes:
time: 999 us; the launch traced here: 990 us
  waiting for transfers between devices  400 us (40%)
  matrix products  326 us (33%)
  blocking collectives  121 us (12%)
  other arithmetic  68.4 us (7%)
  local copies, waits for them, and re-layouts  58.5 us (6%)
  between operations  15.7 us (2%)
    psum x1, waiting for transfers between devices, body(): lax.psum((grad_a_part, grad_a_ffp, grad_b_part, grad_b_ffp, gain_part, sh...  104 us
    all_gather x1, waiting for transfers between devices, body(): lax.all_gather(grad_att.reshape(seqs, span, width), 'blk', axis=1, tiled=...  93.3 us
    dot_general x12, matrix products, matrix_product(): return jnp.dot(left, right, preferred_element_type=jnp.float32)  91.1 us
    dot_general x12, matrix products, product_right_transposed(): lax.dot_general(left, right, (((1,), (1,)), ((), ())), preferred_element_...  72.7 us
    all_gather x1, waiting for transfers between devices, body(): lax.all_gather(shards[0], 'dp', axis=0, tiled=True)  72.5 us
    all_gather x1, waiting for transfers between devices, body(): value_piece = lax.all_gather(value_send, 'blk', axis=1, tiled=True)  50.5 us
    psum x1, blocking collectives, body(): lax.psum((grad_a_part, grad_a_ffp, grad_b_part, grad_b_ffp, gain_part, sh...  39.3 us
    all_gather x1, waiting for transfers between devices, body(): lax.all_gather(query_b.reshape(seqs, span, width), 'blk', axis=1, tiled=T...  35.5 us
  transfers between devices with their start and end apart: 10, of which 8 were waited for; matrix products, arithmetic and copies ran while one was open for 36% of the time, Pallas kernels for 0%

commit v1 on v0

v1 whole, which is shorter than its diff:
```python
import functools
import math

import jax
import jax.numpy as jnp
from jax import lax
from jax.experimental import pallas as pl
from jax.experimental.pallas import tpu as pltpu
from jax.sharding import PartitionSpec as P

HEADS = 16
ROTARY = 16
DOMAINS = 22

adapter_scale = 0.25
rope_base = 10000.0
norm_eps = 1e-05
masked_score = -1e30
first_fix = 1.0 - (0.9**10) ** 10
second_fix = 1.0 - (0.999**10) ** 10

f32 = jnp.float32
bf16 = jnp.bfloat16


def nn(left, right):
    return lax.dot_general(left, right, (((1,), (0,)), ((), ())), preferred_element_type=f32)


def nt(left, right):
    return lax.dot_general(left, right, (((1,), (1,)), ((), ())), preferred_element_type=f32)


def tn(left, right):
    return lax.dot_general(left, right, (((0,), (0,)), ((), ())), preferred_element_type=f32)


def rope_lane_tables(length, depth, lanes):
    half = ROTARY // 2
    freqs = rope_base ** (-(jnp.arange(half, dtype=f32) * 2.0) / ROTARY)
    angles = jnp.arange(length, dtype=f32)[:, None] * freqs[None, :]
    cosine, sine = jnp.cos(angles), jnp.sin(angles)
    rest = depth - ROTARY
    ones, zero_half = jnp.ones((length, rest), f32), jnp.zeros((length, half), f32)
    zero_rest = jnp.zeros((length, rest), f32)
    keep = jnp.concatenate([cosine, cosine, ones], axis=1)
    from_above = jnp.concatenate([-sine, zero_half, zero_rest], axis=1)
    from_below = jnp.concatenate([zero_half, sine, zero_rest], axis=1)
    times = lanes // depth
    return tuple(jnp.tile(table, (1, times)) for table in (keep, from_above, from_below))


def turn(values, keep, above, below, sign):
    lanes = values.shape[-1]
    half = ROTARY // 2
    up = pltpu.roll(values, lanes - half, 1)
    down = pltpu.roll(values, half, 1)
    return values * keep + sign * (up * above + down * below)


def qkv_kernel(
    z_ref, x_ref, gain_ref, shift_ref, wq_ref, wk_ref, wv_ref, a_ref, b_ref, bias_ref,
    keep_ref, above_ref, below_ref, q_ref, k_ref, v_ref, first_ref, mid_ref,
):
    cols = wq_ref.shape[1]
    x = x_ref[...].reshape(x_ref.shape[2:]).astype(f32)
    centre = x - jnp.mean(x, axis=-1, keepdims=True)
    spread = jnp.mean(centre * centre, axis=-1, keepdims=True)
    first = (centre * lax.rsqrt(spread + norm_eps) * gain_ref[...] + shift_ref[...]).astype(bf16)
    mid = nn(first, a_ref[...]).astype(bf16)
    first_ref[...] = first.reshape(first_ref.shape)
    mid_ref[...] = mid.reshape(mid_ref.shape)
    low = adapter_scale * nn(mid, b_ref[...]) + bias_ref[...]
    lanes = keep_ref.shape[1]
    tables = keep_ref[...], above_ref[...], below_ref[...]
    query = nn(first, wq_ref[...]) + low[:, :cols]
    keys = nn(first, wk_ref[...]) + low[:, cols : 2 * cols]
    values = nn(first, wv_ref[...]) + low[:, 2 * cols :]
    for at in range(0, cols, lanes):
        part = slice(at, at + lanes)
        q_ref[0, :, part] = turn(query[:, part], *tables, 1.0).astype(bf16)
        k_ref[0, :, part] = turn(keys[:, part], *tables, 1.0).astype(bf16)
    v_ref[0] = values.astype(bf16)


MESH = pl.DeviceIdType.MESH


def attend_pair(query, keys, values, grad, tables, dk_ref, dv_ref, depth, blocks, store):
    lanes = keys.shape[1]
    span = keys.shape[0] // blocks
    scale = 1.0 / math.sqrt(depth)
    lane = lax.broadcasted_iota(jnp.int32, (1, lanes), 1)
    masks = [jnp.where(lane // depth == h, 1.0, 0.0).astype(bf16) for h in range(lanes // depth)]
    diagonal = lax.broadcasted_iota(jnp.int32, (span, span), 0) <= lax.broadcasted_iota(
        jnp.int32, (span, span), 1
    )
    keys_t, values_t = keys.T, values.T
    dk_ref[...] = jnp.zeros_like(dk_ref)
    dv_ref[...] = jnp.zeros_like(dv_ref)
    for i in range(blocks):
        rows = slice(i * span, (i + 1) * span)
        end = (i + 1) * span
        q_i, g_i = query[rows], grad[rows]
        g_t = g_i.T
        outs, grads = [], []
        dk, dv = None, None
        for h, mask in enumerate(masks):
            part = slice(h * depth, (h + 1) * depth)
            q_h, g_h = q_i * mask, g_i * mask
            scores = nt(keys[:end], q_h) * scale
            last = jnp.where(diagonal, scores[i * span :], masked_score)
            scores = last if i == 0 else jnp.concatenate([scores[: i * span], last], axis=0)
            weights = jnp.exp(scores - jnp.max(scores, axis=0, keepdims=True))
            weights = weights * (1.0 / jnp.sum(weights, axis=0, keepdims=True))
            low = weights.astype(bf16)
            out_t = nn(values_t[part, :end], low)
            grad_p = nt(values[:end], g_h)
            delta = jnp.sum(out_t * g_t[part].astype(f32), axis=0, keepdims=True)
            grad_s = (weights * (grad_p - delta)).astype(bf16)
            outs.append(out_t)
            grads.append(nn(keys_t[part, :end], grad_s))
            dk_h, dv_h = nn(grad_s, q_h), nn(low, g_h)
            dk = dk_h if dk is None else dk + dk_h
            dv = dv_h if dv is None else dv + dv_h
        dk_ref[:end] += dk
        dv_ref[:end] += dv
        store(i, 0, jnp.concatenate(outs, axis=0).T.astype(bf16))
        dq = jnp.concatenate(grads, axis=0).T * scale
        store(i, 1, turn(dq, *[t[rows] for t in tables], -1.0).astype(bf16))
    for i in range(blocks):
        rows = slice(i * span, (i + 1) * span)
        dk = dk_ref[rows] * scale
        store(i, 2, turn(dk, *[t[rows] for t in tables], -1.0).astype(bf16))
        store(i, 3, dv_ref[rows].astype(bf16))


def middle_kernel(
    q_ref, k_ref, v_ref, g_ref, keep_ref, above_ref, below_ref, mid_qkv_t_ref,
    second_ref, low_ref, mid_ref, mid_t_ref, dmid_ref, dmid_t_ref,
    up_ref, down_ref, a_ref, b_ref, bias_ref,
    local_ref, own_ref, ff_ref, back_ref, mid_ff_ref, dmid_up_ref, ga_ref, gb_ref,
    buffer, dk_ref, dv_ref, mid_acc, dmid_acc, send_sem, recv_sem, own_sem,
    *, n, pairs, steps, depth,
):
    step = pl.program_id(0)
    z = lax.axis_index("blk")
    dp = lax.axis_index("dp")
    lanes = q_ref.shape[2]

    def copies(s):
        seq, pair = s // pairs, lax.rem(s, pairs)
        at = pl.ds(pl.multiple_of((z * pairs + pair) * lanes, lanes), lanes)
        target = local_ref.at[seq, :, :, at]
        own = pltpu.make_async_copy(buffer.at[s, z], target, own_sem.at[s])
        away = []
        for t in range(1, n):
            peer = lax.rem(z + t, n)
            away.append(
                pltpu.make_async_remote_copy(
                    src_ref=buffer.at[s, peer], dst_ref=target,
                    send_sem=send_sem.at[s, t], recv_sem=recv_sem.at[s, t],
                    device_id=(dp, peer), device_id_type=MESH,
                )
            )
        return own, away

    @pl.when(step == 0)
    def _():
        barrier = pltpu.get_barrier_semaphore()
        for t in range(1, n):
            pl.semaphore_signal(barrier, inc=1, device_id=(dp, lax.rem(z + t, n)), device_id_type=MESH)
        pl.semaphore_wait(barrier, n - 1)

    @pl.when(step < steps)
    def _():
        def store(i, kind, value):
            buffer[step, i, kind] = value
            if kind:
                own_ref[0, kind - 1, i * value.shape[0] : (i + 1) * value.shape[0], :] = value

        tables = keep_ref[...], above_ref[...], below_ref[...]
        attend_pair(q_ref[0], k_ref[0], v_ref[0], g_ref[0], tables, dk_ref, dv_ref, depth, n, store)
        own, away = copies(step)
        own.start()
        for copy in away:
            copy.start()

    @pl.when(step == steps)
    def _():
        ff_ref[...] = jnp.zeros_like(ff_ref)
        back_ref[...] = jnp.zeros_like(back_ref)
        mid_acc[...] = jnp.zeros_like(mid_acc)
        dmid_acc[...] = jnp.zeros_like(dmid_acc)

    @pl.when(step >= steps)
    def _():
        total = second_ref.shape[0]
        size = 256 if total % 256 == 0 else 128
        for at in range(0, total, size):
            rows = slice(at, at + size)
            pre = nn(second_ref[rows], up_ref[...]) + bias_ref[...] + adapter_scale * nn(mid_ref[rows], b_ref[...])
            cdf = 0.5 + 0.5 * lax.erf(pre * (1.0 / math.sqrt(2.0)))
            hidden = (pre * cdf).astype(bf16)
            slope = cdf + pre * (jnp.exp(-0.5 * pre * pre) * (1.0 / math.sqrt(2.0 * math.pi)))
            grad_hidden = nt(low_ref[rows], down_ref[...]) + nt(dmid_ref[rows], a_ref[...])
            dup = (slope * grad_hidden).astype(bf16)
            ff_ref[rows] += nn(hidden, down_ref[...])
            back_ref[rows] += nt(dup, up_ref[...])
            mid_acc[rows] += nn(hidden, a_ref[...])
            dmid_acc[rows] += nt(dup, b_ref[...])
            ga = nn(dmid_t_ref[:, rows], hidden)
            gb = nn(mid_t_ref[:, rows], dup)
            ga_ref[...] = ga if at == 0 else ga_ref[...] + ga
            gb_ref[...] = gb if at == 0 else gb_ref[...] + gb

    @pl.when(step == pl.num_programs(0) - 1)
    def _():
        mid_ff_ref[...] = mid_acc[...].astype(bf16)
        dmid_up_ref[...] = (adapter_scale * dmid_acc[...]).astype(bf16)
        for s in range(steps):
            own, away = copies(s)
            own.wait()
            for copy in away:
                copy.wait()


def finish_kernel(
    local_ref, wo_ref, wq_ref, wk_ref, wv_ref, a_out_ref, a_qkv_ref, b_out_ref, bq_ref, bk_ref, bv_ref,
    bias_ref, x_ref, cot_ref, weight_ref, ff_ref, bias_ff_ref, mid_ff_ref, b_ff_ref,
    second_ref, dmid_up_ref, a_up_ref, gain_ref, dmid_out_t_ref, low_ref,
    mixed_ref, tokens_ref, norm_ref, ga_ref, gb_ref,
    att_acc, mid_acc, first_acc, dmid_acc,
):
    t = pl.program_id(0)
    rows = x_ref.shape[0] * x_ref.shape[1]
    cols = wq_ref.shape[1]

    @pl.when(t == 0)
    def _():
        att_acc[...] = jnp.zeros_like(att_acc)
        mid_acc[...] = jnp.zeros_like(mid_acc)
        first_acc[...] = jnp.zeros_like(first_acc)
        dmid_acc[...] = jnp.zeros_like(dmid_acc)

    out, dq, dk, dv = (local_ref[:, i].reshape(rows, cols) for i in range(4))
    att_acc[...] += nn(out, wo_ref[...])
    mid_acc[...] += nn(out, a_out_ref[...])
    first_acc[...] += nt(dq, wq_ref[...]) + nt(dk, wk_ref[...]) + nt(dv, wv_ref[...])
    dmid_acc[...] += nt(dq, bq_ref[...]) + nt(dk, bk_ref[...]) + nt(dv, bv_ref[...])
    ga_ref[...] = nn(dmid_out_t_ref[...], out)

    @pl.when(t == pl.num_programs(0) - 1)
    def _():
        size = x_ref.shape[1]
        norm = [jnp.zeros((1, first_acc.shape[1]), f32) for _ in range(4)]
        for q in range(x_ref.shape[0]):
            part = slice(q * size, (q + 1) * size)
            x = x_ref[q].astype(f32)
            mid = mid_acc[part].astype(bf16)
            gb = tn(mid, low_ref[part])
            gb_ref[...] = gb if q == 0 else gb_ref[...] + gb
            att = att_acc[part] + bias_ref[...] + adapter_scale * nn(mid, b_out_ref[...])
            ff = ff_ref[part] + bias_ff_ref[...] + adapter_scale * nn(mid_ff_ref[part], b_ff_ref[...])
            mixed_ref[q] = (x + att + ff).astype(bf16)
            dmid = (adapter_scale * dmid_acc[part]).astype(bf16)
            grad_first = first_acc[part] + nt(dmid, a_qkv_ref[...])
            grad_second = second_ref[part] + nt(dmid_up_ref[part], a_up_ref[...])
            centre = x - jnp.mean(x, axis=-1, keepdims=True)
            inv = lax.rsqrt(jnp.mean(centre * centre, axis=-1, keepdims=True) + norm_eps)
            unit = centre * inv
            pulled = grad_first * gain_ref[0:1] + grad_second * gain_ref[1:2]
            back = inv * (
                pulled
                - jnp.mean(pulled, axis=-1, keepdims=True)
                - unit * jnp.mean(pulled * unit, axis=-1, keepdims=True)
            )
            row_grad = cot_ref[q].astype(f32) * weight_ref[part]
            tokens_ref[q] = (row_grad + back).astype(bf16)
            for k, value in enumerate((grad_first * unit, grad_second * unit, grad_first, grad_second)):
                norm[k] += jnp.sum(value, axis=0, keepdims=True)
        norm_ref[...] = jnp.concatenate(norm, axis=0)


def adam_update(param, grad, mean, square, keep):
    mean_new = 0.9 * mean + 0.1 * grad
    square_new = 0.999 * square + 0.001 * grad * grad
    fresh = param - 0.01 * (mean_new / first_fix) / (jnp.sqrt(square_new / second_fix) + 1e-08)
    kept = keep.astype(f32)
    return (fresh, mean_new * kept, square_new * kept)


def body(
    dp_n,
    n,
    tokens,
    cotangent,
    domain_ids,
    domain_weight,
    frozen_input_weights,
    bias_in,
    frozen_down_weight,
    bias_ff,
    norm_gain,
    norm_shift,
    adapt_a,
    adapt_a_ff,
    adapt_b,
    adapt_b_ff,
    mean_a,
    mean_a_ff,
    mean_b,
    mean_b_ff,
    square_a,
    square_a_ff,
    square_b,
    square_b_ff,
    keep_a,
    keep_a_ff,
    keep_b,
    keep_b_ff,
):
    seqs, span, width = tokens.shape
    rows = seqs * span
    rank = adapt_b.shape[0]
    depth = width // HEADS
    cz = width // n
    length = n * span
    z = lax.axis_index("blk")
    z_arr = jnp.full((1,), z, jnp.int32)
    kr = frozen_input_weights.shape[0]
    down_rows, inner = frozen_down_weight.shape[0], frozen_down_weight.shape[0] * dp_n
    lanes = 128

    def shift_by(values, s):
        return lax.ppermute(values, "blk", [(i, (i + s) % n) for i in range(n)])

    b_cols = adapt_b.shape[1] + adapt_b_ff.shape[1]
    b_shard = jnp.concatenate([adapt_b, adapt_b_ff], axis=1).astype(bf16)
    one = jnp.concatenate(
        [frozen_input_weights[:, : 4 * width], adapt_a.astype(bf16), b_shard.reshape(kr, -1)], axis=1
    )
    one = lax.all_gather(one, "dp", axis=0, tiled=True)
    two = lax.all_gather(frozen_input_weights[:, 4 * width :], "dp", axis=0, tiled=True)
    three = jnp.concatenate([frozen_down_weight, adapt_a_ff.astype(bf16)], axis=1)
    three = lax.all_gather(three, "dp", axis=0, tiled=True)
    a_at = 4 * width
    b_at = a_at + 3 * rank
    a_all = one[:, a_at:b_at]
    b_all = one[:, b_at:].reshape(dp_n, rank, b_cols)
    b_in = jnp.transpose(b_all[:, :, : adapt_b.shape[1]], (1, 0, 2)).reshape(rank, -1)
    b_ff = jnp.transpose(b_all[:, :, adapt_b.shape[1] :], (1, 0, 2)).reshape(rank, width)
    w_out = one[:, 3 * width : 4 * width]
    w_up = two
    w_down, a_ff = three[:, :width], three[:, width:]

    right, left = tokens, tokens
    rights, lefts = [None], [None]
    for s in range(1, n):
        right = lax.ppermute(right, "blk", [(i, i + 1) for i in range(n - 1)])
        left = lax.ppermute(left, "blk", [(i + 1, i) for i in range(n - 1)])
        rights.append(right)
        lefts.append(left)
    x_all = jnp.stack(
        [tokens] + [jnp.where(z >= s, rights[s], lefts[n - s]) for s in range(1, n)]
    )

    lookup = (domain_ids[..., None] == jnp.arange(DOMAINS, dtype=jnp.int32)).astype(f32)
    row_weight = jnp.sum(lookup * domain_weight, axis=-1).reshape(rows, 1)
    row_grad = cotangent.astype(f32).reshape(rows, width) * row_weight
    grad_low = row_grad.astype(bf16)
    b_out = b_in[:, 3 * width : 4 * width]
    a_out = a_all[:, rank : 2 * rank]
    dmid_out = (adapter_scale * nt(grad_low, b_out)).astype(bf16)
    grad_att = (nt(grad_low, w_out) + nt(dmid_out, a_out)).astype(bf16)
    grad_att = jnp.transpose(grad_att.reshape(seqs, span, n, cz), (2, 0, 1, 3))

    def piece(values, s):
        return lax.dynamic_index_in_dim(values, lax.rem(z + s, n), 0, keepdims=False)

    g_all = jnp.stack(
        [piece(grad_att, 0)] + [shift_by(piece(grad_att, s), s) for s in range(1, n)]
    )

    tables = rope_lane_tables(length, depth, lanes)
    own = [lax.dynamic_slice_in_dim(b_in[:, t * width : (t + 1) * width], z * cz, cz, 1) for t in range(3)]
    b_own = jnp.concatenate(own, axis=1)
    bias32 = bias_in.astype(f32)
    bias_own = jnp.concatenate(
        [lax.dynamic_slice_in_dim(bias32, t * width + z * cz, cz, 0) for t in range(3)]
    ).reshape(1, 3 * cz)

    def block_of(s, z_ref):
        return lax.rem(z_ref[0] - s + n, n)

    table_spec = pl.BlockSpec((span, lanes), lambda s, q, z_ref: (block_of(s, z_ref), 0))
    head_spec = pl.BlockSpec((1, span, cz), lambda s, q, z_ref: (q, block_of(s, z_ref), 0))
    query, keys, values, first_all, mid_all = pl.pallas_call(
        qkv_kernel,
        grid_spec=pltpu.PrefetchScalarGridSpec(
            num_scalar_prefetch=1,
            grid=(n, seqs),
            in_specs=[
                pl.BlockSpec((1, 1, span, width), lambda s, q, z_ref: (s, q, 0, 0)),
                pl.BlockSpec((1, width), lambda s, q, z_ref: (0, 0)),
                pl.BlockSpec((1, width), lambda s, q, z_ref: (0, 0)),
                pl.BlockSpec((width, cz), lambda s, q, z_ref: (0, z_ref[0])),
                pl.BlockSpec((width, cz), lambda s, q, z_ref: (0, n + z_ref[0])),
                pl.BlockSpec((width, cz), lambda s, q, z_ref: (0, 2 * n + z_ref[0])),
                pl.BlockSpec((width, rank), lambda s, q, z_ref: (0, a_at // rank)),
                pl.BlockSpec((rank, 3 * cz), lambda s, q, z_ref: (0, 0)),
                pl.BlockSpec((1, 3 * cz), lambda s, q, z_ref: (0, 0)),
                table_spec,
                table_spec,
                table_spec,
            ],
            out_specs=[
                head_spec,
                head_spec,
                head_spec,
                pl.BlockSpec((1, 1, span, width), lambda s, q, z_ref: (block_of(s, z_ref), q, 0, 0)),
                pl.BlockSpec((1, 1, span, rank), lambda s, q, z_ref: (block_of(s, z_ref), q, 0, 0)),
            ],
        ),
        out_shape=[jax.ShapeDtypeStruct((seqs, length, cz), bf16)] * 3
        + [
            jax.ShapeDtypeStruct((n, seqs, span, width), bf16),
            jax.ShapeDtypeStruct((n, seqs, span, rank), bf16),
        ],
        compiler_params=pltpu.CompilerParams(vmem_limit_bytes=48 << 20),
        cost_estimate=pl.CostEstimate(
            flops=2 * n * rows * width * 4 * cz, bytes_accessed=6 * n * rows * width, transcendentals=0
        ),
        name="qkv",
    )(
        z_arr, x_all, norm_gain[0:1], norm_shift[0:1], one, one, one, one, b_own, bias_own, *tables
    )

    input_rows = tokens.astype(f32).reshape(rows, width)
    centre = input_rows - jnp.mean(input_rows, axis=-1, keepdims=True)
    inv = lax.rsqrt(jnp.mean(centre * centre, axis=-1, keepdims=True) + norm_eps)
    second = (centre * inv * norm_gain[1] + norm_shift[1]).astype(bf16)
    a_up = a_all[:, 2 * rank :]
    mid_up = nn(second, a_up).astype(bf16)
    dmid_ff = (adapter_scale * nt(grad_low, b_ff)).astype(bf16)
    pairs = cz // lanes
    steps = seqs * pairs
    inner_block = min(512, inner)
    g_pos = jnp.concatenate([g_all, g_all])
    g_pos = lax.rev(g_pos, (0,))
    g_pos = lax.dynamic_slice_in_dim(g_pos, lax.rem(n - 1 - z + n, n), n, 0)
    g_pos = jnp.transpose(g_pos, (1, 0, 2, 3)).reshape(seqs, length, cz)

    def one_buffer(shape):
        zeros = (0,) * len(shape)
        return pl.BlockSpec(shape, lambda s: zeros, pipeline_mode=pl.Buffered(1))

    def seq_pair(s):
        s = jnp.minimum(s, steps - 1)
        return s // pairs, lax.rem(s, pairs)

    def head_map(s):
        seq, pair = seq_pair(s)
        return seq, 0, pair

    def inner_at(s):
        return jnp.maximum(s - steps, 0)

    head = pl.BlockSpec((1, length, lanes), head_map)
    local, own, ff, grad_second, mid_ff, dmid_up, grad_a_ff_t, grad_b_up = pl.pallas_call(
        functools.partial(middle_kernel, n=n, pairs=pairs, steps=steps, depth=depth),
        grid=(steps + inner // inner_block,),
        in_specs=[head] * 4
        + [one_buffer((length, lanes))] * 3
        + [one_buffer((8, lanes))]
        + [one_buffer((rows, width))] * 2
        + [one_buffer((rows, rank)), one_buffer((rank, rows))] * 2
        + [
            pl.BlockSpec((width, inner_block), lambda s: (0, inner_at(s))),
            pl.BlockSpec((inner_block, width), lambda s: (inner_at(s), 0)),
            pl.BlockSpec((inner_block, rank), lambda s: (inner_at(s), width // rank)),
            pl.BlockSpec((rank, inner_block), lambda s: (0, 4 * width // inner_block + inner_at(s))),
            pl.BlockSpec((1, inner_block), lambda s: (0, 4 * width // inner_block + inner_at(s))),
        ],
        out_specs=[
            pl.BlockSpec(memory_space=pl.ANY),
            pl.BlockSpec((1, 3, length, lanes), lambda s: (seq_pair(s)[0], 0, 0, seq_pair(s)[1])),
            one_buffer((rows, width)),
            one_buffer((rows, width)),
            one_buffer((rows, rank)),
            one_buffer((rows, rank)),
            pl.BlockSpec((rank, inner_block), lambda s: (0, inner_at(s))),
            pl.BlockSpec((rank, inner_block), lambda s: (0, inner_at(s))),
        ],
        out_shape=[
            jax.ShapeDtypeStruct((seqs, 4, span, width), bf16),
            jax.ShapeDtypeStruct((seqs, 3, length, cz), bf16),
            jax.ShapeDtypeStruct((rows, width), f32),
            jax.ShapeDtypeStruct((rows, width), f32),
            jax.ShapeDtypeStruct((rows, rank), bf16),
            jax.ShapeDtypeStruct((rows, rank), bf16),
            jax.ShapeDtypeStruct((rank, inner), f32),
            jax.ShapeDtypeStruct((rank, inner), f32),
        ],
        scratch_shapes=[
            pltpu.VMEM((steps, n, 4, span, lanes), bf16),
            pltpu.VMEM((length, lanes), f32),
            pltpu.VMEM((length, lanes), f32),
            pltpu.VMEM((rows, rank), f32),
            pltpu.VMEM((rows, rank), f32),
            pltpu.SemaphoreType.DMA((steps, n)),
            pltpu.SemaphoreType.DMA((steps, n)),
            pltpu.SemaphoreType.DMA((steps,)),
        ],
        compiler_params=pltpu.CompilerParams(
            collective_id=0, has_side_effects=True, vmem_limit_bytes=60 << 20
        ),
        name="middle",
    )(
        query, keys, values, g_pos, *tables, tables[0][:8], second, grad_low, mid_up, mid_up.T, dmid_ff, dmid_ff.T,
        w_up, three, three, b_in, bias32.reshape(1, -1),
    )
    grad_b_up = adapter_scale * grad_b_up

    first_pos = jnp.transpose(first_all, (1, 0, 2, 3)).reshape(seqs * length, width)
    mid_pos = jnp.transpose(mid_all, (1, 0, 2, 3)).reshape(seqs * length, rank)
    djoint_own = [own[:, t].reshape(seqs * length, cz) for t in range(3)]
    dmid_own = sum(nt(djoint_own[t], b_own[:, t * cz : (t + 1) * cz]) for t in range(3))
    dmid_own = (adapter_scale * dmid_own).astype(bf16)
    grad_a_qkv_t = tn(dmid_own, first_pos)
    mine = (jnp.arange(n, dtype=jnp.int32) == z)[None, :, None]
    grad_b_qkv = jnp.concatenate(
        [
            jnp.where(mine, adapter_scale * tn(mid_pos, part)[:, None, :], 0.0).reshape(rank, width)
            for part in djoint_own
        ],
        axis=1,
    )
    grad_a_up_t = tn(dmid_up, second)
    grad_b_ffp = adapter_scale * tn(mid_ff, grad_low)

    def fixed(shape, *at):
        return pl.BlockSpec(shape, lambda t: at, pipeline_mode=pl.Buffered(1))

    def column(at, height):
        return pl.BlockSpec((height, cz), lambda t: (0, at * n + t))

    mixed, grad_tokens, norm_part, grad_a_out_t, grad_b_out = pl.pallas_call(
        finish_kernel,
        grid=(n,),
        in_specs=[
            pl.BlockSpec((seqs, 4, span, cz), lambda t: (0, 0, 0, t)),
            pl.BlockSpec((cz, width), lambda t: (t, 3)),
            column(0, width), column(1, width), column(2, width),
            pl.BlockSpec((cz, rank), lambda t: (t, a_at // rank + 1)),
            fixed((width, rank), 0, a_at // rank),
            fixed((rank, width), 0, 3),
            column(0, rank), column(1, rank), column(2, rank),
            fixed((1, width), 0, 3),
            fixed((seqs, span, width), 0, 0, 0),
            fixed((seqs, span, width), 0, 0, 0),
            fixed((rows, 1), 0, 0),
            fixed((rows, width), 0, 0),
            fixed((1, width), 0, 0),
            fixed((rows, rank), 0, 0),
            fixed((rank, width), 0, 0),
            fixed((rows, width), 0, 0),
            fixed((rows, rank), 0, 0),
            fixed((width, rank), 0, a_at // rank + 2),
            fixed((2, width), 0, 0),
            fixed((rank, rows), 0, 0),
            fixed((rows, width), 0, 0),
        ],
        out_specs=[
            fixed((seqs, span, width), 0, 0, 0),
            fixed((seqs, span, width), 0, 0, 0),
            fixed((4, width), 0, 0),
            pl.BlockSpec((rank, cz), lambda t: (0, t)),
            fixed((rank, width), 0, 0),
        ],
        out_shape=[
            jax.ShapeDtypeStruct((seqs, span, width), bf16),
            jax.ShapeDtypeStruct((seqs, span, width), bf16),
            jax.ShapeDtypeStruct((4, width), f32),
            jax.ShapeDtypeStruct((rank, width), f32),
            jax.ShapeDtypeStruct((rank, width), f32),
        ],
        scratch_shapes=[
            pltpu.VMEM((rows, width), f32),
            pltpu.VMEM((rows, rank), f32),
            pltpu.VMEM((rows, width), f32),
            pltpu.VMEM((rows, rank), f32),
        ],
        compiler_params=pltpu.CompilerParams(vmem_limit_bytes=56 << 20),
        name="finish",
    )(
        local, one, one, one, one, one, one, b_in, b_in, b_in, b_in, bias32.reshape(1, -1),
        tokens, cotangent, row_weight, ff, bias_ff.astype(f32).reshape(1, -1), mid_ff, b_ff,
        grad_second, dmid_up, one, norm_gain, dmid_out.T, grad_low,
    )
    grad_b_out = adapter_scale * grad_b_out

    def by_owner(values):
        return values.reshape(rank, dp_n, -1)

    parts = [
        by_owner(grad_a_qkv_t), by_owner(grad_a_out_t), by_owner(grad_a_up_t), by_owner(grad_a_ff_t),
        by_owner(jnp.concatenate([grad_b_qkv, grad_b_out, grad_b_up], axis=1)), by_owner(grad_b_ffp),
    ]
    widths = [p.shape[2] for p in parts]
    owned = jnp.transpose(jnp.concatenate(parts, axis=2), (1, 0, 2))
    norm_rows = jnp.broadcast_to(norm_part.reshape(1, -1, owned.shape[2]), (dp_n, 4 * width // owned.shape[2], owned.shape[2]))
    owned = jnp.concatenate([owned, norm_rows], axis=1)
    owned = lax.psum_scatter(owned, "dp", scatter_dimension=0, tiled=True)
    owned = lax.psum(owned[0], "blk")
    norm_sum = owned[rank:].reshape(4, width)
    grad_gain, grad_shift = norm_sum[:2], norm_sum[2:]
    cuts = [sum(widths[:i]) for i in range(len(widths) + 1)]
    pieces = [owned[:rank, cuts[i] : cuts[i + 1]] for i in range(len(widths))]
    grad_a = jnp.concatenate([p.T for p in pieces[:3]], axis=1)
    grad_a_ff = pieces[3].T
    grad_b, grad_b_ff = pieces[4], pieces[5]

    fresh_a, new_mean_a, new_square_a = adam_update(adapt_a, grad_a, mean_a, square_a, keep_a)
    fresh_a_ff, new_mean_a_ff, new_square_a_ff = adam_update(
        adapt_a_ff, grad_a_ff, mean_a_ff, square_a_ff, keep_a_ff
    )
    fresh_b, new_mean_b, new_square_b = adam_update(adapt_b, grad_b, mean_b, square_b, keep_b)
    fresh_b_ff, new_mean_b_ff, new_square_b_ff = adam_update(
        adapt_b_ff, grad_b_ff, mean_b_ff, square_b_ff, keep_b_ff
    )
    fresh = jnp.concatenate([fresh_b, fresh_b_ff], axis=1).astype(bf16)
    fresh = lax.all_gather(fresh, "dp", axis=0, tiled=False)
    fresh_in = jnp.transpose(fresh[:, :, : adapt_b.shape[1]], (1, 0, 2)).reshape(rank, -1)
    fresh_ff = jnp.transpose(fresh[:, :, adapt_b.shape[1] :], (1, 0, 2)).reshape(rank, width)
    fa = fresh_a.astype(bf16)
    update = jnp.concatenate(
        [
            nn(fa[:, :rank], fresh_in[:, : 3 * width]),
            nn(fa[:, rank : 2 * rank], fresh_in[:, 3 * width : 4 * width]),
            nn(fa[:, 2 * rank :], fresh_in[:, 4 * width :]),
        ],
        axis=1,
    )
    folded_input_weights = (frozen_input_weights.astype(f32) + adapter_scale * update).astype(bf16)
    folded_down_weight = (
        frozen_down_weight.astype(f32) + adapter_scale * nn(fresh_a_ff.astype(bf16), fresh_ff)
    ).astype(bf16)
    return (
        mixed,
        grad_tokens,
        grad_gain,
        grad_shift,
        grad_a,
        grad_a_ff,
        grad_b,
        grad_b_ff,
        new_mean_a,
        new_square_a,
        new_mean_a_ff,
        new_square_a_ff,
        new_mean_b,
        new_square_b,
        new_mean_b_ff,
        new_square_b_ff,
        folded_input_weights,
        folded_down_weight,
    )


def solution(mesh):
    in_specs = (
        P("dp", "blk", None),
        P("dp", "blk", None),
        P("dp", "blk"),
        P(),
        P("dp", None),
        P(),
        P("dp", None),
        P(),
        P(),
        P(),
        P("dp", None),
        P("dp", None),
        P(None, "dp"),
        P(None, "dp"),
        P("dp", None),
        P("dp", None),
        P(None, "dp"),
        P(None, "dp"),
        P("dp", None),
        P("dp", None),
        P(None, "dp"),
        P(None, "dp"),
        P("dp", None),
        P("dp", None),
        P(None, "dp"),
        P(None, "dp"),
    )
    out_specs = (
        P("dp", "blk", None),
        P("dp", "blk", None),
        P(),
        P(),
        P("dp", None),
        P("dp", None),
        P(None, "dp"),
        P(None, "dp"),
        P("dp", None),
        P("dp", None),
        P("dp", None),
        P("dp", None),
        P(None, "dp"),
        P(None, "dp"),
        P(None, "dp"),
        P(None, "dp"),
        P("dp", None),
        P("dp", None),
    )
    return jax.shard_map(
        functools.partial(body, mesh.shape["dp"], mesh.shape["blk"]), mesh=mesh, in_specs=in_specs, out_specs=out_specs, check_vma=False)
```

time: 999 us -> 639 us (0.64)
  matrix products: 326 us -> 29.7 us
  Pallas kernels: 0 us -> 190 us
  waiting for transfers between devices: 400 us -> 212 us
  blocking collectives: 121 us -> 0 us
  local copies, waits for them, and re-layouts: 58.5 us -> 108 us
  starting transfers between devices: 0.62 us -> 37 us
  other arithmetic: 68.4 us -> 42.7 us
    dot_general x42 -> x17, matrix products: 326 us -> 29.7 us  [the longest x6 11.2 us: nt(): lax.dot_general(left, right, (((1,), (1,)), ((), ())), preferred_element_...]
    all_gather x9 -> x4, waiting for transfers between devices: 295 us -> 0.01 us  [the longest x1 0.01 us: body(): one = lax.all_gather(one, 'dp', axis=0, tiled=True)]
    pallas_call x0 -> x3, Pallas kernels: none -> 190 us  [the longest x1 146 us: body(): pl.pallas_call(functools.partial(middle_kernel, n=n, pairs=pairs, steps=s...]
    all_gather x5 -> x0, blocking collectives: 81.6 us -> none  [the longest x1 27.6 us: body(): lax.all_gather(delta.astype(jnp.bfloat16), 'blk', axis=2, tiled=True)]
    reduce_scatter x0 -> x1, waiting for transfers between devices: none -> 77.7 us  [body(): owned = lax.psum_scatter(owned, 'dp', scatter_dimension=0, tiled=True)]
    ppermute x0 -> x9, waiting for transfers between devices: none -> 77.3 us  [the longest x3 71.8 us: body(): right = lax.ppermute(right, 'blk', [(i, i + 1) for i in range(n - 1)])]
    psum x1, waiting for transfers between devices: 104 us -> 56 us  [body(): owned = lax.psum(owned[0], 'blk')]
    psum x1 -> x0, blocking collectives: 39.3 us -> none  [body(): lax.psum((grad_a_part, grad_a_ffp, grad_b_part, grad_b_ffp, gain_part, sh...]
  transfers between devices with their start and end apart: 10 -> 15, of which waited for: 8 -> 6; matrix products, arithmetic and copies ran while one was open for 36% -> 18% of each run, Pallas kernels for 0% -> 3%
where the time goes in v1:
time: 639 us; the launch traced here: 634 us
  waiting for transfers between devices  212 us (33%)
  Pallas kernels  190 us (30%)
  local copies, waits for them, and re-layouts  108 us (17%)
  other arithmetic  42.7 us (7%)
  starting transfers between devices  37 us (6%)
  matrix products  29.7 us (5%)
  between operations  15.3 us (2%)
    pallas_call x1, Pallas kernels, body(): pl.pallas_call(functools.partial(middle_kernel, n=n, pairs=pairs, steps=s...  146 us
    reduce_scatter x1, waiting for transfers between devices, body(): owned = lax.psum_scatter(owned, 'dp', scatter_dimension=0, tiled=True)  77.7 us
    ppermute x3, waiting for transfers between devices, body(): right = lax.ppermute(right, 'blk', [(i, i + 1) for i in range(n - 1)])  71.8 us
    psum x1, waiting for transfers between devices, body(): owned = lax.psum(owned[0], 'blk')  56 us
    unnamed x155, local copies, waits for them, and re-layouts  51.2 us
    pallas_call x1, Pallas kernels, body(): pl.pallas_call(finish_kernel, grid=(n,), in_specs=[pl.BlockSpec((seqs, 4,...  23.2 us
    pallas_call x1, Pallas kernels, body(): pl.pallas_call(qkv_kernel, grid_spec=pltpu.PrefetchScalarGridSpec(num_sca...  19.8 us
    ppermute x3, starting transfers between devices, body(): right = lax.ppermute(right, 'blk', [(i, i + 1) for i in range(n - 1)])  17.2 us
  transfers between devices with their start and end apart: 15, of which 6 were waited for; matrix products, arithmetic and copies ran while one was open for 18% of the time, Pallas kernels for 3%

profile of v1, /device:TPU:0, one launch (start us, length us, event | category | flops | bytes accessed | tf_op | source)
XLA Modules:
  0.0 634.3 jit_solution(2651702310416220199)
XLA Ops:
  7.3 2.8 fusion.52
  13.8 6.1 collective-permute-start
  21.2 31.1 %collective-permute-done = bf16[3,256,1024]{2,1,0:T(8,128)(2,1)} collective-permute-done((bf16[3,256,1024]{2,1,0:T(8,128)(2,1)S(1)}, bf16[3,256,1024]{2,1,0:T(8,128)(2,1)}, u32[]{:S(2)}, u32[]{:S(2)}) %collective-permute-start) | collective-permute-done | bytes 1572896 | tf_op jit(solution)/shard_map/ppermute | solution.py:360
  52.3 5.6 collective-permute-start.4
  66.7 23.2 %collective-permute-done.4 = bf16[3,256,1024]{2,1,0:T(8,128)(2,1)} collective-permute-done((bf16[3,256,1024]{2,1,0:T(8,128)(2,1)}, bf16[3,256,1024]{2,1,0:T(8,128)(2,1)}, u32[]{:S(2)}, u32[]{:S(2)}) %collective-permute-start.4) | collective-permute-done | bytes 1572896 | tf_op jit(solution)/shard_map/ppermute | solution.py:360
  89.9 5.5 collective-permute-start.5
  98.5 1.8 fusion.8.second_ref
  100.2 2.6 copy.250
  102.8 3.0 multiply_convert_fusion
  108.9 17.6 %collective-permute-done.5 = bf16[3,256,1024]{2,1,0:T(8,128)(2,1)} collective-permute-done((bf16[3,256,1024]{2,1,0:T(8,128)(2,1)}, bf16[3,256,1024]{2,1,0:T(8,128)(2,1)}, u32[]{:S(2)}, u32[]{:S(2)}) %collective-permute-start.5) | collective-permute-done | bytes 1572896 | tf_op jit(solution)/shard_map/ppermute | solution.py:360
  128.0 5.4 collective-permute-done.3
  135.0 3.2 pad_maximum_fusion.1.x_ref
  138.2 1.8 slice.160
  144.4 3.5 fusion.10
  147.9 2.7 add_convert_fusion
  150.7 2.9 reshape.228
  153.6 4.0 constant_dynamic-slice_fusion
  161.7 14.1 %collective-permute-start.8 = (bf16[3,256,256]{2,1,0:T(8,128)(2,1)}, bf16[3,256,256]{2,1,0:T(8,128)(2,1)}, u32[]{:S(2)}, u32[]{:S(2)}) collective-permute-start(bf16[3,256,256]{2,1,0:T(8,128)(2,1)} %bitcast.164), channel_id=1, source_target_pairs={{0,3},{1,0},{2,1},{3,2},{4,7},{5,4},{6,5},{7,6},{8,11},{9,8},{10,9... | collective-permute-start | bytes 1179656 | tf_op jit(solution)/shard_map/ppermute | solution.py:336
  178.2 2.1 fusion.14
  183.0 19.8 %qkv.1 = (bf16[3,1024,256]{2,1,0:T(8,128)(2,1)S(1)}, bf16[3,1024,256]{2,1,0:T(8,128)(2,1)S(1)}, bf16[3,1024,256]{2,1,0:T(8,128)(2,1)}, bf16[4,3,256,1024]{3,2,1,0:T(8,128)(2,1)}, bf16[4,3,256,128]{3,2,1,0:T(8,128)(2,1)S(1)}) custom-call(s32[1]{0:T(128)} %bitcast.z_ref, bf16[4,3,256,1024]{3,2,1,0:T(8,128)(2,1)} %pad_maximum_fusion.1.x_ref, ...), custom_call_target="tpu_custom_call" | custom-call | flops 6442450944 | bytes 18874368 | tf_op jit(solution)/shard_map/qkv/pallas_call | solution.py:398
  203.0 7.2 %copy.218 = bf16[3,4,256,1024]{3,2,1,0:T(8,128)(2,1)} copy(bf16[3,4,256,1024]{3,2,0,1:T(8,128)(2,1)} %bitcast.196) | data formatting | bytes 12582912 | tf_op jit(solution)/shard_map/transpose | solution.py:525
  210.2 8.7 %copy.249 = bf16[1024,3072]{1,0:T(8,128)(2,1)} copy(bf16[1024,3072]{0,1:T(8,128)(2,1)} %bitcast.178) | data formatting | bytes 12582912 | tf_op jit(solution)/shard_map/dot_general | solution.py:35
  227.1 1.8 bitcast_dynamic-update-slice_fusion.5
  228.9 3.8 rev.3
  235.5 146.4 %middle.1 = (bf16[3,4,256,1024]{3,2,1,0:T(8,128)(2,1)}, bf16[3,3,1024,256]{3,2,1,0:T(8,128)(2,1)}, f32[768,1024]{1,0:T(8,128)}, f32[768,1024]{1,0:T(8,128)}, bf1...) custom-call(bf16[3,1024,256]{2,1,0:T(8,128)(2,1)} %copy-done.3, ...), custom_call_target="tpu_custom_call" | custom-call | tf_op jit(solution)/shard_map/middle/pallas_call | solution.py:470
  382.0 2.7 fusion.51
  390.3 23.2 %finish.1 = (bf16[3,256,1024]{2,1,0:T(8,128)(2,1)}, bf16[3,256,1024]{2,1,0:T(8,128)(2,1)}, f32[4,1024]{1,0:T(4,128)}, f32[128,1024]{1,0:T(8,128)}, f32[128,1024]{1,0:T(8,128)}) custom-call(bf16[3,4,256,1024]{3,2,1,0:T(8,128)(2,1)} %get-tuple-element.39.local_ref, ...), custom_call_target="tpu_custom_call" | custom-call | tf_op jit(solution)/shard_map/finish/pallas_call | solution.py:548
  416.3 2.0 copy-done.14
  418.3 6.8 %convolution_dynamic-update-slice_fusion.1 = f32[128,8,2048]{2,0,1:T(8,128)} fusion(bf16[8,128,3072]{2,1,0:T(8,128)(2,1)} %bitcast.177, f32[3072,128]{1,0:T(8,128)} %convolution_add_fusion.1, bf16[3072,256]{1,0:T(8,128)(2,1)S(1)} %bitcast.180, bf16[128,256]{1,0:T(8,128)(2,1)S(1)} %copy-done.39), kind=kOutput, calls=%fused_computation.34 | convolution fusion | flops 1007812608 | bytes 10027008 | tf_op jit(solution)/shard_map/dot_general | solution.py:35
  425.1 2.1 bitcast_dynamic-update-slice_fusion.3
  431.6 2.4 bitcast_dynamic-update-slice_fusion
  434.9 8.2 %pad_maximum_fusion = f32[8,130,2048]{2,1,0:T(8,128)} fusion(f32[8,2,2048]{2,1,0:T(2,128)S(1)} %broadcast_in_dim.93, f32[8,128,2048]{2,1,0:T(8,128)} %bitcast.188), kind=kLoop, calls=%fused_computation | loop fusion | flops 2129920 | bytes 17039360 | tf_op jit(solution)/shard_map/concatenate | solution.py:613
  443.2 77.7 %reduce-scatter.2.cloned.1.call-done = f32[1,130,2048]{2,1,0:T(8,128)} async-done(((f32[8,130,2048]{2,1,0:T(8,128)}), f32[1,130,2048]{2,1,0:T(8,128)}) %reduce-scatter.2.cloned.1.call-update) | async-done | bytes 1064976 | tf_op jit(solution)/shard_map/reduce_scatter | solution.py:614
  520.9 56.0 %all-reduce.2.cloned.1.call-done = f32[130,2048]{1,0:T(8,128)} async-done(((f32[130,2048]{1,0:T(8,128)}), f32[130,2048]{1,0:T(8,128)}) %all-reduce.2.cloned.1.call-update) | async-done | bytes 1064976 | tf_op jit(solution)/shard_map/psum | solution.py:615
  580.0 1.8 copy.236
  585.2 1.8 copy.228
  590.5 1.8 copy.232
  592.3 2.1 subtract_convert_fusion.2
  597.8 1.9 copy.241
  599.7 1.8 convert_multiply_fusion.2
  601.5 1.8 copy.242
  603.4 1.8 copy.243
  608.0 2.2 convert_multiply_fusion
  610.2 3.1 slice.180
  613.3 3.0 copy.255
  618.1 1.8 fusion.15
  620.1 4.6 fusion.1
  624.8 2.5 add_convert_fusion.1
  (259 shorter events, 79.2 us)
Async XLA Ops:
  7.2 131.0 %all-gather.5.cloned.1.call-start = ((), (), s32[]{:S(2)}) async-start(), calls=%async_computation.1 | async-start | bytes 12976128 | tf_op jit(solution)/shard_map/all_gather | solution.py:343
  11.4 224.1 %all-gather.7.cloned.1.call-start = ((), (), s32[]{:S(2)}) async-start(), calls=%async_computation.2 | async-start | bytes 9437184 | tf_op jit(solution)/shard_map/all_gather | solution.py:344
  12.1 9.0 %copy-start.57 = (s32[3,256]{1,0:T(4,128)S(1)}, s32[3,256]{1,0:T(4,128)}, u32[]{:S(2)}) copy-start(s32[3,256]{1,0:T(4,128)} %param.28) | copy-start | bytes 9220
  12.1 9.0 %copy-start.59 = (f32[22]{0:T(128)S(1)}, f32[22]{0:T(128)}, u32[]{:S(2)}) copy-start(f32[22]{0:T(128)} %param.29) | copy-start | bytes 268
  12.2 45.8 %copy-start.55 = (bf16[8192]{0:T(1024)(128)(2,1)S(1)}, bf16[8192]{0:T(1024)(128)(2,1)}, u32[]{:S(2)}) copy-start(bf16[8192]{0:T(1024)(128)(2,1)} %param.31) | copy-start | bytes 49156
  12.2 223.3 %all-gather.9.cloned.1.call-start = ((), (), s32[]{:S(2)}) async-start(), calls=%async_computation.3 | async-start | bytes 10616832 | tf_op jit(solution)/shard_map/all_gather | solution.py:346
  13.7 507.1 %reduce-scatter.2.cloned.1.call-start = ((), (), s32[]{:S(2)}) async-start(), calls=%async_computation.4 | async-start | bytes 10027008 | tf_op jit(solution)/shard_map/reduce_scatter | solution.py:614
  13.8 38.6 %collective-permute-start = (bf16[3,256,1024]{2,1,0:T(8,128)(2,1)S(1)}, bf16[3,256,1024]{2,1,0:T(8,128)(2,1)}, u32[]{:S(2)}, u32[]{:S(2)}) collective-permute-start(bf16[3,256,1024]{2,1,0:T(8,128)(2,1)S(1)} %copy-done.6), channel_id=1, source_target_pairs={{0,1},{1,2},{2,3},{4,5},{5,6},{6,7},{8,9},{9,10},{10,11},{12,13},{... | collective-permute-start | bytes 4718600 | tf_op jit(solution)/shard_map/ppermute | solution.py:360
  19.8 39.0 %collective-permute-start.1 = (bf16[3,256,1024]{2,1,0:T(8,128)(2,1)S(1)}, bf16[3,256,1024]{2,1,0:T(8,128)(2,1)}, u32[]{:S(2)}, u32[]{:S(2)}) collective-permute-start(bf16[3,256,1024]{2,1,0:T(8,128)(2,1)S(1)} %copy-done.6), channel_id=1, source_target_pairs={{1,0},{2,1},{3,2},{5,4},{6,5},{7,6},{9,8},{10,9},{11,10},{13,12},{... | collective-permute-start | bytes 4718600 | tf_op jit(solution)/shard_map/ppermute | solution.py:361
  52.3 37.6 %collective-permute-start.4 = (bf16[3,256,1024]{2,1,0:T(8,128)(2,1)}, bf16[3,256,1024]{2,1,0:T(8,128)(2,1)}, u32[]{:S(2)}, u32[]{:S(2)}) collective-permute-start(bf16[3,256,1024]{2,1,0:T(8,128)(2,1)} %collective-permute-done), channel_id=1, source_target_pairs={{0,1},{1,2},{2,3},{4,5},{5,6},{6,7},{8,9},{9,10},{10,11},{12,13},{... | collective-permute-start | bytes 4718600 | tf_op jit(solution)/shard_map/ppermute | solution.py:360
  58.9 38.3 %collective-permute-start.2 = (bf16[3,256,1024]{2,1,0:T(8,128)(2,1)}, bf16[3,256,1024]{2,1,0:T(8,128)(2,1)}, u32[]{:S(2)}, u32[]{:S(2)}) collective-permute-start(bf16[3,256,1024]{2,1,0:T(8,128)(2,1)} %collective-permute-done.1), channel_id=1, source_target_pairs={{1,0},{2,1},{3,2},{5,4},{6,5},{7,6},{9,8},{10,9},{11,10},{13,12},{... | collective-permute-start | bytes 4718600 | tf_op jit(solution)/shard_map/ppermute | solution.py:361
  61.4 121.6 %copy-start = (f32[1024,128]{1,0:T(8,128)}, f32[1024,128]{1,0:T(8,128)S(1)}, u32[]{:S(2)}) copy-start(f32[1024,128]{1,0:T(8,128)S(1)} %copy.199.keep_ref) | copy-start | bytes 1572868
  62.8 120.2 %copy-start.1 = (f32[1024,128]{1,0:T(8,128)}, f32[1024,128]{1,0:T(8,128)S(1)}, u32[]{:S(2)}) copy-start(f32[1024,128]{1,0:T(8,128)S(1)} %copy.200.above_ref) | copy-start | bytes 1572868
  63.8 32.7 %copy-start.58 = (bf16[1024]{0:T(1024)(128)(2,1)S(1)}, bf16[1024]{0:T(1024)(128)(2,1)}, u32[]{:S(2)}) copy-start(bf16[1024]{0:T(1024)(128)(2,1)} %param.33) | copy-start | bytes 6148
  65.0 118.0 %copy-start.2 = (f32[1024,128]{1,0:T(8,128)}, f32[1024,128]{1,0:T(8,128)S(1)}, u32[]{:S(2)}) copy-start(f32[1024,128]{1,0:T(8,128)S(1)} %copy.201.below_ref) | copy-start | bytes 1572868
  65.0 32.1 %copy-start.54 = (f32[2,1024]{1,0:T(2,128)S(1)}, f32[2,1024]{1,0:T(2,128)}, u32[]{:S(2)}) copy-start(f32[2,1024]{1,0:T(2,128)} %gain_ref.1) | copy-start | bytes 24580
  65.1 32.1 %copy-start.56 = (f32[2,1024]{1,0:T(2,128)S(1)}, f32[2,1024]{1,0:T(2,128)}, u32[]{:S(2)}) copy-start(f32[2,1024]{1,0:T(2,128)} %param.35) | copy-start | bytes 24580
  89.9 36.5 %collective-permute-start.5 = (bf16[3,256,1024]{2,1,0:T(8,128)(2,1)}, bf16[3,256,1024]{2,1,0:T(8,128)(2,1)}, u32[]{:S(2)}, u32[]{:S(2)}) collective-permute-start(bf16[3,256,1024]{2,1,0:T(8,128)(2,1)} %collective-permute-done.4), channel_id=1, source_target_pairs={{0,1},{1,2},{2,3},{4,5},{5,6},{6,7},{8,9},{9,10},{10,11},{12,13},{... | collective-permute-start | bytes 4718600 | tf_op jit(solution)/shard_map/ppermute | solution.py:360
  97.2 36.3 %collective-permute-start.3 = (bf16[3,256,1024]{2,1,0:T(8,128)(2,1)}, bf16[3,256,1024]{2,1,0:T(8,128)(2,1)}, u32[]{:S(2)}, u32[]{:S(2)}) collective-permute-start(bf16[3,256,1024]{2,1,0:T(8,128)(2,1)} %collective-permute-done.2), channel_id=1, source_target_pairs={{1,0},{2,1},{3,2},{5,4},{6,5},{7,6},{9,8},{10,9},{11,10},{13,12},{... | collective-permute-start | bytes 4718600 | tf_op jit(solution)/shard_map/ppermute | solution.py:361
  142.0 5.9 copy-start.5
  157.6 18.2 %copy-start.7 = (bf16[768,1024]{1,0:T(8,128)(2,1)S(1)}, bf16[768,1024]{1,0:T(8,128)(2,1)}, u32[]{:S(2)}) copy-start(bf16[768,1024]{1,0:T(8,128)(2,1)} %fusion.8.second_ref) | copy-start | bytes 4718596
  158.4 63.0 %collective-permute-start.6 = (bf16[3,256,256]{2,1,0:T(8,128)(2,1)}, bf16[3,256,256]{2,1,0:T(8,128)(2,1)S(1)}, u32[]{:S(2)}, u32[]{:S(2)}) collective-permute-start(bf16[3,256,256]{2,1,0:T(8,128)(2,1)} %bitcast.166), channel_id=1, source_target_pairs={{0,1},{1,2},{2,3},{3,0},{4,5},{5,6},{6,7},{7,4},{8,9},{9,10},{10,1... | collective-permute-start | bytes 1179656 | tf_op jit(solution)/shard_map/ppermute | solution.py:336
  159.9 62.3 %collective-permute-start.7 = (bf16[3,256,256]{2,1,0:T(8,128)(2,1)}, bf16[3,256,256]{2,1,0:T(8,128)(2,1)S(1)}, u32[]{:S(2)}, u32[]{:S(2)}) collective-permute-start(bf16[3,256,256]{2,1,0:T(8,128)(2,1)} %bitcast.165), channel_id=1, source_target_pairs={{0,2},{1,3},{2,0},{3,1},{4,6},{5,7},{6,4},{7,5},{8,10},{9,11},{10,... | collective-permute-start | bytes 1179656 | tf_op jit(solution)/shard_map/ppermute | solution.py:336
  161.7 61.3 %collective-permute-start.8 = (bf16[3,256,256]{2,1,0:T(8,128)(2,1)}, bf16[3,256,256]{2,1,0:T(8,128)(2,1)}, u32[]{:S(2)}, u32[]{:S(2)}) collective-permute-start(bf16[3,256,256]{2,1,0:T(8,128)(2,1)} %bitcast.164), channel_id=1, source_target_pairs={{0,3},{1,0},{2,1},{3,2},{4,7},{5,4},{6,5},{7,6},{8,11},{9,8},{10,9... | collective-permute-start | bytes 1179656 | tf_op jit(solution)/shard_map/ppermute | solution.py:336
  177.4 4.9 copy-start.24
  180.3 22.6 %copy-start.33 = (bf16[768,128]{0,1:T(8,128)(2,1)}, bf16[768,128]{0,1:T(8,128)(2,1)S(1)}, u32[]{:S(2)}) copy-start(bf16[768,128]{0,1:T(8,128)(2,1)S(1)} %fusion.14) | copy-start | bytes 589828
  202.9 7.3 %copy-start.3 = (bf16[3,1024,256]{2,1,0:T(8,128)(2,1)}, bf16[3,1024,256]{2,1,0:T(8,128)(2,1)S(1)}, u32[]{:S(2)}) copy-start(bf16[3,1024,256]{2,1,0:T(8,128)(2,1)S(1)} %get-tuple-element.36.q_ref) | copy-start | bytes 4718596
  202.9 7.3 %copy-start.4 = (bf16[3,1024,256]{2,1,0:T(8,128)(2,1)}, bf16[3,1024,256]{2,1,0:T(8,128)(2,1)S(1)}, u32[]{:S(2)}) copy-start(bf16[3,1024,256]{2,1,0:T(8,128)(2,1)S(1)} %get-tuple-element.37.k_ref) | copy-start | bytes 4718596
  210.2 8.7 %copy-start.12 = (bf16[3,256,1,256]{3,2,1,0:T(2,128)(2,1)S(1)}, bf16[3,256,1,256]{3,2,1,0:T(2,128)(2,1)}, u32[]{:S(2)}) copy-start(bf16[3,256,1,256]{3,2,1,0:T(2,128)(2,1)} %get-tuple-element.161) | copy-start | bytes 1179652
  418.3 8.9 %copy-start.13 = (bf16[1024,768]{1,0:T(8,128)(2,1)S(1)}, bf16[1024,768]{1,0:T(8,128)(2,1)}, u32[]{:S(2)}) copy-start(bf16[1024,768]{1,0:T(8,128)(2,1)} %copy.250) | copy-start | bytes 4718596
  418.3 8.9 %copy-start.36 = (bf16[768,128]{1,0:T(8,128)(2,1)S(1)}, bf16[768,128]{1,0:T(8,128)(2,1)}, u32[]{:S(2)}) copy-start(bf16[768,128]{1,0:T(8,128)(2,1)} %get-tuple-element.43.dmid_up_ref) | copy-start | bytes 589828
  443.1 133.9 %copy-start.19 = (f32[128,1024]{1,0:T(8,128)S(1)}, f32[128,1024]{1,0:T(8,128)}, u32[]{:S(2)}) copy-start(f32[128,1024]{1,0:T(8,128)} %param.38) | copy-start | bytes 1572868
  443.1 133.9 %copy-start.21 = (f32[128,1024]{1,0:T(8,128)S(1)}, f32[128,1024]{1,0:T(8,128)}, u32[]{:S(2)}) copy-start(f32[128,1024]{1,0:T(8,128)} %param.42) | copy-start | bytes 1572868
  443.1 133.9 %copy-start.22 = (f32[128,1024]{1,0:T(8,128)S(1)}, f32[128,1024]{1,0:T(8,128)}, u32[]{:S(2)}) copy-start(f32[128,1024]{1,0:T(8,128)} %param.46) | copy-start | bytes 1572868
  443.1 135.4 %copy-start.46 = (f32[128,128]{1,0:T(8,128)S(1)}, f32[128,128]{1,0:T(8,128)}, u32[]{:S(2)}) copy-start(f32[128,128]{1,0:T(8,128)} %param.39) | copy-start | bytes 196612
  443.1 135.4 %copy-start.48 = (f32[128,128]{1,0:T(8,128)S(1)}, f32[128,128]{1,0:T(8,128)}, u32[]{:S(2)}) copy-start(f32[128,128]{1,0:T(8,128)} %param.43) | copy-start | bytes 196612
  443.1 135.3 %copy-start.50 = (f32[128,128]{1,0:T(8,128)S(1)}, f32[128,128]{1,0:T(8,128)}, u32[]{:S(2)}) copy-start(f32[128,128]{1,0:T(8,128)} %param.47) | copy-start | bytes 196612
  443.1 133.8 %all-reduce.2.cloned.1.call-start = ((), (), s32[]{:S(2)}) async-start(), calls=%async_computation.5 | async-start | bytes 2228224 | tf_op jit(solution)/shard_map/psum | solution.py:615
  520.8 89.3 %all-gather.11.cloned.1.call-start = ((), (), s32[]{:S(2)}) async-start(), calls=%async_computation.6 | async-start | bytes 2654208 | tf_op jit(solution)/shard_map/all_gather | solution.py:633
  578.5 29.5 %copy-start.23 = (f32[128,1024]{1,0:T(8,128)}, f32[128,1024]{1,0:T(8,128)S(1)}, u32[]{:S(2)}) copy-start(f32[128,1024]{1,0:T(8,128)S(1)} %get-tuple-element.147) | copy-start | bytes 1572868
  584.0 15.7 %copy-start.29 = (f32[512,128]{0,1:T(8,128)}, f32[512,128]{0,1:T(8,128)S(1)}, u32[]{:S(2)}) copy-start(f32[512,128]{0,1:T(8,128)S(1)} %copy.231) | copy-start | bytes 786436
  585.2 14.5 %copy-start.31 = (f32[512,128]{0,1:T(8,128)}, f32[512,128]{0,1:T(8,128)S(1)}, u32[]{:S(2)}) copy-start(f32[512,128]{0,1:T(8,128)S(1)} %copy.233) | copy-start | bytes 786436
  597.8 9.4 %copy-start.49 = (f32[128,128]{1,0:T(8,128)S(1)}, f32[128,128]{1,0:T(8,128)}, u32[]{:S(2)}) copy-start(f32[128,128]{1,0:T(8,128)} %param.43) | copy-start | bytes 196612
  597.8 9.4 %copy-start.51 = (f32[128,128]{1,0:T(8,128)S(1)}, f32[128,128]{1,0:T(8,128)}, u32[]{:S(2)}) copy-start(f32[128,128]{1,0:T(8,128)} %param.47) | copy-start | bytes 196612
  597.8 9.4 %copy-start.52 = (f32[128,128]{1,0:T(8,128)S(1)}, f32[128,128]{1,0:T(8,128)}, u32[]{:S(2)}) copy-start(f32[128,128]{1,0:T(8,128)} %get-tuple-element.149) | copy-start | bytes 196612
  601.5 5.7 copy-start.53
  620.1 4.7 copy-start.27
  620.1 4.7 copy-start.30
  (28 other events, 61.1 us)
Sparse Core Ops, SparseCore 0:
  11.5 70.3 all-gather.4
  84.4 54.3 all-gather.6
  140.7 58.8 all-gather.8
  443.2 77.5 reduce-scatter.1
  523.0 53.8 all-reduce.1
  580.1 28.4 all-gather.10

commit v2 on v1

--- a/solution.py
+++ b/solution.py
@@ -282,12 +282,225 @@
         norm_ref[...] = jnp.concatenate(norm, axis=0)
 
 
-def adam_update(param, grad, mean, square, keep):
+def reduce_kernel(
+    g_ref, norm_in_ref, b_ref, mean_ref, square_ref, bf_ref, mean_f_ref, square_f_ref,
+    out_ref, norm_ref, fresh_ref,
+    r1, h, r2a, r2b, ia, ib, r3a, r3b, total, r4, nr, nsum,
+    s1, q1, s2, q2, s3, q3, s4, q4, s5, q5, sn, qn, sg, qg,
+    *, n, chunks, b_at,
+):
+    z = lax.axis_index("blk")
+    dp = lax.axis_index("dp")
+    y, x, c = dp // 4, lax.rem(dp // 2, 2), lax.rem(dp, 2)
+    core = (dp + 1 - 2 * c, z)
+    along_x = (dp + 2 - 4 * x, z)
+    along_y = (dp + 4 - 8 * y, z)
+    peers = [(dp, lax.rem(z + t, n)) for t in range(1, n)]
+    half = g_ref.shape[2] // 2
+    part = g_ref.shape[2] // n
+    width = g_ref.shape[3] // chunks
+
+    barrier = pltpu.get_barrier_semaphore()
+    for peer in [core, along_x, along_y] + peers:
+        pl.semaphore_signal(barrier, inc=1, device_id=peer, device_id_type=MESH)
+    pl.semaphore_wait(barrier, 2 + n)
+
+    def remote(src, dst, send, recv, peer):
+        return pltpu.make_async_remote_copy(
+            src_ref=src, dst_ref=dst, send_sem=send, recv_sem=recv, device_id=peer, device_id_type=MESH
+        )
+
+    def cols(k):
+        return slice(k * width, (k + 1) * width)
+
+    def mine(k=None):
+        return pl.ds(pl.multiple_of(z * part, part), part)
+
+    def first(k):
+        return [remote(g_ref.at[:, 1 - c, :, cols(k)], r1.at[:, :, cols(k)], s1.at[k], q1.at[k], core)]
+
+    def second(k):
+        return [
+            remote(h.at[:, 1 - x, 0:half, cols(k)], r2a.at[:, :, cols(k)], s2.at[0, k], q2.at[0, k], along_x),
+            remote(h.at[1 - y, :, half:, cols(k)], r2b.at[:, :, cols(k)], s2.at[1, k], q2.at[1, k], along_y),
+        ]
+
+    def third(k):
+        return [
+            remote(ia.at[1 - y, :, cols(k)], r3a.at[:, cols(k)], s3.at[0, k], q3.at[0, k], along_y),
+            remote(ib.at[1 - x, :, cols(k)], r3b.at[:, cols(k)], s3.at[1, k], q3.at[1, k], along_x),
+        ]
+
+    def fourth(k):
+        found = []
+        for t in range(1, n):
+            to = lax.rem(z + t, n)
+            rows = pl.ds(pl.multiple_of(to * part, part), part)
+            found.append(
+                remote(total.at[rows, cols(k)], r4.at[t, :, cols(k)], s4.at[t, k], q4.at[t, k], peers[t - 1])
+            )
+        return found
+
+    def fifth(k):
+        return [
+            remote(out_ref.at[mine(), cols(k)], out_ref.at[mine(), cols(k)], s5.at[t, k], q5.at[t, k], peers[t - 1])
+            for t in range(1, n)
+        ]
+
+    def add(a, b):
+        return (a.astype(f32) + b.astype(f32)).astype(bf16)
+
+    def norm_copy(i, peer):
+        return remote(nsum.at[i], nr.at[i], sn.at[i], qn.at[i], peer)
+
+    nsum[0] = norm_in_ref[...]
+    norm_stages = [norm_copy(0, core), norm_copy(1, along_x), norm_copy(2, along_y)]
+    norm_last = [
+        remote(nsum.at[3], nr.at[2 + t], sn.at[2 + t], qn.at[2 + t], peers[t - 1]) for t in range(1, n)
+    ]
+    for k in range(chunks):
+        first(k)[0].start()
+    norm_stages[0].start()
+
+    def after_first(k):
+        for copy in first(k):
+            copy.wait()
+        for yy in range(2):
+            for xx in range(2):
+                h[yy, xx, :, cols(k)] = add(g_ref[2 * yy + xx, c, :, cols(k)], r1[2 * yy + xx, :, cols(k)])
+        for copy in second(k):
+            copy.start()
+
+    def after_second(k):
+        for copy in second(k):
+            copy.wait()
+        for i in range(2):
+            ia[i, :, cols(k)] = add(h[i, x, 0:half, cols(k)], r2a[i, :, cols(k)])
+            ib[i, :, cols(k)] = add(h[y, i, half:, cols(k)], r2b[i, :, cols(k)])
+        for copy in third(k):
+            copy.start()
+
+    def after_third(k):
+        for copy in third(k):
+            copy.wait()
+        total[0:half, cols(k)] = add(ia[y, :, cols(k)], r3a[:, cols(k)])
+        total[half:, cols(k)] = add(ib[x, :, cols(k)], r3b[:, cols(k)])
+        for copy in fourth(k):
+            copy.start()
+
+    def after_fourth(k):
+        for copy in fourth(k):
+            copy.wait()
+        value = total[mine(), cols(k)].astype(f32)
+        for t in range(1, n):
+            value += r4[t, :, cols(k)].astype(f32)
+        out_ref[mine(), cols(k)] = value.astype(bf16)
+        for copy in fifth(k):
+            copy.start()
+
+    def after_fifth(k):
+        for copy in fifth(k):
+            copy.wait()
+
+    stages = [after_first, after_second, after_third, after_fourth, after_fifth]
+    for step in range(chunks + len(stages) - 1):
+        for at in reversed(range(len(stages))):
+            if 0 <= step - at < chunks:
+                stages[at](step - at)
+        if step < 3:
+            norm_stages[step].wait()
+            nsum[step + 1] = nsum[step] + nr[step]
+            if step < 2:
+                norm_stages[step + 1].start()
+            else:
+                for copy in norm_last:
+                    copy.start()
+    for copy in norm_last:
+        copy.wait()
+    value = jnp.zeros_like(nsum[3])
+    for blk in range(n):
+        there = lax.rem(z - blk + n, n)
+        value += jnp.where(there == 0, nsum[3], nr[2 + jnp.maximum(there, 1)])
+    norm_ref[...] = value
+
+    cut = b_ref.shape[1]
+    grads = out_ref[:, b_at:].astype(f32)
+    new_b = adam_fresh(b_ref[...], grads[:, :cut], mean_ref[...], square_ref[...])
+    new_f = adam_fresh(bf_ref[...], grads[:, cut:], mean_f_ref[...], square_f_ref[...])
+    fresh_ref[dp] = jnp.concatenate([new_b, new_f], axis=1).astype(bf16)
+
+    def gather(i, slot, peer):
+        return remote(fresh_ref.at[slot], fresh_ref.at[slot], sg.at[i], qg.at[i], peer)
+
+    from_x, from_y = dp + 2 - 4 * x, dp + 4 - 8 * y
+    across = dp + 2 - 4 * x + 4 - 8 * y
+    onward = jnp.where(c == 0, from_y, from_x)
+    target = (jnp.where(c == 0, along_x[0], along_y[0]), z)
+    direct = [gather(0, dp, along_x), gather(1, dp, along_y), gather(2, dp, core)]
+    for copy in direct:
+        copy.start()
+    direct[0].wait()
+    direct[1].wait()
+    more = [gather(3, onward, target), gather(4, from_x, core), gather(5, from_y, core)]
+    for copy in more:
+        copy.start()
+    more[0].wait()
+    last = gather(6, across, core)
+    last.start()
+    direct[2].wait()
+    more[1].wait()
+    more[2].wait()
+    last.wait()
+
+
+def update_kernel(
+    g_ref, fresh_ref, w_ref, wd_ref, *refs, rank, width,
+):
+    params, outs = refs[:16], refs[16:30]
+    a_new, aff_new = refs[30:]
+    j = pl.program_id(0)
+    cols = w_ref.shape[1]
+
+    @pl.when(j == 0)
+    def _():
+        rows, inner = params[0].shape[0], params[4].shape[0]
+        got = g_ref[...].astype(f32)
+        grads = [
+            jnp.concatenate([got[:, i * rows : (i + 1) * rows].T for i in range(3)], axis=1),
+            got[:, 3 * rows : 3 * rows + inner].T,
+        ]
+        at = 3 * rows + inner
+        cut = params[8].shape[1]
+        grads += [got[:, at : at + cut], got[:, at + cut :]]
+        for i, grad in enumerate(grads):
+            param, mean, square, keep = (r[...] for r in params[4 * i : 4 * i + 4])
+            mean_new = 0.9 * mean + 0.1 * grad
+            square_new = 0.999 * square + 0.001 * grad * grad
+            kept = keep.astype(f32)
+            outs[i][...] = grad
+            outs[4 + 2 * i][...] = mean_new * kept
+            outs[5 + 2 * i][...] = square_new * kept
+            if i < 2:
+                fresh = param - 0.01 * (mean_new / first_fix) / (jnp.sqrt(square_new / second_fix) + 1e-08)
+                if i == 0:
+                    for k in range(3):
+                        a_new[k] = fresh[:, k * rank : (k + 1) * rank].astype(bf16)
+                else:
+                    aff_new[...] = fresh.astype(bf16)
+
+    block = jnp.where(j * cols < 3 * width, 0, jnp.where(j * cols < 4 * width, 1, 2))
+    cut = params[8].shape[1]
+    fresh = [fresh_ref[i] for i in range(fresh_ref.shape[0])]
+    update = nn(a_new[block], jnp.concatenate([f[:, :cut] for f in fresh], axis=1))
+    outs[12][...] = (w_ref[...].astype(f32) + adapter_scale * update).astype(bf16)
+    update = nn(aff_new[...], jnp.concatenate([f[:, cut:] for f in fresh], axis=1))
+    outs[13][...] = (wd_ref[...].astype(f32) + adapter_scale * update).astype(bf16)
+
+
+def adam_fresh(param, grad, mean, square):
     mean_new = 0.9 * mean + 0.1 * grad
     square_new = 0.999 * square + 0.001 * grad * grad
-    fresh = param - 0.01 * (mean_new / first_fix) / (jnp.sqrt(square_new / second_fix) + 1e-08)
-    kept = keep.astype(f32)
-    return (fresh, mean_new * kept, square_new * kept)
+    return param - 0.01 * (mean_new / first_fix) / (jnp.sqrt(square_new / second_fix) + 1e-08)
 
 
 def body(
@@ -608,44 +821,104 @@
         by_owner(jnp.concatenate([grad_b_qkv, grad_b_out, grad_b_up], axis=1)), by_owner(grad_b_ffp),
     ]
     widths = [p.shape[2] for p in parts]
-    owned = jnp.transpose(jnp.concatenate(parts, axis=2), (1, 0, 2))
-    norm_rows = jnp.broadcast_to(norm_part.reshape(1, -1, owned.shape[2]), (dp_n, 4 * width // owned.shape[2], owned.shape[2]))
-    owned = jnp.concatenate([owned, norm_rows], axis=1)
-    owned = lax.psum_scatter(owned, "dp", scatter_dimension=0, tiled=True)
-    owned = lax.psum(owned[0], "blk")
-    norm_sum = owned[rank:].reshape(4, width)
+    owned = jnp.transpose(jnp.concatenate([p.astype(bf16) for p in parts], axis=2), (1, 0, 2))
+    total_cols = owned.shape[2]
+    b_at = sum(widths[:4])
+    if dp_n == 8 and rank % (16 * n) == 0:
+        chunks = 4
+        half = rank // 2
+        vmem = pl.BlockSpec(memory_space=pltpu.VMEM)
+        dma = pltpu.SemaphoreType.DMA
+        reduced, norm_sum, fresh = pl.pallas_call(
+            functools.partial(reduce_kernel, n=n, chunks=chunks, b_at=b_at),
+            in_specs=[vmem] * 8,
+            out_specs=[vmem] * 3,
+            out_shape=[
+                jax.ShapeDtypeStruct((rank, total_cols), bf16),
+                jax.ShapeDtypeStruct((4, width), f32),
+                jax.ShapeDtypeStruct((dp_n, rank, b_cols), bf16),
+            ],
+            scratch_shapes=[
+                pltpu.VMEM((4, rank, total_cols), bf16),
+                pltpu.VMEM((2, 2, rank, total_cols), bf16),
+                pltpu.VMEM((2, half, total_cols), bf16),
+                pltpu.VMEM((2, half, total_cols), bf16),
+                pltpu.VMEM((2, half, total_cols), bf16),
+                pltpu.VMEM((2, half, total_cols), bf16),
+                pltpu.VMEM((half, total_cols), bf16),
+                pltpu.VMEM((half, total_cols), bf16),
+                pltpu.VMEM((rank, total_cols), bf16),
+                pltpu.VMEM((n, rank // n, total_cols), bf16),
+                pltpu.VMEM((2 + n, 4, width), f32),
+                pltpu.VMEM((4, 4, width), f32),
+                dma((chunks,)), dma((chunks,)),
+                dma((2, chunks)), dma((2, chunks)),
+                dma((2, chunks)), dma((2, chunks)),
+                dma((n, chunks)), dma((n, chunks)),
+                dma((n, chunks)), dma((n, chunks)),
+                dma((2 + n,)), dma((2 + n,)),
+                dma((7,)), dma((7,)),
+            ],
+            compiler_params=pltpu.CompilerParams(
+                collective_id=1, has_side_effects=True, vmem_limit_bytes=48 << 20
+            ),
+            name="reduce",
+        )(
+            owned.reshape(4, 2, rank, total_cols), norm_part,
+            adapt_b, mean_b, square_b, adapt_b_ff, mean_b_ff, square_b_ff,
+        )
+    else:
+        reduced = lax.psum_scatter(owned.astype(f32), "dp", scatter_dimension=0, tiled=True)
+        reduced = lax.psum(reduced[0], "blk").astype(bf16)
+        norm_sum = lax.psum(norm_part, ("dp", "blk"))
+        grads_b = reduced[:, b_at:].astype(f32)
+        cut = adapt_b.shape[1]
+        fresh = jnp.concatenate(
+            [
+                adam_fresh(adapt_b, grads_b[:, :cut], mean_b, square_b),
+                adam_fresh(adapt_b_ff, grads_b[:, cut:], mean_b_ff, square_b_ff),
+            ],
+            axis=1,
+        ).astype(bf16)
+        fresh = lax.all_gather(fresh, "dp", axis=0, tiled=False)
     grad_gain, grad_shift = norm_sum[:2], norm_sum[2:]
-    cuts = [sum(widths[:i]) for i in range(len(widths) + 1)]
-    pieces = [owned[:rank, cuts[i] : cuts[i + 1]] for i in range(len(widths))]
-    grad_a = jnp.concatenate([p.T for p in pieces[:3]], axis=1)
-    grad_a_ff = pieces[3].T
-    grad_b, grad_b_ff = pieces[4], pieces[5]
-
-    fresh_a, new_mean_a, new_square_a = adam_update(adapt_a, grad_a, mean_a, square_a, keep_a)
-    fresh_a_ff, new_mean_a_ff, new_square_a_ff = adam_update(
-        adapt_a_ff, grad_a_ff, mean_a_ff, square_a_ff, keep_a_ff
-    )
-    fresh_b, new_mean_b, new_square_b = adam_update(adapt_b, grad_b, mean_b, square_b, keep_b)
-    fresh_b_ff, new_mean_b_ff, new_square_b_ff = adam_update(
-        adapt_b_ff, grad_b_ff, mean_b_ff, square_b_ff, keep_b_ff
-    )
-    fresh = jnp.concatenate([fresh_b, fresh_b_ff], axis=1).astype(bf16)
-    fresh = lax.all_gather(fresh, "dp", axis=0, tiled=False)
-    fresh_in = jnp.transpose(fresh[:, :, : adapt_b.shape[1]], (1, 0, 2)).reshape(rank, -1)
-    fresh_ff = jnp.transpose(fresh[:, :, adapt_b.shape[1] :], (1, 0, 2)).reshape(rank, width)
-    fa = fresh_a.astype(bf16)
-    update = jnp.concatenate(
-        [
-            nn(fa[:, :rank], fresh_in[:, : 3 * width]),
-            nn(fa[:, rank : 2 * rank], fresh_in[:, 3 * width : 4 * width]),
-            nn(fa[:, 2 * rank :], fresh_in[:, 4 * width :]),
-        ],
-        axis=1,
-    )
-    folded_input_weights = (frozen_input_weights.astype(f32) + adapter_scale * update).astype(bf16)
-    folded_down_weight = (
-        frozen_down_weight.astype(f32) + adapter_scale * nn(fresh_a_ff.astype(bf16), fresh_ff)
-    ).astype(bf16)
+
+    state = [
+        adapt_a, mean_a, square_a, keep_a,
+        adapt_a_ff, mean_a_ff, square_a_ff, keep_a_ff,
+        adapt_b, mean_b, square_b, keep_b,
+        adapt_b_ff, mean_b_ff, square_b_ff, keep_b_ff,
+    ]
+
+    def all_of(value):
+        zeros = (0,) * value.ndim
+        return pl.BlockSpec(value.shape, lambda j: zeros, pipeline_mode=pl.Buffered(1))
+
+    four = [adapt_a, adapt_a_ff, adapt_b, adapt_b_ff]
+    results = [v for v in four] + [v for v in four for _ in range(2)]
+    b_w, f_w = adapt_b.shape[1], adapt_b_ff.shape[1]
+    owners = max(1, lanes // f_w)
+    w_spec = pl.BlockSpec((kr, owners * b_w), lambda j: (0, j))
+    wd_spec = pl.BlockSpec((down_rows, owners * f_w), lambda j: (0, j))
+    updated = pl.pallas_call(
+        functools.partial(update_kernel, rank=rank, width=width),
+        grid=(dp_n // owners,),
+        in_specs=[all_of(reduced), pl.BlockSpec((owners, rank, b_cols), lambda j: (j, 0, 0)), w_spec, wd_spec]
+        + [all_of(v) for v in state],
+        out_specs=[all_of(v) for v in results] + [w_spec, wd_spec],
+        out_shape=[jax.ShapeDtypeStruct(v.shape, f32) for v in results]
+        + [
+            jax.ShapeDtypeStruct(frozen_input_weights.shape, bf16),
+            jax.ShapeDtypeStruct(frozen_down_weight.shape, bf16),
+        ],
+        scratch_shapes=[pltpu.VMEM((3, kr, rank), bf16), pltpu.VMEM((down_rows, rank), bf16)],
+        compiler_params=pltpu.CompilerParams(vmem_limit_bytes=48 << 20),
+        name="update",
+    )(reduced, fresh, frozen_input_weights, frozen_down_weight, *state)
+    grad_a, grad_a_ff, grad_b, grad_b_ff = updated[:4]
+    new_mean_a, new_square_a, new_mean_a_ff, new_square_a_ff = updated[4:8]
+    new_mean_b, new_square_b, new_mean_b_ff, new_square_b_ff = updated[8:12]
+    folded_input_weights, folded_down_weight = updated[12:]
     return (
         mixed,
         grad_tokens,

time: 639 us -> 521 us (0.82)
  waiting for transfers between devices: 212 us -> 76.9 us
  Pallas kernels: 190 us -> 262 us
  local copies, waits for them, and re-layouts: 108 us -> 76.7 us
  other arithmetic: 42.7 us -> 33.2 us
  starting transfers between devices: 37 us -> 28.9 us
    reduce_scatter x1 -> x0, waiting for transfers between devices: 77.7 us -> none  [body(): owned = lax.psum_scatter(owned, 'dp', scatter_dimension=0, tiled=True)]
    pallas_call x0 -> x2, Pallas kernels: none -> 73 us  [the longest x1 64.1 us: body(): pl.pallas_call(functools.partial(reduce_kernel, n=n, chunks=chunks, b_at=...]
    ppermute x3, waiting for transfers between devices: 71.8 us -> 4.02 us  [body(): right = lax.ppermute(right, 'blk', [(i, i + 1) for i in range(n - 1)])]
    ppermute x3, waiting for transfers between devices: 5.42 us -> 72.1 us  [body(): left = lax.ppermute(left, 'blk', [(i + 1, i) for i in range(n - 1)])]
    psum x1 -> x0, waiting for transfers between devices: 56 us -> none  [body(): owned = lax.psum(owned[0], 'blk')]
    unnamed x155 -> x120, local copies, waits for them, and re-layouts: 51.2 us -> 25.3 us
    concatenate x4 -> x0, other arithmetic: 11.2 us -> none  [the longest x1 8.16 us: body(): owned = jnp.concatenate([owned, norm_rows], axis=1)]
    ppermute x3, starting transfers between devices: 15.7 us -> 6.62 us  [shift_by(): return lax.ppermute(values, 'blk', [(i, (i + s) % n) for i in range(n)])]
  transfers between devices with their start and end apart: 15 -> 12, of which waited for: 6 -> 4; matrix products, arithmetic and copies ran while one was open for 18% -> 18% of each run, Pallas kernels for 3% -> 4%
where the time goes in v2:
time: 521 us; the launch traced here: 516 us
  Pallas kernels  262 us (50%)
  waiting for transfers between devices  76.9 us (15%)
  local copies, waits for them, and re-layouts  76.7 us (15%)
  other arithmetic  33.2 us (6%)
  starting transfers between devices  28.9 us (6%)
  matrix products  23.6 us (5%)
  between operations  15 us (3%)
    pallas_call x1, Pallas kernels, body(): pl.pallas_call(functools.partial(middle_kernel, n=n, pairs=pairs, steps=s...  146 us
    ppermute x3, waiting for transfers between devices, body(): left = lax.ppermute(left, 'blk', [(i + 1, i) for i in range(n - 1)])  72.1 us
    pallas_call x1, Pallas kernels, body(): pl.pallas_call(functools.partial(reduce_kernel, n=n, chunks=chunks, b_at=...  64.1 us
    unnamed x120, local copies, waits for them, and re-layouts  25.3 us
    pallas_call x1, Pallas kernels, body(): pl.pallas_call(finish_kernel, grid=(n,), in_specs=[pl.BlockSpec((seqs, 4,...  23.2 us
    pallas_call x1, Pallas kernels, body(): pl.pallas_call(qkv_kernel, grid_spec=pltpu.PrefetchScalarGridSpec(num_sca...  19.8 us
    ppermute x3, starting transfers between devices, body(): right = lax.ppermute(right, 'blk', [(i, i + 1) for i in range(n - 1)])  18.3 us
    dot_general x6, matrix products, tn(): lax.dot_general(left, right, (((0,), (0,)), ((), ())), preferred_element_...  11.8 us
  transfers between devices with their start and end apart: 12, of which 4 were waited for; matrix products, arithmetic and copies ran while one was open for 18% of the time, Pallas kernels for 4%

profile of v2, /device:TPU:0, one launch (start us, length us, event | category | flops | bytes accessed | tf_op | source)
XLA Modules:
  0.0 516.2 jit_solution(12649957191463206460)
XLA Ops:
  10.1 2.7 fusion.30
  17.7 6.7 %collective-permute-start = (bf16[3,256,1024]{2,1,0:T(8,128)(2,1)S(1)}, bf16[3,256,1024]{2,1,0:T(8,128)(2,1)}, u32[]{:S(2)}, u32[]{:S(2)}) collective-permute-start(bf16[3,256,1024]{2,1,0:T(8,128)(2,1)S(1)} %copy-done.25), channel_id=1, source_target_pairs={{0,1},{1,2},{2,3},{4,5},{5,6},{6,7},{8,9},{9,10},{10,11},{12,13},{... | collective-permute-start | bytes 4718600 | tf_op jit(solution)/shard_map/ppermute | solution.py:573
  24.5 31.3 %collective-permute-done.1 = bf16[3,256,1024]{2,1,0:T(8,128)(2,1)} collective-permute-done((bf16[3,256,1024]{2,1,0:T(8,128)(2,1)S(1)}, bf16[3,256,1024]{2,1,0:T(8,128)(2,1)}, u32[]{:S(2)}, u32[]{:S(2)}) %collective-permute-start.1) | collective-permute-done | bytes 1572896 | tf_op jit(solution)/shard_map/ppermute | solution.py:574
  58.4 5.7 %collective-permute-start.4 = (bf16[3,256,1024]{2,1,0:T(8,128)(2,1)}, bf16[3,256,1024]{2,1,0:T(8,128)(2,1)}, u32[]{:S(2)}, u32[]{:S(2)}) collective-permute-start(bf16[3,256,1024]{2,1,0:T(8,128)(2,1)} %collective-permute-done), channel_id=1, source_target_pairs={{0,1},{1,2},{2,3},{4,5},{5,6},{6,7},{8,9},{9,10},{10,11},{12,13},{... | collective-permute-start | bytes 4718600 | tf_op jit(solution)/shard_map/ppermute | solution.py:573
  65.7 27.9 %collective-permute-done.2 = bf16[3,256,1024]{2,1,0:T(8,128)(2,1)} collective-permute-done((bf16[3,256,1024]{2,1,0:T(8,128)(2,1)}, bf16[3,256,1024]{2,1,0:T(8,128)(2,1)}, u32[]{:S(2)}, u32[]{:S(2)}) %collective-permute-start.2) | collective-permute-done | bytes 1572896 | tf_op jit(solution)/shard_map/ppermute | solution.py:574
  99.3 5.9 %collective-permute-start.5 = (bf16[3,256,1024]{2,1,0:T(8,128)(2,1)}, bf16[3,256,1024]{2,1,0:T(8,128)(2,1)}, u32[]{:S(2)}, u32[]{:S(2)}) collective-permute-start(bf16[3,256,1024]{2,1,0:T(8,128)(2,1)} %collective-permute-done.4), channel_id=1, source_target_pairs={{0,1},{1,2},{2,3},{4,5},{5,6},{6,7},{8,9},{9,10},{10,11},{12,13},{... | collective-permute-start | bytes 4718600 | tf_op jit(solution)/shard_map/ppermute | solution.py:573
  105.2 3.2 fusion.6.second_ref
  108.4 2.6 copy.122
  111.0 3.0 multiply_convert_fusion
  114.0 1.5 fusion.7.low_ref
  115.5 2.0 select_bitcast_fusion.1
  117.6 12.9 %collective-permute-done.3 = bf16[3,256,1024]{2,1,0:T(8,128)(2,1)} collective-permute-done((bf16[3,256,1024]{2,1,0:T(8,128)(2,1)}, bf16[3,256,1024]{2,1,0:T(8,128)(2,1)}, u32[]{:S(2)}, u32[]{:S(2)}) %collective-permute-start.3) | collective-permute-done | bytes 1572896 | tf_op jit(solution)/shard_map/ppermute | solution.py:574
  130.5 1.6 select_bitcast_fusion.2
  132.1 4.0 collective-permute-done.5
  136.1 1.6 select_bitcast_fusion
  137.7 3.2 pad_maximum_fusion.x_ref
  140.9 2.1 convolution_convert_fusion.2
  143.8 2.0 slice.93
  145.8 1.4 copy-done.31
  148.6 1.9 slice_bitcast_fusion
  150.9 2.0 copy-done.27
  153.6 3.5 fusion.8
  157.1 2.7 add_convert_fusion
  159.8 3.9 reshape.185
  163.6 6.2 %constant_dynamic-slice_fusion = (bf16[3,256,1,256]{3,2,1,0:T(2,128)(2,1)S(1)}, bf16[3,256,1,256]{3,2,1,0:T(2,128)(2,1)S(1)}, bf16[3,256,1,256]{3,2,1,0:T(2,128)(2,1)S(1)}, bf16[3,256,1,256]{3,2,1,0:T(2,128)(2,1)}) fusion(bf16[3,256,4,256]{3,2,1,0:T(4,128)(2,1)} %reshape.185, s32[]{:T(128)S(6)} %select_n.76, s32[]{:T(128)S(6)} %select_n.75, ...), kind=kLoop, calls=%fused_computation.87 | loop fusion | bytes 3145744 | tf_op jit(solution)/shard_map/dynamic-slice.3
  172.4 2.5 collective-permute-start.6
  174.9 3.4 collective-permute-start.7
  180.3 19.8 %qkv.1 = (bf16[3,1024,256]{2,1,0:T(8,128)(2,1)S(1)}, bf16[3,1024,256]{2,1,0:T(8,128)(2,1)S(1)}, bf16[3,1024,256]{2,1,0:T(8,128)(2,1)}, bf16[4,3,256,1024]{3,2,1,0:T(8,128)(2,1)}, bf16[4,3,256,128]{3,2,1,0:T(8,128)(2,1)S(1)}) custom-call(s32[1]{0:T(128)} %bitcast.z_ref, bf16[4,3,256,1024]{3,2,1,0:T(8,128)(2,1)} %pad_maximum_fusion.x_ref, ...), custom_call_target="tpu_custom_call" | custom-call | flops 6442450944 | bytes 18874368 | tf_op jit(solution)/shard_map/qkv/pallas_call | solution.py:611
  201.2 6.6 %copy.108 = bf16[3,4,256,1024]{3,2,1,0:T(8,128)(2,1)} copy(bf16[3,4,256,1024]{3,2,0,1:T(8,128)(2,1)} %bitcast.167) | data formatting | bytes 12582912 | tf_op jit(solution)/shard_map/transpose | solution.py:738
  207.8 8.7 %copy.121 = bf16[1024,3072]{1,0:T(8,128)(2,1)} copy(bf16[1024,3072]{0,1:T(8,128)(2,1)} %bitcast.153) | data formatting | bytes 12582912 | tf_op jit(solution)/shard_map/dot_general | solution.py:35
  217.3 1.7 copy_bitcast_fusion.4.b_ff_ref
  219.8 1.8 bitcast_dynamic-update-slice_fusion.4
  221.6 1.8 bitcast_dynamic-update-slice_fusion.2
  225.0 1.8 bitcast_dynamic-update-slice_fusion.5
  226.7 1.8 bitcast_dynamic-update-slice_fusion.3
  228.5 3.8 rev.3
  232.3 1.5 dynamic-slice_bitcast_fusion
  235.1 146.0 %middle.1 = (bf16[3,4,256,1024]{3,2,1,0:T(8,128)(2,1)}, bf16[3,3,1024,256]{3,2,1,0:T(8,128)(2,1)}, f32[768,1024]{1,0:T(8,128)}, f32[768,1024]{1,0:T(8,128)}, bf1...) custom-call(bf16[3,1024,256]{2,1,0:T(8,128)(2,1)} %copy-done.8, ...), custom_call_target="tpu_custom_call" | custom-call | tf_op jit(solution)/shard_map/middle/pallas_call | solution.py:683
  381.1 2.2 convolution_convert_fusion
  383.5 2.2 fusion.13
  385.7 2.7 convert_element_type.100
  391.4 1.7 convolution_add_fusion.1
  395.5 5.9 %convolution_convert_fusion.1 = bf16[128,8,128]{0,2,1:T(8,128)(2,1)S(1)} fusion(bf16[8,128,3072]{2,1,0:T(8,128)(2,1)} %bitcast.152, f32[3072,128]{1,0:T(8,128)} %convolution_add_fusion.1, bf16[3072,256]{1,0:T(8,128)(2,1)S(1)} %bitcast.155, bf16[128,256]{1,0:T(8,128)(2,1)S(1)} %get-tuple-element.114), kind=kOutput, calls=%fused_computation.30 | convolution fusion | flops 1007943680 | bytes 9764864 | tf_op jit(solution)/shard_map/dot_general | solution.py:35
  404.7 23.2 %finish.1 = (bf16[3,256,1024]{2,1,0:T(8,128)(2,1)}, bf16[3,256,1024]{2,1,0:T(8,128)(2,1)}, f32[4,1024]{1,0:T(4,128)}, f32[128,1024]{1,0:T(8,128)}, f32[128,1024]{1,0:T(8,128)}) custom-call(bf16[3,4,256,1024]{3,2,1,0:T(8,128)(2,1)} %get-tuple-element.56.local_ref, ...), custom_call_target="tpu_custom_call" | custom-call | tf_op jit(solution)/shard_map/finish/pallas_call | solution.py:761
  429.1 1.8 fusion.14
  432.4 2.0 copy-done.33
  434.5 64.1 %reduce.3 = (bf16[128,2048]{1,0:T(8,128)(2,1)S(1)}, f32[4,1024]{1,0:T(4,128)S(1)}, bf16[8,128,1152]{2,1,0:T(8,128)(2,1)S(1)}) custom-call(bf16[4,2,128,2048]{3,2,1,0:T(8,128)(2,1)} %bitcast.169, f32[4,1024]{1,0:T(4,128)S(1)} %copy-done.23, f32[128,1024]{1,0:T(8,128)S(1)} %copy-done.3, f32[128,1024]{1,0:T(8,128)S(1)} %copy-done.6, f32[128,1024]{1,0:T(8,128)S(1)} %copy-done.7, ...), custom_call_target="tpu_custom_call" | custom-call | tf_op jit(solution)/shard_map/reduce/pallas_call | solution.py:832
  500.7 8.8 %update.1 = (f32[128,384]{1,0:T(8,128)}, f32[512,128]{1,0:T(8,128)}, f32[128,1024]{1,0:T(8,128)}, f32[128,128]{1,0:T(8,128)}, f32[128,384]{1,0:T(8,128)}, /*inde...) custom-call(bf16[128,2048]{1,0:T(8,128)(2,1)S(1)} %get-tuple-element, ...), custom_call_target="tpu_custom_call" | custom-call | tf_op jit(solution)/shard_map/update/pallas_call | solution.py:903
  (200 shorter events, 44.0 us)
Async XLA Ops:
  7.2 133.7 %all-gather.4.cloned.1.call-start = ((), (), s32[]{:S(2)}) async-start(), calls=%async_computation | async-start | bytes 12976128 | tf_op jit(solution)/shard_map/all_gather | solution.py:556
  14.1 221.0 %all-gather.6.cloned.1.call-start = ((), (), s32[]{:S(2)}) async-start(), calls=%async_computation.1 | async-start | bytes 9437184 | tf_op jit(solution)/shard_map/all_gather | solution.py:557
  14.8 9.6 %copy-start.45 = (bf16[8192]{0:T(1024)(128)(2,1)S(1)}, bf16[8192]{0:T(1024)(128)(2,1)}, u32[]{:S(2)}) copy-start(bf16[8192]{0:T(1024)(128)(2,1)} %param.31) | copy-start | bytes 49156
  14.8 220.3 %all-gather.8.cloned.1.call-start = ((), (), s32[]{:S(2)}) async-start(), calls=%async_computation.2 | async-start | bytes 10616832 | tf_op jit(solution)/shard_map/all_gather | solution.py:559
  16.4 39.4 %collective-permute-start.1 = (bf16[3,256,1024]{2,1,0:T(8,128)(2,1)S(1)}, bf16[3,256,1024]{2,1,0:T(8,128)(2,1)}, u32[]{:S(2)}, u32[]{:S(2)}) collective-permute-start(bf16[3,256,1024]{2,1,0:T(8,128)(2,1)S(1)} %copy-done.25), channel_id=1, source_target_pairs={{1,0},{2,1},{3,2},{5,4},{6,5},{7,6},{9,8},{10,9},{11,10},{13,12},{... | collective-permute-start | bytes 4718600 | tf_op jit(solution)/shard_map/ppermute | solution.py:574
  17.7 40.7 %collective-permute-start = (bf16[3,256,1024]{2,1,0:T(8,128)(2,1)S(1)}, bf16[3,256,1024]{2,1,0:T(8,128)(2,1)}, u32[]{:S(2)}, u32[]{:S(2)}) collective-permute-start(bf16[3,256,1024]{2,1,0:T(8,128)(2,1)S(1)} %copy-done.25), channel_id=1, source_target_pairs={{0,1},{1,2},{2,3},{4,5},{5,6},{6,7},{8,9},{9,10},{10,11},{12,13},{... | collective-permute-start | bytes 4718600 | tf_op jit(solution)/shard_map/ppermute | solution.py:573
  55.8 37.8 %collective-permute-start.2 = (bf16[3,256,1024]{2,1,0:T(8,128)(2,1)}, bf16[3,256,1024]{2,1,0:T(8,128)(2,1)}, u32[]{:S(2)}, u32[]{:S(2)}) collective-permute-start(bf16[3,256,1024]{2,1,0:T(8,128)(2,1)} %collective-permute-done.1), channel_id=1, source_target_pairs={{1,0},{2,1},{3,2},{5,4},{6,5},{7,6},{9,8},{10,9},{11,10},{13,12},{... | collective-permute-start | bytes 4718600 | tf_op jit(solution)/shard_map/ppermute | solution.py:574
  58.0 36.9 %copy-start.47 = (s32[3,256]{1,0:T(4,128)S(1)}, s32[3,256]{1,0:T(4,128)}, u32[]{:S(2)}) copy-start(s32[3,256]{1,0:T(4,128)} %param.28) | copy-start | bytes 9220
  58.1 36.9 %copy-start.49 = (f32[22]{0:T(128)S(1)}, f32[22]{0:T(128)}, u32[]{:S(2)}) copy-start(f32[22]{0:T(128)} %param.29) | copy-start | bytes 268
  58.1 37.0 %copy-start.48 = (bf16[1024]{0:T(1024)(128)(2,1)S(1)}, bf16[1024]{0:T(1024)(128)(2,1)}, u32[]{:S(2)}) copy-start(bf16[1024]{0:T(1024)(128)(2,1)} %param.33) | copy-start | bytes 6148
  58.4 41.0 %collective-permute-start.4 = (bf16[3,256,1024]{2,1,0:T(8,128)(2,1)}, bf16[3,256,1024]{2,1,0:T(8,128)(2,1)}, u32[]{:S(2)}, u32[]{:S(2)}) collective-permute-start(bf16[3,256,1024]{2,1,0:T(8,128)(2,1)} %collective-permute-done), channel_id=1, source_target_pairs={{0,1},{1,2},{2,3},{4,5},{5,6},{6,7},{8,9},{9,10},{10,11},{12,13},{... | collective-permute-start | bytes 4718600 | tf_op jit(solution)/shard_map/ppermute | solution.py:573
  93.6 36.9 %collective-permute-start.3 = (bf16[3,256,1024]{2,1,0:T(8,128)(2,1)}, bf16[3,256,1024]{2,1,0:T(8,128)(2,1)}, u32[]{:S(2)}, u32[]{:S(2)}) collective-permute-start(bf16[3,256,1024]{2,1,0:T(8,128)(2,1)} %collective-permute-done.2), channel_id=1, source_target_pairs={{1,0},{2,1},{3,2},{5,4},{6,5},{7,6},{9,8},{10,9},{11,10},{13,12},{... | collective-permute-start | bytes 4718600 | tf_op jit(solution)/shard_map/ppermute | solution.py:574
  97.6 82.7 %copy-start = (f32[1024,128]{1,0:T(8,128)}, f32[1024,128]{1,0:T(8,128)S(1)}, u32[]{:S(2)}) copy-start(f32[1024,128]{1,0:T(8,128)S(1)} %copy.89.keep_ref) | copy-start | bytes 1572868
  97.9 82.4 %copy-start.1 = (f32[1024,128]{1,0:T(8,128)}, f32[1024,128]{1,0:T(8,128)S(1)}, u32[]{:S(2)}) copy-start(f32[1024,128]{1,0:T(8,128)S(1)} %copy.91.below_ref) | copy-start | bytes 1572868
  99.3 81.0 %copy-start.2 = (f32[1024,128]{1,0:T(8,128)}, f32[1024,128]{1,0:T(8,128)S(1)}, u32[]{:S(2)}) copy-start(f32[1024,128]{1,0:T(8,128)S(1)} %copy.90.above_ref) | copy-start | bytes 1572868
  99.3 36.8 %collective-permute-start.5 = (bf16[3,256,1024]{2,1,0:T(8,128)(2,1)}, bf16[3,256,1024]{2,1,0:T(8,128)(2,1)}, u32[]{:S(2)}, u32[]{:S(2)}) collective-permute-start(bf16[3,256,1024]{2,1,0:T(8,128)(2,1)} %collective-permute-done.4), channel_id=1, source_target_pairs={{0,1},{1,2},{2,3},{4,5},{5,6},{6,7},{8,9},{9,10},{10,11},{12,13},{... | collective-permute-start | bytes 4718600 | tf_op jit(solution)/shard_map/ppermute | solution.py:573
  111.0 3.0 copy-start.29
  132.1 5.6 %copy-start.26 = (bf16[3,256,1024]{2,1,0:T(8,128)(2,1)S(1)}, bf16[3,256,1024]{2,1,0:T(8,128)(2,1)}, u32[]{:S(2)}) copy-start(bf16[3,256,1024]{2,1,0:T(8,128)(2,1)} %x_ref.1) | copy-start | bytes 4718596
  143.0 2.8 copy-start.36
  143.8 3.4 copy-start.37
  147.8 2.8 copy-start.39
  150.8 6.2 %copy-start.24 = (bf16[8,16,8,1024]{3,2,0,1:T(8,128)(2,1)}, bf16[8,16,8,1024]{3,2,0,1:T(8,128)(2,1)S(1)}, u32[]{:S(2)}) copy-start(bf16[8,16,8,1024]{3,2,0,1:T(8,128)(2,1)S(1)} %copy.131) | copy-start | bytes 6291460
  153.6 3.5 copy-start.40
  172.4 46.6 %collective-permute-start.6 = (bf16[3,256,256]{2,1,0:T(8,128)(2,1)}, bf16[3,256,256]{2,1,0:T(8,128)(2,1)S(1)}, u32[]{:S(2)}, u32[]{:S(2)}) collective-permute-start(bf16[3,256,256]{2,1,0:T(8,128)(2,1)} %bitcast.141), channel_id=1, source_target_pairs={{0,1},{1,2},{2,3},{3,0},{4,5},{5,6},{6,7},{7,4},{8,9},{9,10},{10,1... | collective-permute-start | bytes 1179656 | tf_op jit(solution)/shard_map/ppermute | solution.py:549
  174.9 44.9 %collective-permute-start.7 = (bf16[3,256,256]{2,1,0:T(8,128)(2,1)}, bf16[3,256,256]{2,1,0:T(8,128)(2,1)}, u32[]{:S(2)}, u32[]{:S(2)}) collective-permute-start(bf16[3,256,256]{2,1,0:T(8,128)(2,1)} %bitcast.140), channel_id=1, source_target_pairs={{0,2},{1,3},{2,0},{3,1},{4,6},{5,7},{6,4},{7,5},{8,10},{9,11},{10,... | collective-permute-start | bytes 1179656 | tf_op jit(solution)/shard_map/ppermute | solution.py:549
  178.2 43.4 %collective-permute-start.8 = (bf16[3,256,256]{2,1,0:T(8,128)(2,1)}, bf16[3,256,256]{2,1,0:T(8,128)(2,1)}, u32[]{:S(2)}, u32[]{:S(2)}) collective-permute-start(bf16[3,256,256]{2,1,0:T(8,128)(2,1)} %bitcast.139), channel_id=1, source_target_pairs={{0,3},{1,0},{2,1},{3,2},{4,7},{5,4},{6,5},{7,6},{8,11},{9,8},{10,9... | collective-permute-start | bytes 1179656 | tf_op jit(solution)/shard_map/ppermute | solution.py:549
  180.2 19.9 %copy-start.41 = (bf16[128,256]{1,0:T(8,128)(2,1)}, bf16[128,256]{1,0:T(8,128)(2,1)S(1)}, u32[]{:S(2)}) copy-start(bf16[128,256]{1,0:T(8,128)(2,1)S(1)} %constant_dynamic-slice_fusion.6) | copy-start | bytes 196612
  200.1 7.6 %copy-start.8 = (bf16[3,1024,256]{2,1,0:T(8,128)(2,1)}, bf16[3,1024,256]{2,1,0:T(8,128)(2,1)S(1)}, u32[]{:S(2)}) copy-start(bf16[3,1024,256]{2,1,0:T(8,128)(2,1)S(1)} %get-tuple-element.53.q_ref) | copy-start | bytes 4718596
  200.1 7.6 %copy-start.9 = (bf16[3,1024,256]{2,1,0:T(8,128)(2,1)}, bf16[3,1024,256]{2,1,0:T(8,128)(2,1)S(1)}, u32[]{:S(2)}) copy-start(bf16[3,1024,256]{2,1,0:T(8,128)(2,1)S(1)} %get-tuple-element.54.k_ref) | copy-start | bytes 4718596
  207.8 8.7 %copy-start.32 = (bf16[3,256,1,256]{3,2,1,0:T(2,128)(2,1)S(1)}, bf16[3,256,1,256]{3,2,1,0:T(2,128)(2,1)}, u32[]{:S(2)}) copy-start(bf16[3,256,1,256]{3,2,1,0:T(2,128)(2,1)} %get-tuple-element.99) | copy-start | bytes 1179652
  383.5 4.9 copy-start.34
  427.9 3.0 copy-start.43
  431.3 3.1 copy-start.3
  431.3 3.0 copy-start.6
  431.3 3.0 copy-start.7
  431.3 3.0 copy-start.12
  431.3 3.0 copy-start.14
  431.3 3.0 copy-start.15
  431.3 3.0 copy-start.23
  434.4 66.3 %copy-start.11 = (f32[128,384]{1,0:T(8,128)S(1)}, f32[128,384]{1,0:T(8,128)}, u32[]{:S(2)}) copy-start(f32[128,384]{1,0:T(8,128)} %refs_0_.1) | copy-start | bytes 589828
  434.4 66.3 %copy-start.13 = (s32[128,1024]{1,0:T(8,128)S(1)}, s32[128,1024]{1,0:T(8,128)}, u32[]{:S(2)}) copy-start(s32[128,1024]{1,0:T(8,128)} %refs_11_.1) | copy-start | bytes 1572868
  434.4 66.2 %copy-start.16 = (f32[512,128]{1,0:T(8,128)S(1)}, f32[512,128]{1,0:T(8,128)}, u32[]{:S(2)}) copy-start(f32[512,128]{1,0:T(8,128)} %refs_5_.1) | copy-start | bytes 786436
  434.4 66.2 %copy-start.17 = (f32[512,128]{1,0:T(8,128)S(1)}, f32[512,128]{1,0:T(8,128)}, u32[]{:S(2)}) copy-start(f32[512,128]{1,0:T(8,128)} %refs_6_.1) | copy-start | bytes 786436
  434.4 66.2 %copy-start.18 = (s32[512,128]{1,0:T(8,128)S(1)}, s32[512,128]{1,0:T(8,128)}, u32[]{:S(2)}) copy-start(s32[512,128]{1,0:T(8,128)} %refs_7_.1) | copy-start | bytes 786436
  434.4 66.2 %copy-start.19 = (f32[128,384]{1,0:T(8,128)S(1)}, f32[128,384]{1,0:T(8,128)}, u32[]{:S(2)}) copy-start(f32[128,384]{1,0:T(8,128)} %refs_1_.1) | copy-start | bytes 589828
  434.4 66.2 %copy-start.20 = (f32[128,384]{1,0:T(8,128)S(1)}, f32[128,384]{1,0:T(8,128)}, u32[]{:S(2)}) copy-start(f32[128,384]{1,0:T(8,128)} %refs_2_.1) | copy-start | bytes 589828
  434.5 66.2 %copy-start.21 = (s32[128,384]{1,0:T(8,128)S(1)}, s32[128,384]{1,0:T(8,128)}, u32[]{:S(2)}) copy-start(s32[128,384]{1,0:T(8,128)} %refs_3_.1) | copy-start | bytes 589828
  434.5 66.2 %copy-start.22 = (s32[128,128]{1,0:T(8,128)S(1)}, s32[128,128]{1,0:T(8,128)}, u32[]{:S(2)}) copy-start(s32[128,128]{1,0:T(8,128)} %refs_15_.1) | copy-start | bytes 196612
  (14 other events, 22.7 us)
Sparse Core Ops, SparseCore 0:
  14.2 70.3 all-gather.3
  87.1 54.3 all-gather.5
  143.4 58.8 all-gather.7

commit v3 on v2

--- a/solution.py
+++ b/solution.py
@@ -3,6 +3,7 @@
 
 import jax
 import jax.numpy as jnp
+import numpy as np
 from jax import lax
 from jax.experimental import pallas as pl
 from jax.experimental.pallas import tpu as pltpu
@@ -135,6 +136,277 @@
         store(i, 3, dv_ref[rows].astype(bf16))
 
 
+def normal(x):
+    centre = x - jnp.mean(x, axis=-1, keepdims=True)
+    return centre * lax.rsqrt(jnp.mean(centre * centre, axis=-1, keepdims=True) + norm_eps)
+
+
+def front_kernel(
+    tokens_ref, win_ref, wdown_ref, a_ref, aff_ref, b_ref, bff_ref,
+    cot_ref, weight_ref, gain_ref, shift_ref, bias_ref, freq_ref,
+    win_out, wdown_out, a_out, aff_out, b_out, bff_out,
+    q_out, k_out, v_out, first_out, mid_out, g_out,
+    low_ref, second_ref, mid_up_ref, mid_up_t_ref, dmid_ff_ref, dmid_ff_t_ref, dmid_out_t_ref,
+    keep_ref, above_ref, below_ref,
+    x_all, q_s, k_s, v_s, first_s, mid_s, ga, wout_v, wqkv_v, a_v, b_v, bff_v,
+    sx, qx, own_sem, sr, qr, sl, ql, sd, qd, load_sem, store_sem, token_sem,
+    *, n, depth,
+):
+    z = lax.axis_index("blk")
+    dp = lax.axis_index("dp")
+    y, x, c = dp // 4, lax.rem(dp // 2, 2), lax.rem(dp, 2)
+    core = (dp + 1 - 2 * c, z)
+    along_x = (dp + 2 - 4 * x, z)
+    along_y = (dp + 4 - 8 * y, z)
+    peers = [(dp, lax.rem(z + t, n)) for t in range(1, n)]
+    seqs, span, width = tokens_ref.shape
+    kr, down_rows, rank = win_ref.shape[0], wdown_ref.shape[0], b_ref.shape[0]
+    b_w, f_w = b_ref.shape[1], bff_ref.shape[1]
+    cz = q_s.shape[2]
+    lanes = keep_ref.shape[1]
+    four = 4 * width
+
+    barrier = pltpu.get_barrier_semaphore()
+    for peer in [core, along_x, along_y] + peers:
+        pl.semaphore_signal(barrier, inc=1, device_id=peer, device_id_type=MESH)
+    pl.semaphore_wait(barrier, 2 + n)
+
+    def remote(src, dst, send, recv, peer):
+        return pltpu.make_async_remote_copy(
+            src_ref=src, dst_ref=dst, send_sem=send, recv_sem=recv, device_id=peer, device_id_type=MESH
+        )
+
+    shards = [
+        (win_ref.at[:, :four], lambda d: win_out.at[pl.ds(pl.multiple_of(d * kr, kr), kr), :four]),
+        (a_ref, lambda d: a_out.at[pl.ds(pl.multiple_of(d * kr, kr), kr), :]),
+        (b_ref, lambda d: b_out.at[:, pl.ds(pl.multiple_of(d * b_w, b_w), b_w)]),
+        (bff_ref, lambda d: bff_out.at[:, pl.ds(pl.multiple_of(d * f_w, f_w), f_w)]),
+        (win_ref.at[:, four:], lambda d: win_out.at[pl.ds(pl.multiple_of(d * kr, kr), kr), four:]),
+        (wdown_ref, lambda d: wdown_out.at[pl.ds(pl.multiple_of(d * down_rows, down_rows), down_rows), :]),
+        (aff_ref, lambda d: aff_out.at[pl.ds(pl.multiple_of(d * down_rows, down_rows), down_rows), :]),
+    ]
+    groups = [(0, 1, 2, 3), (4,), (5, 6)]
+    from_x, from_y = dp + 2 - 4 * x, dp + 4 - 8 * y
+    across = dp + 2 - 4 * x + 4 - 8 * y
+    onward = jnp.where(c == 0, from_y, from_x)
+    target = (jnp.where(c == 0, along_x[0], along_y[0]), z)
+
+    def hop(i, kind):
+        shard, there = shards[i]
+        src, dst, peer = {
+            0: (shard, there(dp), along_x),
+            1: (shard, there(dp), along_y),
+            2: (shard, there(dp), core),
+            3: (there(onward), there(onward), target),
+            4: (there(from_x), there(from_x), core),
+            5: (there(from_y), there(from_y), core),
+            6: (there(across), there(across), core),
+        }[kind]
+        return remote(src, dst, sx.at[i, kind], qx.at[i, kind], peer)
+
+    def own_copy(i):
+        return pltpu.make_async_copy(shards[i][0], shards[i][1](dp), own_sem.at[i])
+
+    def start_own(group):
+        for kind in (0, 1, 2):
+            for i in groups[group]:
+                hop(i, kind).start()
+        for i in groups[group]:
+            own_copy(i).start()
+
+    def pass_on(group):
+        for i in groups[group]:
+            hop(i, 0).wait_recv()
+            hop(i, 1).wait_recv()
+        for kind in (3, 4, 5):
+            for i in groups[group]:
+                hop(i, kind).start()
+
+    def close(group):
+        for i in groups[group]:
+            hop(i, 3).wait_recv()
+            hop(i, 6).start()
+
+    def arrived(group):
+        for i in groups[group]:
+            own_copy(i).wait()
+            for kind in (2, 4, 5, 6):
+                hop(i, kind).wait_recv()
+
+    def rightward(s):
+        return remote(x_all.at[z - s + 1], x_all.at[z - s + 1], sr.at[s], qr.at[s], (dp, z + 1))
+
+    def leftward(s):
+        return remote(x_all.at[z + s - 1], x_all.at[z + s - 1], sl.at[s], ql.at[s], (dp, z - 1))
+
+    def from_left(s):
+        return remote(x_all.at[z - s], x_all.at[z - s], sr.at[s], qr.at[s], (dp, z - 1))
+
+    def from_right(s):
+        return remote(x_all.at[z + s], x_all.at[z + s], sl.at[s], ql.at[s], (dp, z + 1))
+
+    def ring_start(s):
+        pl.when((z < n - 1) & (z - s + 1 >= 0))(lambda: rightward(s).start())
+        pl.when((z > 0) & (z + s - 1 < n))(lambda: leftward(s).start())
+
+    def ring_wait(s):
+        pl.when(z - s >= 0)(lambda: from_left(s).wait_recv())
+        pl.when(z + s < n)(lambda: from_right(s).wait_recv())
+
+    def ring_end(s):
+        pl.when((z < n - 1) & (z - s + 1 >= 0))(lambda: rightward(s).wait_send())
+        pl.when((z > 0) & (z + s - 1 < n))(lambda: leftward(s).wait_send())
+
+    token_copy = pltpu.make_async_copy(tokens_ref, x_all.at[z], token_sem.at[0])
+    token_copy.start()
+    start_own(0)
+    token_copy.wait()
+    ring_start(1)
+
+    unit_lane = lax.rem(lax.broadcasted_iota(jnp.int32, (1, lanes), 1), depth)
+    half = ROTARY // 2
+    for b in range(n):
+        rows = slice(b * span, (b + 1) * span)
+        place = (lax.broadcasted_iota(jnp.int32, (span, lanes), 0) + b * span).astype(f32)
+        angle = place * freq_ref[...]
+        cosine, sine = jnp.cos(angle), jnp.sin(angle)
+        keep_ref[rows] = jnp.where(unit_lane < ROTARY, cosine, 1.0)
+        above_ref[rows] = jnp.where(unit_lane < half, -sine, 0.0)
+        below_ref[rows] = jnp.where((unit_lane >= half) & (unit_lane < ROTARY), sine, 0.0)
+    for q in range(seqs):
+        part = slice(q * span, (q + 1) * span)
+        low_ref[part] = (cot_ref[q].astype(f32) * weight_ref[part]).astype(bf16)
+        unit = normal(x_all[z, q].astype(f32))
+        second_ref[part] = (unit * gain_ref[1:2] + shift_ref[1:2]).astype(bf16)
+
+    pass_on(0)
+    start_own(1)
+    ring_wait(1)
+    if n > 2:
+        ring_start(2)
+    close(0)
+    arrived(0)
+
+    loads = [
+        pltpu.make_async_copy(win_out.at[:, 3 * width : four], wout_v, load_sem.at[0]),
+        pltpu.make_async_copy(a_out, a_v, load_sem.at[1]),
+        pltpu.make_async_copy(b_out, b_v, load_sem.at[2]),
+        pltpu.make_async_copy(bff_out, bff_v, load_sem.at[3]),
+    ] + [
+        pltpu.make_async_copy(
+            win_out.at[:, pl.ds(pl.multiple_of(t * width + z * cz, cz), cz)], wqkv_v.at[t], load_sem.at[4 + t]
+        )
+        for t in range(3)
+    ]
+    for copy in loads:
+        copy.start()
+    for copy in loads:
+        copy.wait()
+
+    def grad_out(q, _):
+        part = pl.ds(pl.multiple_of(q * span, span), span)
+        low = low_ref[part, :]
+        dmid = (adapter_scale * nt(low, b_v[:, 3 * width : four])).astype(bf16)
+        dmid_out_t_ref[q] = dmid.T
+        for g in range(n):
+            rows = slice(g * cz, (g + 1) * cz)
+            value = nt(low, wout_v[rows]) + nt(dmid, a_v[rows, rank : 2 * rank])
+            ga[g, q] = value.astype(bf16)
+        return 0
+
+    lax.fori_loop(0, seqs, grad_out, 0)
+    place_own = pl.ds(pl.multiple_of(z * span, span), span)
+
+    def grad_send(t):
+        return remote(ga.at[lax.rem(z + t, n)], g_out.at[:, place_own, :], sd.at[t], qd.at[t], peers[t - 1])
+
+    grad_own = pltpu.make_async_copy(ga.at[z], g_out.at[:, place_own, :], token_sem.at[1])
+    grad_own.start()
+    for t in range(1, n):
+        grad_send(t).start()
+
+    def stores(b):
+        rows = pl.ds(pl.multiple_of(b * span, span), span)
+        return [
+            pltpu.make_async_copy(src.at[:, rows, :], dst.at[:, rows, :], store_sem.at[i, b])
+            for i, (src, dst) in enumerate(
+                ((q_s, q_out), (k_s, k_out), (v_s, v_out), (first_s, first_out), (mid_s, mid_out))
+            )
+        ]
+
+    def project_block(b):
+        rows = pl.ds(pl.multiple_of(b * span, span), span)
+
+        def one(q, _):
+            first = (normal(x_all[b, q].astype(f32)) * gain_ref[0:1] + shift_ref[0:1]).astype(bf16)
+            mid = nn(first, a_v[:, 0:rank]).astype(bf16)
+            first_s[q, rows, :] = first
+            mid_s[q, rows, :] = mid
+            for t, kept in enumerate((q_s, k_s, v_s)):
+                at = pl.ds(pl.multiple_of(t * width + z * cz, cz), cz)
+                value = nn(first, wqkv_v[t]) + adapter_scale * nn(mid, b_v[:, at]) + bias_ref[:, at]
+                if t < 2:
+                    value = jnp.concatenate(
+                        [
+                            turn(value[:, i : i + lanes], keep_ref[rows, :], above_ref[rows, :], below_ref[rows, :], 1.0)
+                            for i in range(0, cz, lanes)
+                        ],
+                        axis=1,
+                    )
+                kept[q, rows, :] = value.astype(bf16)
+            return 0
+
+        lax.fori_loop(0, seqs, one, 0)
+        for copy in stores(b):
+            copy.start()
+
+    def project_near(s):
+        def side(i, _):
+            b = z + s * (2 * i - 1)
+            pl.when((b >= 0) & (b < n))(lambda: project_block(b))
+            return 0
+
+        lax.fori_loop(0, 2 if s else 1, side, 0)
+
+    def local_products(q, _):
+        part = pl.ds(pl.multiple_of(q * span, span), span)
+        mid = nn(second_ref[part, :], a_v[:, 2 * rank : 3 * rank]).astype(bf16)
+        mid_up_ref[part, :] = mid
+        mid_up_t_ref[q] = mid.T
+        dmid = (adapter_scale * nt(low_ref[part, :], bff_v[...])).astype(bf16)
+        dmid_ff_ref[part, :] = dmid
+        dmid_ff_t_ref[q] = dmid.T
+        return 0
+
+    project_block(z)
+    pass_on(1)
+    start_own(2)
+    for s in range(2, n):
+        ring_wait(s)
+        if s + 1 < n:
+            ring_start(s + 1)
+        project_near(s - 1)
+        if s == 2:
+            close(1)
+            lax.fori_loop(0, seqs, local_products, 0)
+            pass_on(2)
+    project_near(n - 1)
+    close(2)
+    arrived(1)
+    arrived(2)
+    for i in range(len(shards)):
+        for kind in range(7):
+            hop(i, kind).wait_send()
+    for s in range(1, n):
+        ring_end(s)
+    grad_own.wait()
+    for t in range(1, n):
+        grad_send(t).wait()
+    for b in range(n):
+        for copy in stores(b):
+            copy.wait()
+
+
 def middle_kernel(
     q_ref, k_ref, v_ref, g_ref, keep_ref, above_ref, below_ref, mid_qkv_t_ref,
     second_ref, low_ref, mid_ref, mid_t_ref, dmid_ref, dmid_t_ref,
@@ -195,10 +467,9 @@
 
     @pl.when(step >= steps)
     def _():
-        total = second_ref.shape[0]
-        size = 256 if total % 256 == 0 else 128
-        for at in range(0, total, size):
-            rows = slice(at, at + size)
+        count, size = mid_t_ref.shape[0], mid_t_ref.shape[2]
+        for at in range(count):
+            rows = slice(at * size, (at + 1) * size)
             pre = nn(second_ref[rows], up_ref[...]) + bias_ref[...] + adapter_scale * nn(mid_ref[rows], b_ref[...])
             cdf = 0.5 + 0.5 * lax.erf(pre * (1.0 / math.sqrt(2.0)))
             hidden = (pre * cdf).astype(bf16)
@@ -209,8 +480,8 @@
             back_ref[rows] += nt(dup, up_ref[...])
             mid_acc[rows] += nn(hidden, a_ref[...])
             dmid_acc[rows] += nt(dup, b_ref[...])
-            ga = nn(dmid_t_ref[:, rows], hidden)
-            gb = nn(mid_t_ref[:, rows], dup)
+            ga = nn(dmid_t_ref[at], hidden)
+            gb = nn(mid_t_ref[at], dup)
             ga_ref[...] = ga if at == 0 else ga_ref[...] + ga
             gb_ref[...] = gb if at == 0 else gb_ref[...] + gb
 
@@ -248,7 +519,8 @@
     mid_acc[...] += nn(out, a_out_ref[...])
     first_acc[...] += nt(dq, wq_ref[...]) + nt(dk, wk_ref[...]) + nt(dv, wv_ref[...])
     dmid_acc[...] += nt(dq, bq_ref[...]) + nt(dk, bk_ref[...]) + nt(dv, bv_ref[...])
-    ga_ref[...] = nn(dmid_out_t_ref[...], out)
+    size = x_ref.shape[1]
+    ga_ref[...] = sum(nn(dmid_out_t_ref[q], out[q * size : (q + 1) * size]) for q in range(x_ref.shape[0]))
 
     @pl.when(t == pl.num_programs(0) - 1)
     def _():
@@ -549,121 +821,184 @@
         return lax.ppermute(values, "blk", [(i, (i + s) % n) for i in range(n)])
 
     b_cols = adapt_b.shape[1] + adapt_b_ff.shape[1]
-    b_shard = jnp.concatenate([adapt_b, adapt_b_ff], axis=1).astype(bf16)
-    one = jnp.concatenate(
-        [frozen_input_weights[:, : 4 * width], adapt_a.astype(bf16), b_shard.reshape(kr, -1)], axis=1
-    )
-    one = lax.all_gather(one, "dp", axis=0, tiled=True)
-    two = lax.all_gather(frozen_input_weights[:, 4 * width :], "dp", axis=0, tiled=True)
-    three = jnp.concatenate([frozen_down_weight, adapt_a_ff.astype(bf16)], axis=1)
-    three = lax.all_gather(three, "dp", axis=0, tiled=True)
-    a_at = 4 * width
-    b_at = a_at + 3 * rank
-    a_all = one[:, a_at:b_at]
-    b_all = one[:, b_at:].reshape(dp_n, rank, b_cols)
-    b_in = jnp.transpose(b_all[:, :, : adapt_b.shape[1]], (1, 0, 2)).reshape(rank, -1)
-    b_ff = jnp.transpose(b_all[:, :, adapt_b.shape[1] :], (1, 0, 2)).reshape(rank, width)
-    w_out = one[:, 3 * width : 4 * width]
-    w_up = two
-    w_down, a_ff = three[:, :width], three[:, width:]
-
-    right, left = tokens, tokens
-    rights, lefts = [None], [None]
-    for s in range(1, n):
-        right = lax.ppermute(right, "blk", [(i, i + 1) for i in range(n - 1)])
-        left = lax.ppermute(left, "blk", [(i + 1, i) for i in range(n - 1)])
-        rights.append(right)
-        lefts.append(left)
-    x_all = jnp.stack(
-        [tokens] + [jnp.where(z >= s, rights[s], lefts[n - s]) for s in range(1, n)]
-    )
-
+    bias32 = bias_in.astype(f32)
     lookup = (domain_ids[..., None] == jnp.arange(DOMAINS, dtype=jnp.int32)).astype(f32)
     row_weight = jnp.sum(lookup * domain_weight, axis=-1).reshape(rows, 1)
-    row_grad = cotangent.astype(f32).reshape(rows, width) * row_weight
-    grad_low = row_grad.astype(bf16)
-    b_out = b_in[:, 3 * width : 4 * width]
-    a_out = a_all[:, rank : 2 * rank]
-    dmid_out = (adapter_scale * nt(grad_low, b_out)).astype(bf16)
-    grad_att = (nt(grad_low, w_out) + nt(dmid_out, a_out)).astype(bf16)
-    grad_att = jnp.transpose(grad_att.reshape(seqs, span, n, cz), (2, 0, 1, 3))
-
-    def piece(values, s):
-        return lax.dynamic_index_in_dim(values, lax.rem(z + s, n), 0, keepdims=False)
-
-    g_all = jnp.stack(
-        [piece(grad_att, 0)] + [shift_by(piece(grad_att, s), s) for s in range(1, n)]
-    )
-
-    tables = rope_lane_tables(length, depth, lanes)
-    own = [lax.dynamic_slice_in_dim(b_in[:, t * width : (t + 1) * width], z * cz, cz, 1) for t in range(3)]
-    b_own = jnp.concatenate(own, axis=1)
-    bias32 = bias_in.astype(f32)
-    bias_own = jnp.concatenate(
-        [lax.dynamic_slice_in_dim(bias32, t * width + z * cz, cz, 0) for t in range(3)]
-    ).reshape(1, 3 * cz)
-
-    def block_of(s, z_ref):
-        return lax.rem(z_ref[0] - s + n, n)
-
-    table_spec = pl.BlockSpec((span, lanes), lambda s, q, z_ref: (block_of(s, z_ref), 0))
-    head_spec = pl.BlockSpec((1, span, cz), lambda s, q, z_ref: (q, block_of(s, z_ref), 0))
-    query, keys, values, first_all, mid_all = pl.pallas_call(
-        qkv_kernel,
-        grid_spec=pltpu.PrefetchScalarGridSpec(
-            num_scalar_prefetch=1,
-            grid=(n, seqs),
-            in_specs=[
-                pl.BlockSpec((1, 1, span, width), lambda s, q, z_ref: (s, q, 0, 0)),
-                pl.BlockSpec((1, width), lambda s, q, z_ref: (0, 0)),
-                pl.BlockSpec((1, width), lambda s, q, z_ref: (0, 0)),
-                pl.BlockSpec((width, cz), lambda s, q, z_ref: (0, z_ref[0])),
-                pl.BlockSpec((width, cz), lambda s, q, z_ref: (0, n + z_ref[0])),
-                pl.BlockSpec((width, cz), lambda s, q, z_ref: (0, 2 * n + z_ref[0])),
-                pl.BlockSpec((width, rank), lambda s, q, z_ref: (0, a_at // rank)),
-                pl.BlockSpec((rank, 3 * cz), lambda s, q, z_ref: (0, 0)),
-                pl.BlockSpec((1, 3 * cz), lambda s, q, z_ref: (0, 0)),
-                table_spec,
-                table_spec,
-                table_spec,
+    whole_front = dp_n == 8 and rank % (16 * n) == 0
+    if whole_front:
+        vmem = pl.BlockSpec(memory_space=pltpu.VMEM)
+        hbm = pl.BlockSpec(memory_space=pl.ANY)
+        dma = pltpu.SemaphoreType.DMA
+        half = ROTARY // 2
+        freq = [rope_base ** (-(k * 2.0) / ROTARY) for k in range(half)]
+        freq = np.tile(np.array(freq + freq + [0.0] * (depth - ROTARY), np.float32), lanes // depth)
+
+        def shape(*dims, dtype=bf16):
+            return jax.ShapeDtypeStruct(dims, dtype)
+
+        (
+            w_in, w_down, a_all, a_ff, b_in, b_ff, query, keys, values, first_pos, mid_pos, g_pos,
+            grad_low, second, mid_up, mid_up_t, dmid_ff, dmid_ff_t, dmid_out_t, *tables,
+        ) = pl.pallas_call(
+            functools.partial(front_kernel, n=n, depth=depth),
+            in_specs=[hbm] * 7 + [vmem] * 6,
+            out_specs=[hbm] * 12 + [vmem] * 10,
+            out_shape=[
+                shape(width, 8 * width), shape(inner, width), shape(width, 3 * rank), shape(inner, rank),
+                shape(rank, 8 * width), shape(rank, width),
+                shape(seqs, length, cz), shape(seqs, length, cz), shape(seqs, length, cz),
+                shape(seqs, length, width), shape(seqs, length, rank), shape(seqs, length, cz),
+                shape(rows, width), shape(rows, width),
+                shape(rows, rank), shape(seqs, rank, span), shape(rows, rank), shape(seqs, rank, span),
+                shape(seqs, rank, span),
+                shape(length, lanes, dtype=f32), shape(length, lanes, dtype=f32), shape(length, lanes, dtype=f32),
             ],
-            out_specs=[
-                head_spec,
-                head_spec,
-                head_spec,
-                pl.BlockSpec((1, 1, span, width), lambda s, q, z_ref: (block_of(s, z_ref), q, 0, 0)),
-                pl.BlockSpec((1, 1, span, rank), lambda s, q, z_ref: (block_of(s, z_ref), q, 0, 0)),
+            scratch_shapes=[
+                pltpu.VMEM((n, seqs, span, width), bf16),
+                pltpu.VMEM((seqs, length, cz), bf16),
+                pltpu.VMEM((seqs, length, cz), bf16),
+                pltpu.VMEM((seqs, length, cz), bf16),
+                pltpu.VMEM((seqs, length, width), bf16),
+                pltpu.VMEM((seqs, length, rank), bf16),
+                pltpu.VMEM((n, seqs, span, cz), bf16),
+                pltpu.VMEM((width, width), bf16),
+                pltpu.VMEM((3, width, cz), bf16),
+                pltpu.VMEM((width, 3 * rank), bf16),
+                pltpu.VMEM((rank, 8 * width), bf16),
+                pltpu.VMEM((rank, width), bf16),
+                dma((7, 7)), dma((7, 7)), dma((7,)),
+                dma((n,)), dma((n,)), dma((n,)), dma((n,)), dma((n,)), dma((n,)),
+                dma((7,)), dma((5, n)), dma((2,)),
             ],
-        ),
-        out_shape=[jax.ShapeDtypeStruct((seqs, length, cz), bf16)] * 3
-        + [
-            jax.ShapeDtypeStruct((n, seqs, span, width), bf16),
-            jax.ShapeDtypeStruct((n, seqs, span, rank), bf16),
-        ],
-        compiler_params=pltpu.CompilerParams(vmem_limit_bytes=48 << 20),
-        cost_estimate=pl.CostEstimate(
-            flops=2 * n * rows * width * 4 * cz, bytes_accessed=6 * n * rows * width, transcendentals=0
-        ),
-        name="qkv",
-    )(
-        z_arr, x_all, norm_gain[0:1], norm_shift[0:1], one, one, one, one, b_own, bias_own, *tables
-    )
-
-    input_rows = tokens.astype(f32).reshape(rows, width)
-    centre = input_rows - jnp.mean(input_rows, axis=-1, keepdims=True)
-    inv = lax.rsqrt(jnp.mean(centre * centre, axis=-1, keepdims=True) + norm_eps)
-    second = (centre * inv * norm_gain[1] + norm_shift[1]).astype(bf16)
-    a_up = a_all[:, 2 * rank :]
-    mid_up = nn(second, a_up).astype(bf16)
-    dmid_ff = (adapter_scale * nt(grad_low, b_ff)).astype(bf16)
+            compiler_params=pltpu.CompilerParams(
+                collective_id=2, has_side_effects=True, vmem_limit_bytes=58 << 20
+            ),
+            name="front",
+        )(
+            tokens, frozen_input_weights, frozen_down_weight,
+            adapt_a.astype(bf16), adapt_a_ff.astype(bf16), adapt_b.astype(bf16), adapt_b_ff.astype(bf16),
+            cotangent, row_weight, norm_gain, norm_shift, bias32.reshape(1, -1), freq.reshape(1, -1),
+        )
+    else:
+        row_grad = cotangent.astype(f32).reshape(rows, width) * row_weight
+        grad_low = row_grad.astype(bf16)
+        b_shard = jnp.concatenate([adapt_b, adapt_b_ff], axis=1).astype(bf16)
+        one = jnp.concatenate(
+            [frozen_input_weights[:, : 4 * width], adapt_a.astype(bf16), b_shard.reshape(kr, -1)], axis=1
+        )
+        one = lax.all_gather(one, "dp", axis=0, tiled=True)
+        two = lax.all_gather(frozen_input_weights[:, 4 * width :], "dp", axis=0, tiled=True)
+        three = jnp.concatenate([frozen_down_weight, adapt_a_ff.astype(bf16)], axis=1)
+        three = lax.all_gather(three, "dp", axis=0, tiled=True)
+        a_at = 4 * width
+        b_at = a_at + 3 * rank
+        a_all = one[:, a_at:b_at]
+        b_all = one[:, b_at:].reshape(dp_n, rank, b_cols)
+        b_in = jnp.transpose(b_all[:, :, : adapt_b.shape[1]], (1, 0, 2)).reshape(rank, -1)
+        b_ff = jnp.transpose(b_all[:, :, adapt_b.shape[1] :], (1, 0, 2)).reshape(rank, width)
+        w_out = one[:, 3 * width : 4 * width]
+        w_up = two
+        w_down, a_ff = three[:, :width], three[:, width:]
+
+        right, left = tokens, tokens
+        rights, lefts = [None], [None]
+        for s in range(1, n):
+            right = lax.ppermute(right, "blk", [(i, i + 1) for i in range(n - 1)])
+            left = lax.ppermute(left, "blk", [(i + 1, i) for i in range(n - 1)])
+            rights.append(right)
+            lefts.append(left)
+        x_all = jnp.stack(
+            [tokens] + [jnp.where(z >= s, rights[s], lefts[n - s]) for s in range(1, n)]
+        )
+
+        b_out = b_in[:, 3 * width : 4 * width]
+        a_out = a_all[:, rank : 2 * rank]
+        dmid_out = (adapter_scale * nt(grad_low, b_out)).astype(bf16)
+        grad_att = (nt(grad_low, w_out) + nt(dmid_out, a_out)).astype(bf16)
+        grad_att = jnp.transpose(grad_att.reshape(seqs, span, n, cz), (2, 0, 1, 3))
+
+        def piece(values, s):
+            return lax.dynamic_index_in_dim(values, lax.rem(z + s, n), 0, keepdims=False)
+
+        g_all = jnp.stack(
+            [piece(grad_att, 0)] + [shift_by(piece(grad_att, s), s) for s in range(1, n)]
+        )
+
+        tables = rope_lane_tables(length, depth, lanes)
+        own = [lax.dynamic_slice_in_dim(b_in[:, t * width : (t + 1) * width], z * cz, cz, 1) for t in range(3)]
+        b_own = jnp.concatenate(own, axis=1)
+        bias_own = jnp.concatenate(
+            [lax.dynamic_slice_in_dim(bias32, t * width + z * cz, cz, 0) for t in range(3)]
+        ).reshape(1, 3 * cz)
+
+        def block_of(s, z_ref):
+            return lax.rem(z_ref[0] - s + n, n)
+
+        table_spec = pl.BlockSpec((span, lanes), lambda s, q, z_ref: (block_of(s, z_ref), 0))
+        head_spec = pl.BlockSpec((1, span, cz), lambda s, q, z_ref: (q, block_of(s, z_ref), 0))
+        query, keys, values, first_all, mid_all = pl.pallas_call(
+            qkv_kernel,
+            grid_spec=pltpu.PrefetchScalarGridSpec(
+                num_scalar_prefetch=1,
+                grid=(n, seqs),
+                in_specs=[
+                    pl.BlockSpec((1, 1, span, width), lambda s, q, z_ref: (s, q, 0, 0)),
+                    pl.BlockSpec((1, width), lambda s, q, z_ref: (0, 0)),
+                    pl.BlockSpec((1, width), lambda s, q, z_ref: (0, 0)),
+                    pl.BlockSpec((width, cz), lambda s, q, z_ref: (0, z_ref[0])),
+                    pl.BlockSpec((width, cz), lambda s, q, z_ref: (0, n + z_ref[0])),
+                    pl.BlockSpec((width, cz), lambda s, q, z_ref: (0, 2 * n + z_ref[0])),
+                    pl.BlockSpec((width, rank), lambda s, q, z_ref: (0, a_at // rank)),
+                    pl.BlockSpec((rank, 3 * cz), lambda s, q, z_ref: (0, 0)),
+                    pl.BlockSpec((1, 3 * cz), lambda s, q, z_ref: (0, 0)),
+                    table_spec,
+                    table_spec,
+                    table_spec,
+                ],
+                out_specs=[
+                    head_spec,
+                    head_spec,
+                    head_spec,
+                    pl.BlockSpec((1, 1, span, width), lambda s, q, z_ref: (block_of(s, z_ref), q, 0, 0)),
+                    pl.BlockSpec((1, 1, span, rank), lambda s, q, z_ref: (block_of(s, z_ref), q, 0, 0)),
+                ],
+            ),
+            out_shape=[jax.ShapeDtypeStruct((seqs, length, cz), bf16)] * 3
+            + [
+                jax.ShapeDtypeStruct((n, seqs, span, width), bf16),
+                jax.ShapeDtypeStruct((n, seqs, span, rank), bf16),
+            ],
+            compiler_params=pltpu.CompilerParams(vmem_limit_bytes=48 << 20),
+            cost_estimate=pl.CostEstimate(
+                flops=2 * n * rows * width * 4 * cz, bytes_accessed=6 * n * rows * width, transcendentals=0
+            ),
+            name="qkv",
+        )(
+            z_arr, x_all, norm_gain[0:1], norm_shift[0:1], one, one, one, one, b_own, bias_own, *tables
+        )
+
+        input_rows = tokens.astype(f32).reshape(rows, width)
+        centre = input_rows - jnp.mean(input_rows, axis=-1, keepdims=True)
+        inv = lax.rsqrt(jnp.mean(centre * centre, axis=-1, keepdims=True) + norm_eps)
+        second = (centre * inv * norm_gain[1] + norm_shift[1]).astype(bf16)
+        a_up = a_all[:, 2 * rank :]
+        mid_up = nn(second, a_up).astype(bf16)
+        dmid_ff = (adapter_scale * nt(grad_low, b_ff)).astype(bf16)
+        g_pos = jnp.concatenate([g_all, g_all])
+        g_pos = lax.rev(g_pos, (0,))
+        g_pos = lax.dynamic_slice_in_dim(g_pos, lax.rem(n - 1 - z + n, n), n, 0)
+        g_pos = jnp.transpose(g_pos, (1, 0, 2, 3)).reshape(seqs, length, cz)
+
+        first_pos = jnp.transpose(first_all, (1, 0, 2, 3))
+        mid_pos = jnp.transpose(mid_all, (1, 0, 2, 3))
+        w_in = jnp.concatenate([one[:, :a_at], two], axis=1)
+        mid_up_t, dmid_ff_t, dmid_out_t = (
+            jnp.transpose(v.reshape(seqs, span, rank), (0, 2, 1)) for v in (mid_up, dmid_ff, dmid_out)
+        )
+
     pairs = cz // lanes
     steps = seqs * pairs
     inner_block = min(512, inner)
-    g_pos = jnp.concatenate([g_all, g_all])
-    g_pos = lax.rev(g_pos, (0,))
-    g_pos = lax.dynamic_slice_in_dim(g_pos, lax.rem(n - 1 - z + n, n), n, 0)
-    g_pos = jnp.transpose(g_pos, (1, 0, 2, 3)).reshape(seqs, length, cz)
-
     def one_buffer(shape):
         zeros = (0,) * len(shape)
         return pl.BlockSpec(shape, lambda s: zeros, pipeline_mode=pl.Buffered(1))
@@ -687,11 +1022,11 @@
         + [one_buffer((length, lanes))] * 3
         + [one_buffer((8, lanes))]
         + [one_buffer((rows, width))] * 2
-        + [one_buffer((rows, rank)), one_buffer((rank, rows))] * 2
+        + [one_buffer((rows, rank)), one_buffer((seqs, rank, span))] * 2
         + [
-            pl.BlockSpec((width, inner_block), lambda s: (0, inner_at(s))),
+            pl.BlockSpec((width, inner_block), lambda s: (0, 4 * width // inner_block + inner_at(s))),
             pl.BlockSpec((inner_block, width), lambda s: (inner_at(s), 0)),
-            pl.BlockSpec((inner_block, rank), lambda s: (inner_at(s), width // rank)),
+            pl.BlockSpec((inner_block, rank), lambda s: (inner_at(s), 0)),
             pl.BlockSpec((rank, inner_block), lambda s: (0, 4 * width // inner_block + inner_at(s))),
             pl.BlockSpec((1, inner_block), lambda s: (0, 4 * width // inner_block + inner_at(s))),
         ],
@@ -730,13 +1065,16 @@
         ),
         name="middle",
     )(
-        query, keys, values, g_pos, *tables, tables[0][:8], second, grad_low, mid_up, mid_up.T, dmid_ff, dmid_ff.T,
-        w_up, three, three, b_in, bias32.reshape(1, -1),
+        query, keys, values, g_pos, *tables, tables[0][:8], second, grad_low, mid_up, mid_up_t, dmid_ff, dmid_ff_t,
+        w_in, w_down, a_ff, b_in, bias32.reshape(1, -1),
     )
     grad_b_up = adapter_scale * grad_b_up
 
-    first_pos = jnp.transpose(first_all, (1, 0, 2, 3)).reshape(seqs * length, width)
-    mid_pos = jnp.transpose(mid_all, (1, 0, 2, 3)).reshape(seqs * length, rank)
+    first_pos = first_pos.reshape(seqs * length, width)
+    mid_pos = mid_pos.reshape(seqs * length, rank)
+    b_own = jnp.concatenate(
+        [lax.dynamic_slice_in_dim(b_in[:, t * width : (t + 1) * width], z * cz, cz, 1) for t in range(3)], axis=1
+    )
     djoint_own = [own[:, t].reshape(seqs * length, cz) for t in range(3)]
     dmid_own = sum(nt(djoint_own[t], b_own[:, t * cz : (t + 1) * cz]) for t in range(3))
     dmid_own = (adapter_scale * dmid_own).astype(bf16)
@@ -765,8 +1103,8 @@
             pl.BlockSpec((seqs, 4, span, cz), lambda t: (0, 0, 0, t)),
             pl.BlockSpec((cz, width), lambda t: (t, 3)),
             column(0, width), column(1, width), column(2, width),
-            pl.BlockSpec((cz, rank), lambda t: (t, a_at // rank + 1)),
-            fixed((width, rank), 0, a_at // rank),
+            pl.BlockSpec((cz, rank), lambda t: (t, 1)),
+            fixed((width, rank), 0, 0),
             fixed((rank, width), 0, 3),
             column(0, rank), column(1, rank), column(2, rank),
             fixed((1, width), 0, 3),
@@ -779,9 +1117,9 @@
             fixed((rank, width), 0, 0),
             fixed((rows, width), 0, 0),
             fixed((rows, rank), 0, 0),
-            fixed((width, rank), 0, a_at // rank + 2),
+            fixed((width, rank), 0, 2),
             fixed((2, width), 0, 0),
-            fixed((rank, rows), 0, 0),
+            fixed((seqs, rank, span), 0, 0, 0),
             fixed((rows, width), 0, 0),
         ],
         out_specs=[
@@ -807,9 +1145,9 @@
         compiler_params=pltpu.CompilerParams(vmem_limit_bytes=56 << 20),
         name="finish",
     )(
-        local, one, one, one, one, one, one, b_in, b_in, b_in, b_in, bias32.reshape(1, -1),
+        local, w_in, w_in, w_in, w_in, a_all, a_all, b_in, b_in, b_in, b_in, bias32.reshape(1, -1),
         tokens, cotangent, row_weight, ff, bias_ff.astype(f32).reshape(1, -1), mid_ff, b_ff,
-        grad_second, dmid_up, one, norm_gain, dmid_out.T, grad_low,
+        grad_second, dmid_up, a_all, norm_gain, dmid_out_t, grad_low,
     )
     grad_b_out = adapter_scale * grad_b_out
 

time: 521 us -> 461 us (0.88)
  Pallas kernels: 262 us -> 398 us
  waiting for transfers between devices: 76.9 us -> 0 us
  local copies, waits for them, and re-layouts: 76.7 us -> 26.3 us
  starting transfers between devices: 28.9 us -> 0 us
  other arithmetic: 33.2 us -> 14 us
  between operations: 15 us -> 1.65 us
  matrix products: 23.6 us -> 12.3 us
    pallas_call x1, Pallas kernels: 19.8 us -> 151 us  [body(): pl.pallas_call(functools.partial(front_kernel, n=n, depth=depth), in_spec...]
    ppermute x9 -> x0, waiting for transfers between devices: 76.2 us -> none  [the longest x3 72.1 us: body(): left = lax.ppermute(left, 'blk', [(i + 1, i) for i in range(n - 1)])]
    ppermute x9 -> x0, starting transfers between devices: 28.8 us -> none  [the longest x3 18.3 us: body(): right = lax.ppermute(right, 'blk', [(i, i + 1) for i in range(n - 1)])]
    unnamed x120 -> x73, local copies, waits for them, and re-layouts: 25.3 us -> 10.1 us
    transpose x4 -> x0, local copies, waits for them, and re-layouts: 10.4 us -> none  [the longest x1 6.58 us: body(): jnp.transpose(first_all, (1, 0, 2, 3)).reshape(seqs * length, width)]
    another operation x6 -> x0, other arithmetic: 10.3 us -> none  [the longest x4 8.39 us: body(): jnp.stack([tokens] + [jnp.where(z >= s, rights[s], lefts[n - s]) for s in...]
    another operation x9 -> x0, local copies, waits for them, and re-layouts: 8.75 us -> none
    dot_general x6 -> x2, matrix products: 9.76 us -> 3.72 us  [nt(): lax.dot_general(left, right, (((1,), (1,)), ((), ())), preferred_element_...]
  transfers between devices with their start and end apart: 12 -> 0, of which waited for: 4 -> 0; matrix products, arithmetic and copies ran while one was open for 18% -> 0% of each run, Pallas kernels for 4% -> 0%
where the time goes in v3:
time: 461 us; the launch traced here: 453 us
  Pallas kernels  398 us (86%)
  local copies, waits for them, and re-layouts  26.3 us (6%)
  other arithmetic  14 us (3%)
  matrix products  12.3 us (3%)
    pallas_call x1, Pallas kernels, body(): pl.pallas_call(functools.partial(front_kernel, n=n, depth=depth), in_spec...  151 us
    pallas_call x1, Pallas kernels, body(): pl.pallas_call(functools.partial(middle_kernel, n=n, pairs=pairs, steps=s...  150 us
    pallas_call x1, Pallas kernels, body(): pl.pallas_call(functools.partial(reduce_kernel, n=n, chunks=chunks, b_at=...  65.1 us
    pallas_call x1, Pallas kernels, body(): pl.pallas_call(finish_kernel, grid=(n,), in_specs=[pl.BlockSpec((seqs, 4,...  23.2 us
    unnamed x73, local copies, waits for them, and re-layouts  10.1 us

profile of v3, /device:TPU:0, one launch (start us, length us, event | category | flops | bytes accessed | tf_op | source)
XLA Modules:
  0.0 452.6 jit_solution(3246597190956014394)
XLA Ops:
  0.7 1.3 reshape.101
  2.0 0.8 select_reduce_fusion
  2.8 0.9 copy.76
  3.7 1.8 convert_element_type.51.b_ref
  5.5 1.6 convert_element_type.50.aff_ref
  7.1 1.6 convert_element_type.49.a_ref
  8.7 1.5 convert_element_type.52.bff_ref
  10.2 151.1 %front.1 = (bf16[1024,8192]{1,0:T(8,128)(2,1)}, bf16[4096,1024]{1,0:T(8,128)(2,1)}, bf16[1024,384]{1,0:T(8,128)(2,1)}, bf16[4096,128]{1,0:T(8,128)(2,1)}, bf16[1...) custom-call(bf16[3,256,1024]{2,1,0:T(8,128)(2,1)} %x_ref.1, ...), custom_call_target="tpu_custom_call" | custom-call | tf_op jit(solution)/shard_map/front/pallas_call | solution.py:842
  161.3 1.3 slice.27.mid_qkv_t_ref
  162.5 150.3 %middle.1 = (bf16[3,4,256,1024]{3,2,1,0:T(8,128)(2,1)}, bf16[3,3,1024,256]{3,2,1,0:T(8,128)(2,1)}, f32[768,1024]{1,0:T(8,128)}, f32[768,1024]{1,0:T(8,128)}, bf1...) custom-call(bf16[3,1024,256]{2,1,0:T(8,128)(2,1)} %get-tuple-element.70.q_ref, ...), custom_call_target="tpu_custom_call" | custom-call | tf_op jit(solution)/shard_map/middle/pallas_call | solution.py:1018
  312.9 2.7 fusion.21
  315.6 0.5 convolution_multiply_fusion.1
  316.1 0.1 broadcast_in_dim.63
  316.2 0.5 convolution_multiply_fusion.2
  316.8 0.7 copy.78
  317.6 0.5 convolution_multiply_fusion.3
  318.1 0.1 broadcast_in_dim.58
  318.1 0.7 copy.77
  318.9 0.1 broadcast_in_dim.55
  319.0 1.0 fusion.7
  320.0 1.0 fusion.8
  321.1 0.6 reshape.103
  321.7 23.2 %finish.1 = (bf16[3,256,1024]{2,1,0:T(8,128)(2,1)}, bf16[3,256,1024]{2,1,0:T(8,128)(2,1)}, f32[4,1024]{1,0:T(4,128)}, f32[128,1024]{1,0:T(8,128)}, f32[128,1024]{1,0:T(8,128)}) custom-call(bf16[3,4,256,1024]{3,2,1,0:T(8,128)(2,1)} %get-tuple-element.87.local_ref, bf16[1024,8192]{1,0:T(8,128)(2,1)} %get-tuple-element.83.up_ref.wo_ref.wq_ref.wk_ref.wv_ref, ...), custom_call_target="tpu_custom_call" | custom-call | tf_op jit(solution)/shard_map/finish/pallas_call | solution.py:1099
  344.9 1.2 fusion.10
  346.1 0.1 fusion.6
  346.2 0.2 copy-done.22
  346.4 1.2 fusion.5
  347.6 2.0 fusion.22
  349.6 2.0 fusion.14
  351.6 1.8 convolution_add_fusion.1
  353.3 9.0 %copy.63 = bf16[1024,3072]{1,0:T(8,128)(2,1)} copy(bf16[1024,3072]{0,1:T(8,128)(2,1)} %bitcast.70) | data formatting | bytes 12582912 | tf_op jit(solution)/shard_map/dot_general | solution.py:36
  362.3 5.5 %convolution_convert_fusion.1 = bf16[128,8,128]{0,2,1:T(8,128)(2,1)S(1)} fusion(bf16[8,128,3072]{2,1,0:T(8,128)(2,1)} %bitcast.60, f32[3072,128]{1,0:T(8,128)S(1)} %copy-done.23, bf16[3072,256]{1,0:T(8,128)(2,1)S(1)} %bitcast.62, bf16[128,1024]{1,0:T(8,128)(2,1)} %get-tuple-element.125, s32[]{:T(128)S(6)} %select_n.18), kind=kOutput, calls=%fused_computation.10 | convolution fusion | flops 1007943680 | bytes 9764868 | tf_op jit(solution)/shard_map/dot_general | solution.py:36
  367.8 0.2 copy.64
  368.0 0.1 constant_dynamic-update-slice_fusion
  368.0 1.3 bitcast_dynamic-update-slice_fusion.4
  369.3 1.1 bitcast_dynamic-update-slice_fusion.3
  370.4 0.1 convert_element_type.59
  370.6 0.1 bitcast_dynamic-update-slice_fusion.1
  370.7 1.3 copy-done.26
  372.0 0.2 bitcast_dynamic-update-slice_fusion
  372.2 1.2 copy-done.20
  373.5 0.4 fusion.4
  373.9 0.1 bitcast_dynamic-update-slice_fusion.2
  374.0 2.0 copy-done.24
  376.2 65.1 %reduce.1 = (bf16[128,2048]{1,0:T(8,128)(2,1)S(1)}, f32[4,1024]{1,0:T(4,128)S(1)}, bf16[8,128,1152]{2,1,0:T(8,128)(2,1)S(1)}) custom-call(bf16[4,2,128,2048]{3,2,1,0:T(8,128)(2,1)} %bitcast.71, f32[4,1024]{1,0:T(4,128)S(1)} %copy-done.18, f32[128,1024]{1,0:T(8,128)S(1)} %copy-done, f32[128,1024]{1,0:T(8,128)S(1)} %copy-done.3, f32[128,1024]{1,0:T(8,128)S(1)} %copy-done.4, ...), custom_call_target="tpu_custom_call" | custom-call | tf_op jit(solution)/shard_map/reduce/pallas_call | solution.py:1170
  441.3 1.4 copy-done.2
  442.7 8.8 %update.1 = (f32[128,384]{1,0:T(8,128)}, f32[512,128]{1,0:T(8,128)}, f32[128,1024]{1,0:T(8,128)}, f32[128,128]{1,0:T(8,128)}, f32[128,384]{1,0:T(8,128)}, /*inde...) custom-call(bf16[128,2048]{1,0:T(8,128)(2,1)S(1)} %get-tuple-element, ...), custom_call_target="tpu_custom_call" | custom-call | tf_op jit(solution)/shard_map/update/pallas_call | solution.py:1241
  451.6 0.6 fusion.23
  (65 shorter events, 0.3 us)
Async XLA Ops:
  312.9 2.8 copy-start.21
  315.6 2.0 copy-start.19
  317.6 3.5 copy-start.31
  321.7 24.4 %copy-start.28 = (f32[128,4096]{1,0:T(8,128)S(1)}, f32[128,4096]{1,0:T(8,128)}, u32[]{:S(2)}) copy-start(f32[128,4096]{1,0:T(8,128)} %get-tuple-element.103) | copy-start | bytes 6291460
  344.8 1.6 copy-start.22
  344.8 1.6 copy-start.30
  346.2 1.4 copy-start.25
  353.3 9.0 %copy-start.23 = (f32[3072,128]{1,0:T(8,128)S(1)}, f32[3072,128]{1,0:T(8,128)}, u32[]{:S(2)}) copy-start(f32[3072,128]{1,0:T(8,128)} %convolution_add_fusion.1) | copy-start | bytes 4718596
  367.8 2.6 copy-start.27
  370.4 1.6 copy-start.26
  372.0 1.4 copy-start.20
  372.0 1.4 copy-start.29
  373.4 2.6 copy-start
  373.4 2.6 copy-start.3
  373.4 2.6 copy-start.4
  373.4 2.6 copy-start.7
  373.4 2.6 copy-start.9
  373.5 2.6 copy-start.10
  373.5 2.6 copy-start.18
  374.0 2.0 copy-start.24
  376.0 66.6 %copy-start.1 = (bf16[512,1024]{1,0:T(8,128)(2,1)S(1)}, bf16[512,1024]{1,0:T(8,128)(2,1)}, u32[]{:S(2)}) copy-start(bf16[512,1024]{1,0:T(8,128)(2,1)} %wd_ref.1) | copy-start | bytes 3145732
  376.0 66.6 %copy-start.5 = (f32[512,128]{1,0:T(8,128)S(1)}, f32[512,128]{1,0:T(8,128)}, u32[]{:S(2)}) copy-start(f32[512,128]{1,0:T(8,128)} %refs_4_.1) | copy-start | bytes 786436
  376.1 66.6 %copy-start.6 = (f32[128,384]{1,0:T(8,128)S(1)}, f32[128,384]{1,0:T(8,128)}, u32[]{:S(2)}) copy-start(f32[128,384]{1,0:T(8,128)} %refs_0_.1) | copy-start | bytes 589828
  376.1 66.6 %copy-start.8 = (s32[128,1024]{1,0:T(8,128)S(1)}, s32[128,1024]{1,0:T(8,128)}, u32[]{:S(2)}) copy-start(s32[128,1024]{1,0:T(8,128)} %refs_11_.1) | copy-start | bytes 1572868
  376.1 66.6 %copy-start.11 = (f32[512,128]{1,0:T(8,128)S(1)}, f32[512,128]{1,0:T(8,128)}, u32[]{:S(2)}) copy-start(f32[512,128]{1,0:T(8,128)} %refs_5_.1) | copy-start | bytes 786436
  376.1 66.6 %copy-start.12 = (f32[512,128]{1,0:T(8,128)S(1)}, f32[512,128]{1,0:T(8,128)}, u32[]{:S(2)}) copy-start(f32[512,128]{1,0:T(8,128)} %refs_6_.1) | copy-start | bytes 786436
  376.1 66.6 %copy-start.13 = (s32[512,128]{1,0:T(8,128)S(1)}, s32[512,128]{1,0:T(8,128)}, u32[]{:S(2)}) copy-start(s32[512,128]{1,0:T(8,128)} %refs_7_.1) | copy-start | bytes 786436
  376.1 66.6 %copy-start.14 = (f32[128,384]{1,0:T(8,128)S(1)}, f32[128,384]{1,0:T(8,128)}, u32[]{:S(2)}) copy-start(f32[128,384]{1,0:T(8,128)} %refs_1_.1) | copy-start | bytes 589828
  376.1 66.6 %copy-start.15 = (f32[128,384]{1,0:T(8,128)S(1)}, f32[128,384]{1,0:T(8,128)}, u32[]{:S(2)}) copy-start(f32[128,384]{1,0:T(8,128)} %refs_2_.1) | copy-start | bytes 589828
  376.1 66.6 %copy-start.16 = (s32[128,384]{1,0:T(8,128)S(1)}, s32[128,384]{1,0:T(8,128)}, u32[]{:S(2)}) copy-start(s32[128,384]{1,0:T(8,128)} %refs_3_.1) | copy-start | bytes 589828
  376.2 66.6 %copy-start.17 = (s32[128,128]{1,0:T(8,128)S(1)}, s32[128,128]{1,0:T(8,128)}, u32[]{:S(2)}) copy-start(s32[128,128]{1,0:T(8,128)} %refs_15_.1) | copy-start | bytes 196612
  441.2 1.4 copy-start.2

commit v4 on v3

--- a/solution.py
+++ b/solution.py
@@ -92,28 +92,34 @@
     span = keys.shape[0] // blocks
     scale = 1.0 / math.sqrt(depth)
     lane = lax.broadcasted_iota(jnp.int32, (1, lanes), 1)
-    masks = [jnp.where(lane // depth == h, 1.0, 0.0).astype(bf16) for h in range(lanes // depth)]
+    heads = lanes // depth
+    masks = [jnp.where(lane // depth == h, 1.0, 0.0).astype(bf16) for h in range(heads)]
+    scaled = [jnp.where(lane // depth == h, scale, 0.0).astype(bf16) for h in range(heads)]
     diagonal = lax.broadcasted_iota(jnp.int32, (span, span), 0) <= lax.broadcasted_iota(
         jnp.int32, (span, span), 1
     )
     keys_t, values_t = keys.T, values.T
-    dk_ref[...] = jnp.zeros_like(dk_ref)
-    dv_ref[...] = jnp.zeros_like(dv_ref)
     for i in range(blocks):
-        rows = slice(i * span, (i + 1) * span)
-        end = (i + 1) * span
+        done, end = i * span, (i + 1) * span
+        rows = slice(done, end)
         q_i, g_i = query[rows], grad[rows]
         g_t = g_i.T
-        outs, grads = [], []
-        dk, dv = None, None
-        for h, mask in enumerate(masks):
+        outs, grads, lows, grads_s, q_parts, g_parts = [], [], [], [], [], []
+        for h in range(heads):
             part = slice(h * depth, (h + 1) * depth)
-            q_h, g_h = q_i * mask, g_i * mask
-            scores = nt(keys[:end], q_h) * scale
-            last = jnp.where(diagonal, scores[i * span :], masked_score)
-            scores = last if i == 0 else jnp.concatenate([scores[: i * span], last], axis=0)
-            weights = jnp.exp(scores - jnp.max(scores, axis=0, keepdims=True))
-            weights = weights * (1.0 / jnp.sum(weights, axis=0, keepdims=True))
+            q_h, g_h = q_i * scaled[h], g_i * masks[h]
+            last = jnp.where(diagonal, nt(keys[rows], q_h), masked_score)
+            top = jnp.max(last, axis=0, keepdims=True)
+            if i:
+                scores = nt(keys[:done], q_h)
+                top = jnp.maximum(top, jnp.max(scores, axis=0, keepdims=True))
+            weights = jnp.exp(last - top)
+            total = jnp.sum(weights, axis=0, keepdims=True)
+            if i:
+                before = jnp.exp(scores - top)
+                total += jnp.sum(before, axis=0, keepdims=True)
+                weights = jnp.concatenate([before, weights], axis=0)
+            weights = weights * (1.0 / total)
             low = weights.astype(bf16)
             out_t = nn(values_t[part, :end], low)
             grad_p = nt(values[:end], g_h)
@@ -121,18 +127,23 @@
             grad_s = (weights * (grad_p - delta)).astype(bf16)
             outs.append(out_t)
             grads.append(nn(keys_t[part, :end], grad_s))
-            dk_h, dv_h = nn(grad_s, q_h), nn(low, g_h)
-            dk = dk_h if dk is None else dk + dk_h
-            dv = dv_h if dv is None else dv + dv_h
-        dk_ref[:end] += dk
-        dv_ref[:end] += dv
+            lows.append(low)
+            grads_s.append(grad_s)
+            q_parts.append(q_h)
+            g_parts.append(g_h)
+        dk = nn(jnp.concatenate(grads_s, axis=1), jnp.concatenate(q_parts, axis=0))
+        dv = nn(jnp.concatenate(lows, axis=1), jnp.concatenate(g_parts, axis=0))
+        if i:
+            dk_ref[:done] += dk[:done]
+            dv_ref[:done] += dv[:done]
+        dk_ref[rows] = dk[done:]
+        dv_ref[rows] = dv[done:]
         store(i, 0, jnp.concatenate(outs, axis=0).T.astype(bf16))
         dq = jnp.concatenate(grads, axis=0).T * scale
         store(i, 1, turn(dq, *[t[rows] for t in tables], -1.0).astype(bf16))
     for i in range(blocks):
         rows = slice(i * span, (i + 1) * span)
-        dk = dk_ref[rows] * scale
-        store(i, 2, turn(dk, *[t[rows] for t in tables], -1.0).astype(bf16))
+        store(i, 2, turn(dk_ref[rows], *[t[rows] for t in tables], -1.0).astype(bf16))
         store(i, 3, dv_ref[rows].astype(bf16))
 
 
@@ -142,13 +153,13 @@
 
 
 def front_kernel(
-    tokens_ref, win_ref, wdown_ref, a_ref, aff_ref, b_ref, bff_ref,
-    cot_ref, weight_ref, gain_ref, shift_ref, bias_ref, freq_ref,
+    tokens_ref, win_ref, wdown_ref, a_wide, aff_wide, b_wide, bff_wide,
+    cot_ref, ids_ref, domain_ref, gain_ref, shift_ref, bias_ref, freq_ref,
     win_out, wdown_out, a_out, aff_out, b_out, bff_out,
     q_out, k_out, v_out, first_out, mid_out, g_out,
     low_ref, second_ref, mid_up_ref, mid_up_t_ref, dmid_ff_ref, dmid_ff_t_ref, dmid_out_t_ref,
-    keep_ref, above_ref, below_ref,
-    x_all, q_s, k_s, v_s, first_s, mid_s, ga, wout_v, wqkv_v, a_v, b_v, bff_v,
+    keep_ref, above_ref, below_ref, weight_ref,
+    a_ref, aff_ref, b_ref, bff_ref, x_all, q_s, k_s, v_s, first_s, mid_s, ga, wout_v, wqkv_v, a_v, b_v, bff_v,
     sx, qx, own_sem, sr, qr, sl, ql, sd, qd, load_sem, store_sem, token_sem,
     *, n, depth,
 ):
@@ -257,6 +268,8 @@
         pl.when((z < n - 1) & (z - s + 1 >= 0))(lambda: rightward(s).wait_send())
         pl.when((z > 0) & (z + s - 1 < n))(lambda: leftward(s).wait_send())
 
+    for low, values in ((a_ref, a_wide), (aff_ref, aff_wide), (b_ref, b_wide), (bff_ref, bff_wide)):
+        low[...] = values[...].astype(bf16)
     token_copy = pltpu.make_async_copy(tokens_ref, x_all.at[z], token_sem.at[0])
     token_copy.start()
     start_own(0)
@@ -275,7 +288,13 @@
         below_ref[rows] = jnp.where((unit_lane >= half) & (unit_lane < ROTARY), sine, 0.0)
     for q in range(seqs):
         part = slice(q * span, (q + 1) * span)
-        low_ref[part] = (cot_ref[q].astype(f32) * weight_ref[part]).astype(bf16)
+        ids = ids_ref[q : q + 1, :]
+        found = jnp.zeros((1, span), f32)
+        for k in range(DOMAINS):
+            found = jnp.where(ids == k, domain_ref[k], found)
+        weight = jnp.broadcast_to(found, (8, span)).T[:, :1]
+        weight_ref[part] = weight
+        low_ref[part] = (cot_ref[q].astype(f32) * weight).astype(bf16)
         unit = normal(x_all[z, q].astype(f32))
         second_ref[part] = (unit * gain_ref[1:2] + shift_ref[1:2]).astype(bf16)
 
@@ -407,18 +426,131 @@
             copy.wait()
 
 
+def remote(src, dst, send, recv, peer):
+    return pltpu.make_async_remote_copy(
+        src_ref=src, dst_ref=dst, send_sem=send, recv_sem=recv, device_id=peer, device_id_type=MESH
+    )
+
+
+def add_low(a, b):
+    return (a.astype(f32) + b.astype(f32)).astype(bf16)
+
+
+def plane():
+    dp, z = lax.axis_index("dp"), lax.axis_index("blk")
+    y, x, c = dp // 4, lax.rem(dp // 2, 2), lax.rem(dp, 2)
+    return dp, z, y, x, c, (dp + 1 - 2 * c, z), (dp + 2 - 4 * x, z), (dp + 4 - 8 * y, z)
+
+
+def greet(peers):
+    barrier = pltpu.get_barrier_semaphore()
+    for peer in peers:
+        pl.semaphore_signal(barrier, inc=1, device_id=peer, device_id_type=MESH)
+    pl.semaphore_wait(barrier, len(peers))
+
+
+early_cuts = ((0, 512), (512, 1024), (1024, 1536), (1536, 1920))
+late_end, a_ff_at, b_at_col, early_end = 256, 384, 896, 1920
+
+
+class PlaneSum:
+    def __init__(self, e, r1, r2a, r2b, r3a, r3b, s1, q1, s2, q2, s3, q3):
+        self.refs = e, r1, r2a, r2b, r3a, r3b
+        self.sems = s1, q1, s2, q2, s3, q3
+        self.at = plane()
+        self.half = e.shape[3] // 2
+
+    def first(self, m):
+        e, r1 = self.refs[:2]
+        c, core = self.at[4], self.at[5]
+        s1, q1 = self.sems[:2]
+        if m < 4:
+            cut = slice(late_end, early_end)
+            return remote(e.at[m // 2, m % 2, 1 - c, :, cut], r1.at[m // 2, m % 2, :, cut], s1.at[m], q1.at[m], core)
+        cut = slice(0, late_end)
+        return remote(e.at[:, :, 1 - c, :, cut], r1.at[:, :, :, cut], s1.at[m], q1.at[m], core)
+
+    def take_first(self, m):
+        e, r1 = self.refs[:2]
+        c = self.at[4]
+        self.first(m).wait()
+        for i in (m,) if m < 4 else range(4):
+            yy, xx = i // 2, i % 2
+            cut = slice(late_end, early_end) if m < 4 else slice(0, late_end)
+            e[yy, xx, c, :, cut] = add_low(e[yy, xx, c, :, cut], r1[yy, xx, :, cut])
+
+    def finish(self, out):
+        e, r1, r2a, r2b, r3a, r3b = self.refs
+        dp, z, y, x, c, core, along_x, along_y = self.at
+        s1, q1, s2, q2, s3, q3 = self.sems
+        half = self.half
+
+        def second(k):
+            cut = slice(*early_cuts[k])
+            return [
+                remote(e.at[:, 1 - x, c, 0:half, cut], r2a.at[:, :, cut], s2.at[0, k], q2.at[0, k], along_x),
+                remote(e.at[1 - y, :, c, half:, cut], r2b.at[:, :, cut], s2.at[1, k], q2.at[1, k], along_y),
+            ]
+
+        def third(k):
+            cut = slice(*early_cuts[k])
+            return [
+                remote(e.at[1 - y, x, c, 0:half, cut], r3a.at[:, cut], s3.at[0, k], q3.at[0, k], along_y),
+                remote(e.at[y, 1 - x, c, half:, cut], r3b.at[:, cut], s3.at[1, k], q3.at[1, k], along_x),
+            ]
+
+        def after_second(k):
+            cut = slice(*early_cuts[k])
+            for copy in second(k):
+                copy.wait()
+            for i in range(2):
+                e[i, x, c, 0:half, cut] = add_low(e[i, x, c, 0:half, cut], r2a[i, :, cut])
+                e[y, i, c, half:, cut] = add_low(e[y, i, c, half:, cut], r2b[i, :, cut])
+            for copy in third(k):
+                copy.start()
+
+        def after_third(k):
+            cut = slice(*early_cuts[k])
+            for copy in third(k):
+                copy.wait()
+            out[0:half, cut] = add_low(e[y, x, c, 0:half, cut], r3a[:, cut])
+            out[half:, cut] = add_low(e[y, x, c, half:, cut], r3b[:, cut])
+
+        count = len(early_cuts)
+        for k in range(count):
+            for copy in second(k):
+                copy.start()
+        for k in range(count + 1):
+            if k < count:
+                after_second(k)
+            if k:
+                after_third(k - 1)
+
+
 def middle_kernel(
-    q_ref, k_ref, v_ref, g_ref, keep_ref, above_ref, below_ref, mid_qkv_t_ref,
+    q_ref, k_ref, v_ref, g_ref, keep_ref, above_ref, below_ref,
     second_ref, low_ref, mid_ref, mid_t_ref, dmid_ref, dmid_t_ref,
-    up_ref, down_ref, a_ref, b_ref, bias_ref,
-    local_ref, own_ref, ff_ref, back_ref, mid_ff_ref, dmid_up_ref, ga_ref, gb_ref,
-    buffer, dk_ref, dv_ref, mid_acc, dmid_acc, send_sem, recv_sem, own_sem,
-    *, n, pairs, steps, depth,
+    up_ref, down_ref, a_ref, b_ref, bias_ref, *refs,
+    n, pairs, steps, depth, early,
 ):
+    if early:
+        first_ref, mid_qkv_ref, local_ref, ff_ref, back_ref, mid_ff_ref, dmid_up_ref, sum_ref = refs[:8]
+        buffer, dk_ref, dv_ref, mid_acc, dmid_acc, send_sem, recv_sem, own_sem = refs[8:16]
+        e_ref, dmid_seq, gb_acc, ga_acc = refs[16:20]
+        plane_refs = refs[20:]
+    else:
+        local_ref, own_ref, ff_ref, back_ref, mid_ff_ref, dmid_up_ref, ga_ref, gb_ref = refs[:8]
+        buffer, dk_ref, dv_ref, mid_acc, dmid_acc, send_sem, recv_sem, own_sem = refs[8:]
     step = pl.program_id(0)
     z = lax.axis_index("blk")
     dp = lax.axis_index("dp")
     lanes = q_ref.shape[2]
+    length = q_ref.shape[1]
+    inner_block = up_ref.shape[1]
+    width = up_ref.shape[0]
+    cz = pairs * lanes
+    if early:
+        plane_sum = PlaneSum(e_ref, *plane_refs)
 
     def copies(s):
         seq, pair = s // pairs, lax.rem(s, pairs)
@@ -429,26 +561,20 @@
         for t in range(1, n):
             peer = lax.rem(z + t, n)
             away.append(
-                pltpu.make_async_remote_copy(
-                    src_ref=buffer.at[s, peer], dst_ref=target,
-                    send_sem=send_sem.at[s, t], recv_sem=recv_sem.at[s, t],
-                    device_id=(dp, peer), device_id_type=MESH,
-                )
+                remote(buffer.at[s, peer], target, send_sem.at[s, t], recv_sem.at[s, t], (dp, peer))
             )
         return own, away
 
     @pl.when(step == 0)
     def _():
-        barrier = pltpu.get_barrier_semaphore()
-        for t in range(1, n):
-            pl.semaphore_signal(barrier, inc=1, device_id=(dp, lax.rem(z + t, n)), device_id_type=MESH)
-        pl.semaphore_wait(barrier, n - 1)
+        peers = [(dp, lax.rem(z + t, n)) for t in range(1, n)]
+        greet((list(plane()[5:]) if early else []) + peers)
 
     @pl.when(step < steps)
     def _():
         def store(i, kind, value):
             buffer[step, i, kind] = value
-            if kind:
+            if kind and not early:
                 own_ref[0, kind - 1, i * value.shape[0] : (i + 1) * value.shape[0], :] = value
 
         tables = keep_ref[...], above_ref[...], below_ref[...]
@@ -457,6 +583,23 @@
         own.start()
         for copy in away:
             copy.start()
+        if early:
+            seq, pair = step // pairs, lax.rem(step, pairs)
+            mid_t = mid_qkv_ref[0].T
+            dmid = jnp.zeros((length, lanes), f32)
+            for t in range(3):
+                grad = buffer[step, :, t + 1].reshape(length, lanes)
+                at = pl.ds(pl.multiple_of(t * width + z * cz + pair * lanes, lanes), lanes)
+                dmid += nt(grad, b_ref[:, at])
+                product = nn(mid_t, grad)
+                gb_acc[t, pair] = jnp.where(seq == 0, product, gb_acc[t, pair] + product)
+            dmid = jnp.where(pair == 0, dmid, dmid_seq[...] + dmid)
+            dmid_seq[...] = dmid
+
+            @pl.when(pair == pairs - 1)
+            def _():
+                product = nn((adapter_scale * dmid_seq[...]).astype(bf16).T, first_ref[0])
+                ga_acc[...] = jnp.where(seq == 0, product, ga_acc[...] + product)
 
     @pl.when(step == steps)
     def _():
@@ -464,13 +607,31 @@
         back_ref[...] = jnp.zeros_like(back_ref)
         mid_acc[...] = jnp.zeros_like(mid_acc)
         dmid_acc[...] = jnp.zeros_like(dmid_acc)
+        if early:
+            for owner in range(8):
+                place = (owner // 4, owner // 2 % 2, owner % 2)
+                e_ref[place + (slice(None), slice(late_end, a_ff_at))] = ga_acc[
+                    :, owner * lanes : (owner + 1) * lanes
+                ].astype(bf16)
+                if owner < 4:
+                    e_ref[place + (slice(None), slice(b_at_col, early_end))] = jnp.zeros((lanes, 1024), bf16)
+            for t in range(3):
+                for pair in range(pairs):
+                    at = pl.ds(pl.multiple_of(b_at_col + z * cz + pair * lanes, lanes), lanes)
+                    e_ref[0, t // 2, t % 2, :, at] = (adapter_scale * gb_acc[t, pair]).astype(bf16)
 
     @pl.when(step >= steps)
     def _():
         count, size = mid_t_ref.shape[0], mid_t_ref.shape[2]
+        j = step - steps
+        if early:
+            up_b = b_ref[:, pl.ds(pl.multiple_of(4 * width + j * inner_block, inner_block), inner_block)]
+        else:
+            up_b = b_ref[...]
+        ga, gb = None, None
         for at in range(count):
             rows = slice(at * size, (at + 1) * size)
-            pre = nn(second_ref[rows], up_ref[...]) + bias_ref[...] + adapter_scale * nn(mid_ref[rows], b_ref[...])
+            pre = nn(second_ref[rows], up_ref[...]) + bias_ref[...] + adapter_scale * nn(mid_ref[rows], up_b)
             cdf = 0.5 + 0.5 * lax.erf(pre * (1.0 / math.sqrt(2.0)))
             hidden = (pre * cdf).astype(bf16)
             slope = cdf + pre * (jnp.exp(-0.5 * pre * pre) * (1.0 / math.sqrt(2.0 * math.pi)))
@@ -479,16 +640,49 @@
             ff_ref[rows] += nn(hidden, down_ref[...])
             back_ref[rows] += nt(dup, up_ref[...])
             mid_acc[rows] += nn(hidden, a_ref[...])
-            dmid_acc[rows] += nt(dup, b_ref[...])
-            ga = nn(dmid_t_ref[at], hidden)
-            gb = nn(mid_t_ref[at], dup)
-            ga_ref[...] = ga if at == 0 else ga_ref[...] + ga
-            gb_ref[...] = gb if at == 0 else gb_ref[...] + gb
+            dmid_acc[rows] += nt(dup, up_b)
+            ga_part = nn(dmid_t_ref[at], hidden)
+            gb_part = nn(mid_t_ref[at], dup)
+            ga = ga_part if ga is None else ga + ga_part
+            gb = gb_part if gb is None else gb + gb_part
+        if early:
+            e_ref[j // 4, lax.rem(j // 2, 2), lax.rem(j, 2), :, a_ff_at:b_at_col] = ga.astype(bf16)
+            at = pl.ds(pl.multiple_of(b_at_col + lax.rem(j, 2) * inner_block, lanes), inner_block)
+            e_ref[1, j // 4, lax.rem(j // 2, 2), :, at] = (adapter_scale * gb).astype(bf16)
+            for m in range(3):
+
+                @pl.when(j == 2 * m + 3)
+                def _(m=m):
+                    plane_sum.take_first(m)
+
+            for m in range(4):
+                pl.when(j == 2 * m + 1)(lambda m=m: plane_sum.first(m).start())
+        else:
+            ga_ref[...] = ga
+            gb_ref[...] = gb
 
     @pl.when(step == pl.num_programs(0) - 1)
     def _():
         mid_ff_ref[...] = mid_acc[...].astype(bf16)
         dmid_up_ref[...] = (adapter_scale * dmid_acc[...]).astype(bf16)
+        if early:
+            count, size = mid_t_ref.shape[0], mid_t_ref.shape[2]
+            ga, gb = None, None
+            for at in range(count):
+                rows = slice(at * size, (at + 1) * size)
+                ga_part = nn(dmid_up_ref[rows].T, second_ref[rows])
+                gb_part = nn(mid_ff_ref[rows].T, low_ref[rows])
+                ga = ga_part if ga is None else ga + ga_part
+                gb = gb_part if gb is None else gb + gb_part
+            for owner in range(8):
+                place = (owner // 4, owner // 2 % 2, owner % 2, slice(None))
+                at = slice(owner * lanes, (owner + 1) * lanes)
+                e_ref[place + (slice(0, lanes),)] = ga[:, at].astype(bf16)
+                e_ref[place + (slice(lanes, late_end),)] = (adapter_scale * gb[:, at]).astype(bf16)
+            plane_sum.first(4).start()
+            plane_sum.take_first(3)
+            plane_sum.take_first(4)
+            plane_sum.finish(sum_ref)
         for s in range(steps):
             own, away = copies(s)
             own.wait()
@@ -554,175 +748,279 @@
         norm_ref[...] = jnp.concatenate(norm, axis=0)
 
 
-def reduce_kernel(
-    g_ref, norm_in_ref, b_ref, mean_ref, square_ref, bf_ref, mean_f_ref, square_f_ref,
-    out_ref, norm_ref, fresh_ref,
-    r1, h, r2a, r2b, ia, ib, r3a, r3b, total, r4, nr, nsum,
-    s1, q1, s2, q2, s3, q3, s4, q4, s5, q5, sn, qn, sg, qg,
-    *, n, chunks, b_at,
+def tail_kernel(
+    o_ref, dq_ref, dk_ref, dv_ref, wo_ref, wq_ref, wk_ref, wv_ref, a_out_ref, a_qkv_ref, b_out_ref,
+    bq_ref, bk_ref, bv_ref, bias_ref, x_ref, cot_ref, weight_ref, ff_ref, bias_ff_ref, mid_ff_ref, b_ff_ref,
+    second_ref, dmid_up_ref, a_up_ref, gain_ref, dmid_out_t_ref, low_ref,
+    e_ref, b_ref, mean_ref, square_ref, bf_ref, mean_f_ref, square_f_ref,
+    mixed_ref, tokens_ref, out_hbm, norm_ref, fresh_hbm,
+    out_ref, fresh_ref, att_acc, mid_acc, first_acc, dmid_acc,
+    r4, la, lb, lr1, lr2, lr3, lbr, lj, lr4, lbr4, lbt, nr, nsum,
+    s4, q4, s5, q5, sl, ql, sl4, ql4, sl5, ql5, sn, qn, sg, qg, done_sem,
+    *, n,
 ):
-    z = lax.axis_index("blk")
-    dp = lax.axis_index("dp")
-    y, x, c = dp // 4, lax.rem(dp // 2, 2), lax.rem(dp, 2)
-    core = (dp + 1 - 2 * c, z)
-    along_x = (dp + 2 - 4 * x, z)
-    along_y = (dp + 4 - 8 * y, z)
+    step = pl.program_id(0)
+    dp, z, y, x, c, core, along_x, along_y = plane()
     peers = [(dp, lax.rem(z + t, n)) for t in range(1, n)]
-    half = g_ref.shape[2] // 2
-    part = g_ref.shape[2] // n
-    width = g_ref.shape[3] // chunks
-
-    barrier = pltpu.get_barrier_semaphore()
-    for peer in [core, along_x, along_y] + peers:
-        pl.semaphore_signal(barrier, inc=1, device_id=peer, device_id_type=MESH)
-    pl.semaphore_wait(barrier, 2 + n)
-
-    def remote(src, dst, send, recv, peer):
-        return pltpu.make_async_remote_copy(
-            src_ref=src, dst_ref=dst, send_sem=send, recv_sem=recv, device_id=peer, device_id_type=MESH
+    seqs, size, width = x_ref.shape
+    rows, cols = seqs * size, o_ref.shape[3]
+    rank = e_ref.shape[0]
+    part = rank // n
+    lanes = 128
+    mine = pl.ds(pl.multiple_of(z * part, part), part)
+    late = slice(early_end, early_end + lanes)
+
+    def to_part(t):
+        return pl.ds(pl.multiple_of(lax.rem(z + t, n) * part, part), part)
+
+    def e_out(k, t):
+        cut = slice(*early_cuts[k])
+        return remote(e_ref.at[to_part(t), cut], r4.at[t, :, cut], s4.at[t, k], q4.at[t, k], peers[t - 1])
+
+    def e_back(k, t):
+        cut = slice(*early_cuts[k])
+        return remote(out_ref.at[mine, cut], out_ref.at[mine, cut], s5.at[t, k], q5.at[t, k], peers[t - 1])
+
+    count = len(early_cuts)
+
+    has_b = (c == 1, (c == 1) & (x == 1), dp == 3)
+    gives_b = (c == 0, (c == 1) & (x == 0), (c == 1) & (x == 1) & (y == 1))
+
+    def late_a(i):
+        src, dst, peer = [
+            (la.at[:, :, 1 - c], lr1, core),
+            (la.at[:, 1 - x, c], lr2, along_x),
+            (la.at[1 - y, x, c], lr3, along_y),
+        ][i]
+        return remote(src, dst, sl.at[0, i], ql.at[0, i], peer)
+
+    def late_b(i):
+        return remote(lb, lbr.at[i], sl.at[1, i], ql.at[1, i], (core, along_x, along_y)[i])
+
+    def late_start(i):
+        late_a(i).start()
+        pl.when(gives_b[i])(lambda: late_b(i).start())
+
+    def late_take(i):
+        late_a(i).wait()
+        pl.when(gives_b[i])(lambda: late_b(i).wait_send())
+
+        @pl.when(has_b[i])
+        def _():
+            late_b(i).wait_recv()
+            lb[...] = add_low(lb[...], lbr[i])
+
+        if i == 0:
+            for yy in range(2):
+                for xx in range(2):
+                    la[yy, xx, c] = add_low(la[yy, xx, c], lr1[yy, xx])
+        elif i == 1:
+            for yy in range(2):
+                la[yy, x, c] = add_low(la[yy, x, c], lr2[yy])
+        else:
+            lj[...] = add_low(la[y, x, c], lr3[...])
+
+    def late_out(t):
+        return (
+            remote(lj.at[to_part(t), :], lr4.at[t], sl4.at[0, t], ql4.at[0, t], peers[t - 1]),
+            remote(lb.at[to_part(t), :], lbr4.at[t], sl4.at[1, t], ql4.at[1, t], peers[t - 1]),
         )
 
-    def cols(k):
-        return slice(k * width, (k + 1) * width)
-
-    def mine(k=None):
-        return pl.ds(pl.multiple_of(z * part, part), part)
-
-    def first(k):
-        return [remote(g_ref.at[:, 1 - c, :, cols(k)], r1.at[:, :, cols(k)], s1.at[k], q1.at[k], core)]
-
-    def second(k):
-        return [
-            remote(h.at[:, 1 - x, 0:half, cols(k)], r2a.at[:, :, cols(k)], s2.at[0, k], q2.at[0, k], along_x),
-            remote(h.at[1 - y, :, half:, cols(k)], r2b.at[:, :, cols(k)], s2.at[1, k], q2.at[1, k], along_y),
-        ]
-
-    def third(k):
-        return [
-            remote(ia.at[1 - y, :, cols(k)], r3a.at[:, cols(k)], s3.at[0, k], q3.at[0, k], along_y),
-            remote(ib.at[1 - x, :, cols(k)], r3b.at[:, cols(k)], s3.at[1, k], q3.at[1, k], along_x),
-        ]
-
-    def fourth(k):
-        found = []
+    def late_back(t):
+        return (
+            remote(out_ref.at[mine, late], out_ref.at[mine, late], sl5.at[0, t], ql5.at[0, t], peers[t - 1]),
+            remote(lbt.at[mine, :], lbt.at[mine, :], sl5.at[1, t], ql5.at[1, t], peers[t - 1]),
+        )
+
+    def both(make, act):
         for t in range(1, n):
-            to = lax.rem(z + t, n)
-            rows = pl.ds(pl.multiple_of(to * part, part), part)
-            found.append(
-                remote(total.at[rows, cols(k)], r4.at[t, :, cols(k)], s4.at[t, k], q4.at[t, k], peers[t - 1])
-            )
-        return found
-
-    def fifth(k):
-        return [
-            remote(out_ref.at[mine(), cols(k)], out_ref.at[mine(), cols(k)], s5.at[t, k], q5.at[t, k], peers[t - 1])
-            for t in range(1, n)
-        ]
-
-    def add(a, b):
-        return (a.astype(f32) + b.astype(f32)).astype(bf16)
+            a, b = make(t)
+            act(a)
+            pl.when(dp == 3)(lambda b=b: act(b))
+
+    from_x, from_y, from_c = along_x[0], along_y[0], core[0]
+    across = from_x + from_y - dp
+    onward = jnp.where(c == 0, from_y, from_x)
+    target = (jnp.where(c == 0, from_x, from_y), z)
+    other = 1 - 2 * c
+    hops = [
+        (dp, from_x, along_x), (dp, from_y, along_y), (dp, from_c, core), (onward, across, target),
+        (from_x, from_x + other, core), (from_y, from_y + other, core), (across, across + other, core),
+    ]
+
+    def gather(kind):
+        slot, _, peer = hops[kind]
+        return remote(fresh_ref.at[slot], fresh_ref.at[slot], sg.at[kind], qg.at[kind], peer)
+
+    def make_fresh():
+        cut = b_ref.shape[1]
+        grads = out_ref[:, b_at_col:early_end].astype(f32)
+        new_b = adam_fresh(b_ref[...], grads, mean_ref[...], square_ref[...])
+        grads = out_ref[:, lanes:late_end].astype(f32)
+        new_f = adam_fresh(bf_ref[...], grads, mean_f_ref[...], square_f_ref[...])
+        fresh_ref[dp] = jnp.concatenate([new_b, new_f], axis=1).astype(bf16)
 
     def norm_copy(i, peer):
         return remote(nsum.at[i], nr.at[i], sn.at[i], qn.at[i], peer)
 
-    nsum[0] = norm_in_ref[...]
     norm_stages = [norm_copy(0, core), norm_copy(1, along_x), norm_copy(2, along_y)]
     norm_last = [
         remote(nsum.at[3], nr.at[2 + t], sn.at[2 + t], qn.at[2 + t], peers[t - 1]) for t in range(1, n)
     ]
-    for k in range(chunks):
-        first(k)[0].start()
-    norm_stages[0].start()
-
-    def after_first(k):
-        for copy in first(k):
+
+    def norm_take(i):
+        norm_stages[i].wait()
+        nsum[i + 1] = nsum[i] + nr[i]
+
+    @pl.when(step == 0)
+    def _():
+        greet([core, along_x, along_y] + peers)
+        for k in range(count):
+            for t in range(1, n):
+                e_out(k, t).start()
+        att_acc[...] = jnp.zeros_like(att_acc)
+        mid_acc[...] = jnp.zeros_like(mid_acc)
+        first_acc[...] = jnp.zeros_like(first_acc)
+        dmid_acc[...] = jnp.zeros_like(dmid_acc)
+
+    @pl.when(step < n)
+    def _():
+        out = o_ref[...].reshape(rows, cols)
+        att_acc[...] += nn(out, wo_ref[...])
+        mid_acc[...] += nn(out, a_out_ref[...])
+        ga = sum(nn(dmid_out_t_ref[q], out[q * size : (q + 1) * size]) for q in range(seqs)).astype(bf16)
+        for i in range(cols // lanes):
+            owner = step * (cols // lanes) + i
+            la[owner // 4, lax.rem(owner // 2, 2), lax.rem(owner, 2)] = ga[:, i * lanes : (i + 1) * lanes]
+
+    @pl.when(step == n - 1)
+    def _():
+        gb = None
+        for q in range(seqs):
+            at = slice(q * size, (q + 1) * size)
+            product = nn(mid_acc[at].astype(bf16).T, low_ref[at])
+            gb = product if gb is None else gb + product
+        lb[...] = (adapter_scale * gb).astype(bf16)
+        late_start(0)
+
+    @pl.when(step >= n)
+    def _():
+        dq, dk, dv = (r[...].reshape(rows, cols) for r in (dq_ref, dk_ref, dv_ref))
+        first_acc[...] += nt(dq, wq_ref[...]) + nt(dk, wk_ref[...]) + nt(dv, wv_ref[...])
+        dmid_acc[...] += nt(dq, bq_ref[...]) + nt(dk, bk_ref[...]) + nt(dv, bv_ref[...])
+
+    @pl.when(step == n + 1)
+    def _():
+        late_take(0)
+        late_start(1)
+
+    @pl.when(step == 2 * n - 1)
+    def _():
+        late_take(1)
+        late_start(2)
+        for k in range(count):
+            cut = slice(*early_cuts[k])
+            for t in range(1, n):
+                e_out(k, t).wait()
+            value = e_ref[mine, cut].astype(f32)
+            for t in range(1, n):
+                value += r4[t, :, cut].astype(f32)
+            out_ref[mine, cut] = value.astype(bf16)
+            for t in range(1, n):
+                e_back(k, t).start()
+
+    @pl.when(step == pl.num_programs(0) - 1)
+    def _():
+        norm = [jnp.zeros((1, width), f32) for _ in range(4)]
+
+        def sequence(q):
+            at = slice(q * size, (q + 1) * size)
+            x_in = x_ref[q].astype(f32)
+            mid = mid_acc[at].astype(bf16)
+            att = att_acc[at] + bias_ref[...] + adapter_scale * nn(mid, b_out_ref[...])
+            ff = ff_ref[at] + bias_ff_ref[...] + adapter_scale * nn(mid_ff_ref[at], b_ff_ref[...])
+            mixed_ref[q] = (x_in + att + ff).astype(bf16)
+            dmid = (adapter_scale * dmid_acc[at]).astype(bf16)
+            grad_first = first_acc[at] + nt(dmid, a_qkv_ref[...])
+            grad_second = second_ref[at] + nt(dmid_up_ref[at], a_up_ref[...])
+            centre = x_in - jnp.mean(x_in, axis=-1, keepdims=True)
+            inv = lax.rsqrt(jnp.mean(centre * centre, axis=-1, keepdims=True) + norm_eps)
+            unit = centre * inv
+            pulled = grad_first * gain_ref[0:1] + grad_second * gain_ref[1:2]
+            back = inv * (
+                pulled
+                - jnp.mean(pulled, axis=-1, keepdims=True)
+                - unit * jnp.mean(pulled * unit, axis=-1, keepdims=True)
+            )
+            row_grad = cot_ref[q].astype(f32) * weight_ref[at]
+            tokens_ref[q] = (row_grad + back).astype(bf16)
+            for k, value in enumerate((grad_first * unit, grad_second * unit, grad_first, grad_second)):
+                norm[k] += jnp.sum(value, axis=0, keepdims=True)
+
+        sequence(0)
+        late_take(2)
+        both(late_out, lambda copy: copy.start())
+        for q in range(1, seqs - 1):
+            sequence(q)
+        both(late_out, lambda copy: copy.wait())
+        value = lj[mine, :].astype(f32)
+        for t in range(1, n):
+            value += lr4[t].astype(f32)
+        out_ref[mine, late] = value.astype(bf16)
+
+        @pl.when(dp == 3)
+        def _():
+            value = lb[mine, :].astype(f32)
+            for t in range(1, n):
+                value += lbr4[t].astype(f32)
+            lbt[mine, :] = value.astype(bf16)
+
+        both(late_back, lambda copy: copy.start())
+        sequence(seqs - 1)
+        nsum[0] = jnp.concatenate(norm, axis=0)
+        norm_stages[0].start()
+        both(late_back, lambda copy: copy.wait())
+        for k in range(count):
+            for t in range(1, n):
+                e_back(k, t).wait()
+
+        @pl.when(dp == 3)
+        def _():
+            out_ref[:, b_at_col:early_end] = lbt[...]
+
+        make_fresh()
+        for kind in (0, 1, 2):
+            gather(kind).start()
+        keep_out = pltpu.make_async_copy(out_ref, out_hbm, done_sem.at[0])
+        keep_out.start()
+        norm_take(0)
+        norm_stages[1].start()
+        gather(0).wait_recv()
+        gather(1).wait_recv()
+        for kind in (3, 4, 5):
+            gather(kind).start()
+        norm_take(1)
+        norm_stages[2].start()
+        gather(3).wait_recv()
+        gather(6).start()
+        norm_take(2)
+        for copy in norm_last:
+            copy.start()
+        for kind in (2, 4, 5, 6):
+            gather(kind).wait_recv()
+        keep_fresh = pltpu.make_async_copy(fresh_ref, fresh_hbm, done_sem.at[1])
+        keep_fresh.start()
+        for kind in range(7):
+            gather(kind).wait_send()
+        for copy in norm_last:
             copy.wait()
-        for yy in range(2):
-            for xx in range(2):
-                h[yy, xx, :, cols(k)] = add(g_ref[2 * yy + xx, c, :, cols(k)], r1[2 * yy + xx, :, cols(k)])
-        for copy in second(k):
-            copy.start()
-
-    def after_second(k):
-        for copy in second(k):
-            copy.wait()
-        for i in range(2):
-            ia[i, :, cols(k)] = add(h[i, x, 0:half, cols(k)], r2a[i, :, cols(k)])
-            ib[i, :, cols(k)] = add(h[y, i, half:, cols(k)], r2b[i, :, cols(k)])
-        for copy in third(k):
-            copy.start()
-
-    def after_third(k):
-        for copy in third(k):
-            copy.wait()
-        total[0:half, cols(k)] = add(ia[y, :, cols(k)], r3a[:, cols(k)])
-        total[half:, cols(k)] = add(ib[x, :, cols(k)], r3b[:, cols(k)])
-        for copy in fourth(k):
-            copy.start()
-
-    def after_fourth(k):
-        for copy in fourth(k):
-            copy.wait()
-        value = total[mine(), cols(k)].astype(f32)
-        for t in range(1, n):
-            value += r4[t, :, cols(k)].astype(f32)
-        out_ref[mine(), cols(k)] = value.astype(bf16)
-        for copy in fifth(k):
-            copy.start()
-
-    def after_fifth(k):
-        for copy in fifth(k):
-            copy.wait()
-
-    stages = [after_first, after_second, after_third, after_fourth, after_fifth]
-    for step in range(chunks + len(stages) - 1):
-        for at in reversed(range(len(stages))):
-            if 0 <= step - at < chunks:
-                stages[at](step - at)
-        if step < 3:
-            norm_stages[step].wait()
-            nsum[step + 1] = nsum[step] + nr[step]
-            if step < 2:
-                norm_stages[step + 1].start()
-            else:
-                for copy in norm_last:
-                    copy.start()
-    for copy in norm_last:
-        copy.wait()
-    value = jnp.zeros_like(nsum[3])
-    for blk in range(n):
-        there = lax.rem(z - blk + n, n)
-        value += jnp.where(there == 0, nsum[3], nr[2 + jnp.maximum(there, 1)])
-    norm_ref[...] = value
-
-    cut = b_ref.shape[1]
-    grads = out_ref[:, b_at:].astype(f32)
-    new_b = adam_fresh(b_ref[...], grads[:, :cut], mean_ref[...], square_ref[...])
-    new_f = adam_fresh(bf_ref[...], grads[:, cut:], mean_f_ref[...], square_f_ref[...])
-    fresh_ref[dp] = jnp.concatenate([new_b, new_f], axis=1).astype(bf16)
-
-    def gather(i, slot, peer):
-        return remote(fresh_ref.at[slot], fresh_ref.at[slot], sg.at[i], qg.at[i], peer)
-
-    from_x, from_y = dp + 2 - 4 * x, dp + 4 - 8 * y
-    across = dp + 2 - 4 * x + 4 - 8 * y
-    onward = jnp.where(c == 0, from_y, from_x)
-    target = (jnp.where(c == 0, along_x[0], along_y[0]), z)
-    direct = [gather(0, dp, along_x), gather(1, dp, along_y), gather(2, dp, core)]
-    for copy in direct:
-        copy.start()
-    direct[0].wait()
-    direct[1].wait()
-    more = [gather(3, onward, target), gather(4, from_x, core), gather(5, from_y, core)]
-    for copy in more:
-        copy.start()
-    more[0].wait()
-    last = gather(6, across, core)
-    last.start()
-    direct[2].wait()
-    more[1].wait()
-    more[2].wait()
-    last.wait()
+        keep_out.wait()
+        keep_fresh.wait()
+        value = jnp.zeros_like(nsum[3])
+        for blk in range(n):
+            there = lax.rem(z - blk + n, n)
+            value += jnp.where(there == 0, nsum[3], nr[2 + jnp.maximum(there, 1)])
+        norm_ref[...] = value
 
 
 def update_kernel(
@@ -737,13 +1035,17 @@
     def _():
         rows, inner = params[0].shape[0], params[4].shape[0]
         got = g_ref[...].astype(f32)
+        cut, cut_f = params[8].shape[1], params[12].shape[1]
+        up = got[:, :rows]
+        qkv = got[:, rows + cut_f : 2 * rows + cut_f]
+        out = got[:, 2 * rows + cut_f + inner + cut :]
+        at = 2 * rows + cut_f
         grads = [
-            jnp.concatenate([got[:, i * rows : (i + 1) * rows].T for i in range(3)], axis=1),
-            got[:, 3 * rows : 3 * rows + inner].T,
+            jnp.concatenate([part.T for part in (qkv, out, up)], axis=1),
+            got[:, at : at + inner].T,
+            got[:, at + inner : at + inner + cut],
+            got[:, rows : rows + cut_f],
         ]
-        at = 3 * rows + inner
-        cut = params[8].shape[1]
-        grads += [got[:, at : at + cut], got[:, at + cut :]]
         for i, grad in enumerate(grads):
             param, mean, square, keep = (r[...] for r in params[4 * i : 4 * i + 4])
             mean_new = 0.9 * mean + 0.1 * grad
@@ -822,9 +1124,7 @@
 
     b_cols = adapt_b.shape[1] + adapt_b_ff.shape[1]
     bias32 = bias_in.astype(f32)
-    lookup = (domain_ids[..., None] == jnp.arange(DOMAINS, dtype=jnp.int32)).astype(f32)
-    row_weight = jnp.sum(lookup * domain_weight, axis=-1).reshape(rows, 1)
-    whole_front = dp_n == 8 and rank % (16 * n) == 0
+    whole_front = dp_n == 8 and n == 4 and seqs > 1 and (rank, width, inner) == (128, 1024, 4096)
     if whole_front:
         vmem = pl.BlockSpec(memory_space=pltpu.VMEM)
         hbm = pl.BlockSpec(memory_space=pl.ANY)
@@ -838,11 +1138,11 @@
 
         (
             w_in, w_down, a_all, a_ff, b_in, b_ff, query, keys, values, first_pos, mid_pos, g_pos,
-            grad_low, second, mid_up, mid_up_t, dmid_ff, dmid_ff_t, dmid_out_t, *tables,
+            grad_low, second, mid_up, mid_up_t, dmid_ff, dmid_ff_t, dmid_out_t, *tables, row_weight,
         ) = pl.pallas_call(
             functools.partial(front_kernel, n=n, depth=depth),
-            in_specs=[hbm] * 7 + [vmem] * 6,
-            out_specs=[hbm] * 12 + [vmem] * 10,
+            in_specs=[hbm] * 3 + [vmem] * 6 + [pl.BlockSpec(memory_space=pltpu.SMEM)] + [vmem] * 4,
+            out_specs=[hbm] * 12 + [vmem] * 11,
             out_shape=[
                 shape(width, 8 * width), shape(inner, width), shape(width, 3 * rank), shape(inner, rank),
                 shape(rank, 8 * width), shape(rank, width),
@@ -852,8 +1152,13 @@
                 shape(rows, rank), shape(seqs, rank, span), shape(rows, rank), shape(seqs, rank, span),
                 shape(seqs, rank, span),
                 shape(length, lanes, dtype=f32), shape(length, lanes, dtype=f32), shape(length, lanes, dtype=f32),
+                shape(rows, 1, dtype=f32),
             ],
             scratch_shapes=[
+                pltpu.VMEM(adapt_a.shape, bf16),
+                pltpu.VMEM(adapt_a_ff.shape, bf16),
+                pltpu.VMEM(adapt_b.shape, bf16),
+                pltpu.VMEM(adapt_b_ff.shape, bf16),
                 pltpu.VMEM((n, seqs, span, width), bf16),
                 pltpu.VMEM((seqs, length, cz), bf16),
                 pltpu.VMEM((seqs, length, cz), bf16),
@@ -876,10 +1181,12 @@
             name="front",
         )(
             tokens, frozen_input_weights, frozen_down_weight,
-            adapt_a.astype(bf16), adapt_a_ff.astype(bf16), adapt_b.astype(bf16), adapt_b_ff.astype(bf16),
-            cotangent, row_weight, norm_gain, norm_shift, bias32.reshape(1, -1), freq.reshape(1, -1),
+            adapt_a, adapt_a_ff, adapt_b, adapt_b_ff,
+            cotangent, domain_ids, domain_weight, norm_gain, norm_shift, bias32.reshape(1, -1), freq.reshape(1, -1),
         )
     else:
+        lookup = (domain_ids[..., None] == jnp.arange(DOMAINS, dtype=jnp.int32)).astype(f32)
+        row_weight = jnp.sum(lookup * domain_weight, axis=-1).reshape(rows, 1)
         row_grad = cotangent.astype(f32).reshape(rows, width) * row_weight
         grad_low = row_grad.astype(bf16)
         b_shard = jnp.concatenate([adapt_b, adapt_b_ff], axis=1).astype(bf16)
@@ -1015,206 +1322,281 @@
         return jnp.maximum(s - steps, 0)
 
     head = pl.BlockSpec((1, length, lanes), head_map)
-    local, own, ff, grad_second, mid_ff, dmid_up, grad_a_ff_t, grad_b_up = pl.pallas_call(
-        functools.partial(middle_kernel, n=n, pairs=pairs, steps=steps, depth=depth),
-        grid=(steps + inner // inner_block,),
-        in_specs=[head] * 4
+    early = whole_front
+    dma = pltpu.SemaphoreType.DMA
+    half_rank = rank // 2
+
+    def wide(*dims, dtype=bf16):
+        return jax.ShapeDtypeStruct(dims, dtype)
+
+    in_specs = (
+        [head] * 4
         + [one_buffer((length, lanes))] * 3
-        + [one_buffer((8, lanes))]
         + [one_buffer((rows, width))] * 2
         + [one_buffer((rows, rank)), one_buffer((seqs, rank, span))] * 2
         + [
             pl.BlockSpec((width, inner_block), lambda s: (0, 4 * width // inner_block + inner_at(s))),
             pl.BlockSpec((inner_block, width), lambda s: (inner_at(s), 0)),
             pl.BlockSpec((inner_block, rank), lambda s: (inner_at(s), 0)),
-            pl.BlockSpec((rank, inner_block), lambda s: (0, 4 * width // inner_block + inner_at(s))),
+            one_buffer((rank, 8 * width))
+            if early
+            else pl.BlockSpec((rank, inner_block), lambda s: (0, 4 * width // inner_block + inner_at(s))),
             pl.BlockSpec((1, inner_block), lambda s: (0, 4 * width // inner_block + inner_at(s))),
-        ],
-        out_specs=[
-            pl.BlockSpec(memory_space=pl.ANY),
-            pl.BlockSpec((1, 3, length, lanes), lambda s: (seq_pair(s)[0], 0, 0, seq_pair(s)[1])),
-            one_buffer((rows, width)),
-            one_buffer((rows, width)),
-            one_buffer((rows, rank)),
-            one_buffer((rows, rank)),
-            pl.BlockSpec((rank, inner_block), lambda s: (0, inner_at(s))),
-            pl.BlockSpec((rank, inner_block), lambda s: (0, inner_at(s))),
-        ],
-        out_shape=[
-            jax.ShapeDtypeStruct((seqs, 4, span, width), bf16),
-            jax.ShapeDtypeStruct((seqs, 3, length, cz), bf16),
-            jax.ShapeDtypeStruct((rows, width), f32),
-            jax.ShapeDtypeStruct((rows, width), f32),
-            jax.ShapeDtypeStruct((rows, rank), bf16),
-            jax.ShapeDtypeStruct((rows, rank), bf16),
-            jax.ShapeDtypeStruct((rank, inner), f32),
-            jax.ShapeDtypeStruct((rank, inner), f32),
-        ],
-        scratch_shapes=[
-            pltpu.VMEM((steps, n, 4, span, lanes), bf16),
-            pltpu.VMEM((length, lanes), f32),
-            pltpu.VMEM((length, lanes), f32),
-            pltpu.VMEM((rows, rank), f32),
-            pltpu.VMEM((rows, rank), f32),
-            pltpu.SemaphoreType.DMA((steps, n)),
-            pltpu.SemaphoreType.DMA((steps, n)),
-            pltpu.SemaphoreType.DMA((steps,)),
-        ],
+        ]
+    )
+    operands = [
+        query, keys, values, g_pos, *tables, second, grad_low, mid_up, mid_up_t, dmid_ff, dmid_ff_t,
+        w_in, w_down, a_ff, b_in, bias32.reshape(1, -1),
+    ]
+    partial_specs = [one_buffer((rows, width))] * 2 + [one_buffer((rows, rank))] * 2
+    partial_shapes = [wide(rows, width, dtype=f32)] * 2 + [wide(rows, rank)] * 2
+    local_spec, local_shape = pl.BlockSpec(memory_space=pl.ANY), wide(seqs, 4, span, width)
+    scratch = [
+        pltpu.VMEM((steps, n, 4, span, lanes), bf16),
+        pltpu.VMEM((length, lanes), f32),
+        pltpu.VMEM((length, lanes), f32),
+        pltpu.VMEM((rows, rank), f32),
+        pltpu.VMEM((rows, rank), f32),
+        dma((steps, n)),
+        dma((steps, n)),
+        dma((steps,)),
+    ]
+    if early:
+        in_specs += [
+            pl.BlockSpec((1, length, width), lambda s: (seq_pair(s)[0], 0, 0)),
+            pl.BlockSpec((1, length, rank), lambda s: (seq_pair(s)[0], 0, 0)),
+        ]
+        operands += [first_pos, mid_pos]
+        out_specs = [local_spec] + partial_specs + [one_buffer((rank, early_end))]
+        out_shapes = [local_shape] + partial_shapes + [wide(rank, early_end)]
+        cuts = len(early_cuts)
+        scratch += [
+            pltpu.VMEM((2, 2, 2, rank, early_end), bf16),
+            pltpu.VMEM((length, rank), f32),
+            pltpu.VMEM((3, pairs, rank, lanes), f32),
+            pltpu.VMEM((rank, width), f32),
+            pltpu.VMEM((2, 2, rank, early_end), bf16),
+            pltpu.VMEM((2, half_rank, early_end), bf16),
+            pltpu.VMEM((2, half_rank, early_end), bf16),
+            pltpu.VMEM((half_rank, early_end), bf16),
+            pltpu.VMEM((half_rank, early_end), bf16),
+            dma((5,)), dma((5,)), dma((2, cuts)), dma((2, cuts)), dma((2, cuts)), dma((2, cuts)),
+        ]
+    else:
+        out_specs = (
+            [local_spec, pl.BlockSpec((1, 3, length, lanes), lambda s: (seq_pair(s)[0], 0, 0, seq_pair(s)[1]))]
+            + partial_specs
+            + [pl.BlockSpec((rank, inner_block), lambda s: (0, inner_at(s)))] * 2
+        )
+        out_shapes = (
+            [local_shape, wide(seqs, 3, length, cz)] + partial_shapes + [wide(rank, inner, dtype=f32)] * 2
+        )
+    middle = pl.pallas_call(
+        functools.partial(middle_kernel, n=n, pairs=pairs, steps=steps, depth=depth, early=early),
+        grid=(steps + inner // inner_block,),
+        in_specs=in_specs,
+        out_specs=out_specs,
+        out_shape=out_shapes,
+        scratch_shapes=scratch,
         compiler_params=pltpu.CompilerParams(
             collective_id=0, has_side_effects=True, vmem_limit_bytes=60 << 20
         ),
         name="middle",
-    )(
-        query, keys, values, g_pos, *tables, tables[0][:8], second, grad_low, mid_up, mid_up_t, dmid_ff, dmid_ff_t,
-        w_in, w_down, a_ff, b_in, bias32.reshape(1, -1),
-    )
-    grad_b_up = adapter_scale * grad_b_up
-
-    first_pos = first_pos.reshape(seqs * length, width)
-    mid_pos = mid_pos.reshape(seqs * length, rank)
-    b_own = jnp.concatenate(
-        [lax.dynamic_slice_in_dim(b_in[:, t * width : (t + 1) * width], z * cz, cz, 1) for t in range(3)], axis=1
-    )
-    djoint_own = [own[:, t].reshape(seqs * length, cz) for t in range(3)]
-    dmid_own = sum(nt(djoint_own[t], b_own[:, t * cz : (t + 1) * cz]) for t in range(3))
-    dmid_own = (adapter_scale * dmid_own).astype(bf16)
-    grad_a_qkv_t = tn(dmid_own, first_pos)
-    mine = (jnp.arange(n, dtype=jnp.int32) == z)[None, :, None]
-    grad_b_qkv = jnp.concatenate(
-        [
-            jnp.where(mine, adapter_scale * tn(mid_pos, part)[:, None, :], 0.0).reshape(rank, width)
-            for part in djoint_own
-        ],
-        axis=1,
-    )
-    grad_a_up_t = tn(dmid_up, second)
-    grad_b_ffp = adapter_scale * tn(mid_ff, grad_low)
-
-    def fixed(shape, *at):
-        return pl.BlockSpec(shape, lambda t: at, pipeline_mode=pl.Buffered(1))
-
-    def column(at, height):
-        return pl.BlockSpec((height, cz), lambda t: (0, at * n + t))
-
-    mixed, grad_tokens, norm_part, grad_a_out_t, grad_b_out = pl.pallas_call(
-        finish_kernel,
-        grid=(n,),
-        in_specs=[
-            pl.BlockSpec((seqs, 4, span, cz), lambda t: (0, 0, 0, t)),
-            pl.BlockSpec((cz, width), lambda t: (t, 3)),
-            column(0, width), column(1, width), column(2, width),
-            pl.BlockSpec((cz, rank), lambda t: (t, 1)),
-            fixed((width, rank), 0, 0),
-            fixed((rank, width), 0, 3),
-            column(0, rank), column(1, rank), column(2, rank),
-            fixed((1, width), 0, 3),
-            fixed((seqs, span, width), 0, 0, 0),
-            fixed((seqs, span, width), 0, 0, 0),
-            fixed((rows, 1), 0, 0),
-            fixed((rows, width), 0, 0),
-            fixed((1, width), 0, 0),
-            fixed((rows, rank), 0, 0),
-            fixed((rank, width), 0, 0),
-            fixed((rows, width), 0, 0),
-            fixed((rows, rank), 0, 0),
-            fixed((width, rank), 0, 2),
-            fixed((2, width), 0, 0),
-            fixed((seqs, rank, span), 0, 0, 0),
-            fixed((rows, width), 0, 0),
-        ],
-        out_specs=[
-            fixed((seqs, span, width), 0, 0, 0),
-            fixed((seqs, span, width), 0, 0, 0),
-            fixed((4, width), 0, 0),
-            pl.BlockSpec((rank, cz), lambda t: (0, t)),
-            fixed((rank, width), 0, 0),
-        ],
-        out_shape=[
-            jax.ShapeDtypeStruct((seqs, span, width), bf16),
-            jax.ShapeDtypeStruct((seqs, span, width), bf16),
-            jax.ShapeDtypeStruct((4, width), f32),
-            jax.ShapeDtypeStruct((rank, width), f32),
-            jax.ShapeDtypeStruct((rank, width), f32),
-        ],
-        scratch_shapes=[
-            pltpu.VMEM((rows, width), f32),
-            pltpu.VMEM((rows, rank), f32),
-            pltpu.VMEM((rows, width), f32),
-            pltpu.VMEM((rows, rank), f32),
-        ],
-        compiler_params=pltpu.CompilerParams(vmem_limit_bytes=56 << 20),
-        name="finish",
-    )(
-        local, w_in, w_in, w_in, w_in, a_all, a_all, b_in, b_in, b_in, b_in, bias32.reshape(1, -1),
-        tokens, cotangent, row_weight, ff, bias_ff.astype(f32).reshape(1, -1), mid_ff, b_ff,
-        grad_second, dmid_up, a_all, norm_gain, dmid_out_t, grad_low,
-    )
-    grad_b_out = adapter_scale * grad_b_out
-
-    def by_owner(values):
-        return values.reshape(rank, dp_n, -1)
-
-    parts = [
-        by_owner(grad_a_qkv_t), by_owner(grad_a_out_t), by_owner(grad_a_up_t), by_owner(grad_a_ff_t),
-        by_owner(jnp.concatenate([grad_b_qkv, grad_b_out, grad_b_up], axis=1)), by_owner(grad_b_ffp),
-    ]
-    widths = [p.shape[2] for p in parts]
-    owned = jnp.transpose(jnp.concatenate([p.astype(bf16) for p in parts], axis=2), (1, 0, 2))
-    total_cols = owned.shape[2]
-    b_at = sum(widths[:4])
-    if dp_n == 8 and rank % (16 * n) == 0:
-        chunks = 4
-        half = rank // 2
-        vmem = pl.BlockSpec(memory_space=pltpu.VMEM)
-        dma = pltpu.SemaphoreType.DMA
-        reduced, norm_sum, fresh = pl.pallas_call(
-            functools.partial(reduce_kernel, n=n, chunks=chunks, b_at=b_at),
-            in_specs=[vmem] * 8,
-            out_specs=[vmem] * 3,
+    )(*operands)
+
+    if early:
+        local, ff, grad_second, mid_ff, dmid_up, summed = middle
+        part = rank // n
+
+        def single(shape, *at):
+            return pl.BlockSpec(shape, lambda s: at, pipeline_mode=pl.Buffered(1))
+
+        def of_out(s):
+            return jnp.minimum(s, n - 1)
+
+        def of_grad(s):
+            return jnp.maximum(s - n, 0)
+
+        def piece_spec(kind, at):
+            return pl.BlockSpec((seqs, 1, span, cz), lambda s: (0, kind, 0, at(s)))
+
+        def columns(kind, height):
+            return pl.BlockSpec((height, cz), lambda s: (0, kind * n + of_grad(s)))
+
+        full = single((seqs, span, width), 0, 0, 0)
+        cuts = len(early_cuts)
+        b_here = [adapt_b, mean_b, square_b, adapt_b_ff, mean_b_ff, square_b_ff]
+        mixed, grad_tokens, reduced, norm_sum, fresh = pl.pallas_call(
+            functools.partial(tail_kernel, n=n),
+            grid=(2 * n,),
+            in_specs=[
+                piece_spec(0, of_out), piece_spec(1, of_grad), piece_spec(2, of_grad), piece_spec(3, of_grad),
+                pl.BlockSpec((cz, width), lambda s: (of_out(s), 3)),
+                columns(0, width), columns(1, width), columns(2, width),
+                pl.BlockSpec((cz, rank), lambda s: (of_out(s), 1)),
+                single((width, rank), 0, 0),
+                single((rank, width), 0, 3),
+                columns(0, rank), columns(1, rank), columns(2, rank),
+                single((1, width), 0, 3),
+                full, full,
+                single((rows, 1), 0, 0),
+                single((rows, width), 0, 0),
+                single((1, width), 0, 0),
+                single((rows, rank), 0, 0),
+                single((rank, width), 0, 0),
+                single((rows, width), 0, 0),
+                single((rows, rank), 0, 0),
+                single((width, rank), 0, 2),
+                single((2, width), 0, 0),
+                single((seqs, rank, span), 0, 0, 0),
+                single((rows, width), 0, 0),
+                single((rank, early_end), 0, 0),
+            ]
+            + [single(v.shape, 0, 0) for v in b_here],
+            out_specs=[
+                full, full, pl.BlockSpec(memory_space=pl.ANY), single((4, width), 0, 0),
+                pl.BlockSpec(memory_space=pl.ANY),
+            ],
             out_shape=[
-                jax.ShapeDtypeStruct((rank, total_cols), bf16),
-                jax.ShapeDtypeStruct((4, width), f32),
-                jax.ShapeDtypeStruct((dp_n, rank, b_cols), bf16),
+                wide(seqs, span, width), wide(seqs, span, width), wide(rank, 2048), wide(4, width, dtype=f32),
+                wide(dp_n, rank, b_cols),
             ],
             scratch_shapes=[
-                pltpu.VMEM((4, rank, total_cols), bf16),
-                pltpu.VMEM((2, 2, rank, total_cols), bf16),
-                pltpu.VMEM((2, half, total_cols), bf16),
-                pltpu.VMEM((2, half, total_cols), bf16),
-                pltpu.VMEM((2, half, total_cols), bf16),
-                pltpu.VMEM((2, half, total_cols), bf16),
-                pltpu.VMEM((half, total_cols), bf16),
-                pltpu.VMEM((half, total_cols), bf16),
-                pltpu.VMEM((rank, total_cols), bf16),
-                pltpu.VMEM((n, rank // n, total_cols), bf16),
+                pltpu.VMEM((rank, 2048), bf16),
+                pltpu.VMEM((dp_n, rank, b_cols), bf16),
+                pltpu.VMEM((rows, width), f32),
+                pltpu.VMEM((rows, rank), f32),
+                pltpu.VMEM((rows, width), f32),
+                pltpu.VMEM((rows, rank), f32),
+                pltpu.VMEM((n, part, early_end), bf16),
+                pltpu.VMEM((2, 2, 2, rank, lanes), bf16),
+                pltpu.VMEM((rank, width), bf16),
+                pltpu.VMEM((2, 2, rank, lanes), bf16),
+                pltpu.VMEM((2, rank, lanes), bf16),
+                pltpu.VMEM((rank, lanes), bf16),
+                pltpu.VMEM((3, rank, width), bf16),
+                pltpu.VMEM((rank, lanes), bf16),
+                pltpu.VMEM((n, part, lanes), bf16),
+                pltpu.VMEM((n, part, width), bf16),
+                pltpu.VMEM((rank, width), bf16),
                 pltpu.VMEM((2 + n, 4, width), f32),
                 pltpu.VMEM((4, 4, width), f32),
-                dma((chunks,)), dma((chunks,)),
-                dma((2, chunks)), dma((2, chunks)),
-                dma((2, chunks)), dma((2, chunks)),
-                dma((n, chunks)), dma((n, chunks)),
-                dma((n, chunks)), dma((n, chunks)),
-                dma((2 + n,)), dma((2 + n,)),
-                dma((7,)), dma((7,)),
+                dma((n, cuts)), dma((n, cuts)), dma((n, cuts)), dma((n, cuts)),
+                dma((2, 3)), dma((2, 3)), dma((2, n)), dma((2, n)), dma((2, n)), dma((2, n)),
+                dma((2 + n,)), dma((2 + n,)), dma((7,)), dma((7,)), dma((2,)),
             ],
             compiler_params=pltpu.CompilerParams(
-                collective_id=1, has_side_effects=True, vmem_limit_bytes=48 << 20
+                collective_id=1, has_side_effects=True, vmem_limit_bytes=58 << 20
             ),
-            name="reduce",
+            name="tail",
         )(
-            owned.reshape(4, 2, rank, total_cols), norm_part,
-            adapt_b, mean_b, square_b, adapt_b_ff, mean_b_ff, square_b_ff,
+            local, local, local, local, w_in, w_in, w_in, w_in, a_all, a_all, b_in, b_in, b_in, b_in,
+            bias32.reshape(1, -1), tokens, cotangent, row_weight, ff, bias_ff.astype(f32).reshape(1, -1), mid_ff, b_ff,
+            grad_second, dmid_up, a_all, norm_gain, dmid_out_t, grad_low, summed, *b_here,
         )
     else:
+        local, own, ff, grad_second, mid_ff, dmid_up, grad_a_ff_t, grad_b_up = middle
+        grad_b_up = adapter_scale * grad_b_up
+        first_pos = first_pos.reshape(seqs * length, width)
+        mid_pos = mid_pos.reshape(seqs * length, rank)
+        b_own = jnp.concatenate(
+            [lax.dynamic_slice_in_dim(b_in[:, t * width : (t + 1) * width], z * cz, cz, 1) for t in range(3)], axis=1
+        )
+        djoint_own = [own[:, t].reshape(seqs * length, cz) for t in range(3)]
+        dmid_own = sum(nt(djoint_own[t], b_own[:, t * cz : (t + 1) * cz]) for t in range(3))
+        dmid_own = (adapter_scale * dmid_own).astype(bf16)
+        grad_a_qkv_t = tn(dmid_own, first_pos)
+        mine = (jnp.arange(n, dtype=jnp.int32) == z)[None, :, None]
+        grad_b_qkv = jnp.concatenate(
+            [
+                jnp.where(mine, adapter_scale * tn(mid_pos, part)[:, None, :], 0.0).reshape(rank, width)
+                for part in djoint_own
+            ],
+            axis=1,
+        )
+        grad_a_up_t = tn(dmid_up, second)
+        grad_b_ffp = adapter_scale * tn(mid_ff, grad_low)
+
+        def fixed(shape, *at):
+            return pl.BlockSpec(shape, lambda t: at, pipeline_mode=pl.Buffered(1))
+
+        def column(at, height):
+            return pl.BlockSpec((height, cz), lambda t: (0, at * n + t))
+
+        mixed, grad_tokens, norm_part, grad_a_out_t, grad_b_out = pl.pallas_call(
+            finish_kernel,
+            grid=(n,),
+            in_specs=[
+                pl.BlockSpec((seqs, 4, span, cz), lambda t: (0, 0, 0, t)),
+                pl.BlockSpec((cz, width), lambda t: (t, 3)),
+                column(0, width), column(1, width), column(2, width),
+                pl.BlockSpec((cz, rank), lambda t: (t, 1)),
+                fixed((width, rank), 0, 0),
+                fixed((rank, width), 0, 3),
+                column(0, rank), column(1, rank), column(2, rank),
+                fixed((1, width), 0, 3),
+                fixed((seqs, span, width), 0, 0, 0),
+                fixed((seqs, span, width), 0, 0, 0),
+                fixed((rows, 1), 0, 0),
+                fixed((rows, width), 0, 0),
+                fixed((1, width), 0, 0),
+                fixed((rows, rank), 0, 0),
+                fixed((rank, width), 0, 0),
+                fixed((rows, width), 0, 0),
+                fixed((rows, rank), 0, 0),
+                fixed((width, rank), 0, 2),
+                fixed((2, width), 0, 0),
+                fixed((seqs, rank, span), 0, 0, 0),
+                fixed((rows, width), 0, 0),
+            ],
+            out_specs=[
+                fixed((seqs, span, width), 0, 0, 0),
+                fixed((seqs, span, width), 0, 0, 0),
+                fixed((4, width), 0, 0),
+                pl.BlockSpec((rank, cz), lambda t: (0, t)),
+                fixed((rank, width), 0, 0),
+            ],
+            out_shape=[
+                jax.ShapeDtypeStruct((seqs, span, width), bf16),
+                jax.ShapeDtypeStruct((seqs, span, width), bf16),
+                jax.ShapeDtypeStruct((4, width), f32),
+                jax.ShapeDtypeStruct((rank, width), f32),
+                jax.ShapeDtypeStruct((rank, width), f32),
+            ],
+            scratch_shapes=[
+                pltpu.VMEM((rows, width), f32),
+                pltpu.VMEM((rows, rank), f32),
+                pltpu.VMEM((rows, width), f32),
+                pltpu.VMEM((rows, rank), f32),
+            ],
+            compiler_params=pltpu.CompilerParams(vmem_limit_bytes=56 << 20),
+            name="finish",
+        )(
+            local, w_in, w_in, w_in, w_in, a_all, a_all, b_in, b_in, b_in, b_in, bias32.reshape(1, -1),
+            tokens, cotangent, row_weight, ff, bias_ff.astype(f32).reshape(1, -1), mid_ff, b_ff,
+            grad_second, dmid_up, a_all, norm_gain, dmid_out_t, grad_low,
+        )
+        grad_b_out = adapter_scale * grad_b_out
+
+        def by_owner(values):
+            return values.reshape(rank, dp_n, -1)
+
+        parts = [
+            by_owner(grad_a_up_t), by_owner(grad_b_ffp), by_owner(grad_a_qkv_t), by_owner(grad_a_ff_t),
+            by_owner(jnp.concatenate([grad_b_qkv, grad_b_out, grad_b_up], axis=1)), by_owner(grad_a_out_t),
+        ]
+        widths = [p.shape[2] for p in parts]
+        owned = jnp.transpose(jnp.concatenate([p.astype(bf16) for p in parts], axis=2), (1, 0, 2))
+        b_at = sum(widths[:4])
         reduced = lax.psum_scatter(owned.astype(f32), "dp", scatter_dimension=0, tiled=True)
         reduced = lax.psum(reduced[0], "blk").astype(bf16)
         norm_sum = lax.psum(norm_part, ("dp", "blk"))
-        grads_b = reduced[:, b_at:].astype(f32)
-        cut = adapt_b.shape[1]
+        grads_b = reduced[:, b_at : b_at + adapt_b.shape[1]].astype(f32)
+        grads_f = reduced[:, widths[0] : widths[0] + widths[1]].astype(f32)
         fresh = jnp.concatenate(
             [
-                adam_fresh(adapt_b, grads_b[:, :cut], mean_b, square_b),
-                adam_fresh(adapt_b_ff, grads_b[:, cut:], mean_b_ff, square_b_ff),
+                adam_fresh(adapt_b, grads_b, mean_b, square_b),
+                adam_fresh(adapt_b_ff, grads_f, mean_b_ff, square_b_ff),
             ],
             axis=1,
         ).astype(bf16)

time: 461 us -> 401 us (0.87)
  local copies, waits for them, and re-layouts: 26.3 us -> 4.87 us
  matrix products: 12.3 us -> 0 us
  other arithmetic: 14 us -> 1.93 us
  Pallas kernels: 398 us -> 386 us
    pallas_call x2 -> x1, Pallas kernels: 88.2 us -> 64.8 us  [body(): pl.pallas_call(functools.partial(tail_kernel, n=n), grid=(2 * n,), in_spe...]
    dot_general x8 -> x0, matrix products: 12.3 us -> none  [the longest x6 8.54 us: tn(): lax.dot_general(left, right, (((0,), (0,)), ((), ())), preferred_element_...]
    pallas_call x1, Pallas kernels: 150 us -> 161 us  [body(): pl.pallas_call(functools.partial(middle_kernel, n=n, pairs=pairs, steps=s...]
    dot_general x1 -> x0, local copies, waits for them, and re-layouts: 8.97 us -> none  [tn(): lax.dot_general(left, right, (((0,), (0,)), ((), ())), preferred_element_...]
    convert_element_type x5 -> x0, other arithmetic: 6.56 us -> none  [the longest x1 1.78 us: body(): adapt_b.astype(bf16)]
    slice x3 -> x0, local copies, waits for them, and re-layouts: 5.96 us -> none  [the longest x1 2.74 us: body(): djoint_own = [own[:, t].reshape(seqs * length, cz) for t in range(3)]]
    unnamed x73 -> x46, local copies, waits for them, and re-layouts: 10.1 us -> 4.26 us
where the time goes in v4:
time: 401 us; the launch traced here: 394 us
  Pallas kernels  386 us (96%)
  local copies, waits for them, and re-layouts  4.87 us (1%)
    pallas_call x1, Pallas kernels, body(): pl.pallas_call(functools.partial(middle_kernel, n=n, pairs=pairs, steps=s...  161 us
    pallas_call x1, Pallas kernels, body(): pl.pallas_call(functools.partial(front_kernel, n=n, depth=depth), in_spec...  152 us
    pallas_call x1, Pallas kernels, body(): pl.pallas_call(functools.partial(tail_kernel, n=n), grid=(2 * n,), in_spe...  64.8 us
    pallas_call x1, Pallas kernels, body(): pl.pallas_call(functools.partial(update_kernel, rank=rank, width=width),...  8.8 us

profile of v4, /device:TPU:0, one launch (start us, length us, event | category | flops | bytes accessed | tf_op | source)
XLA Modules:
  0.0 393.9 jit_solution(4542137983800253230)
XLA Ops:
  0.7 1.3 reshape.52
  2.0 151.8 %front.1 = (bf16[1024,8192]{1,0:T(8,128)(2,1)}, bf16[4096,1024]{1,0:T(8,128)(2,1)}, bf16[1024,384]{1,0:T(8,128)(2,1)}, bf16[4096,128]{1,0:T(8,128)(2,1)}, bf16[1...) custom-call(bf16[3,256,1024]{2,1,0:T(8,128)(2,1)} %x_ref.1, ...), custom_call_target="tpu_custom_call" | custom-call | tf_op jit(solution)/shard_map/front/pallas_call | solution.py:1142
  153.8 0.0 copy-start.21
  153.8 160.8 %middle.1 = (bf16[3,4,256,1024]{3,2,1,0:T(8,128)(2,1)}, f32[768,1024]{1,0:T(8,128)}, f32[768,1024]{1,0:T(8,128)}, bf16[768,128]{1,0:T(8,128)(2,1)}, bf16[768,128]{1,0:T(8,128)(2,1)}, /*index=5*/bf16[128,1920]{1,0:T(8,128)(2,1)}) custom-call(bf16[3,1024,256]{2,1,0:T(8,128)(2,1)} %get-tuple-element.66.q_ref, bf16[3,1024,256]{2,1,0:T(8,128)(2,1)} %get-tuple-element.67.k_ref, ...), custom_call_target="tpu_custom_call" | custom-call | tf_op jit(solution)/shard_map/middle/pallas_call | solution.py:1394
  314.6 0.0 copy-done.21
  314.6 0.6 reshape.54
  315.2 0.0 copy-start
  315.2 0.0 copy-start.1
  315.2 0.0 copy-start.4
  315.3 0.0 copy-start.5
  315.3 0.0 copy-start.6
  315.3 0.0 copy-start.7
  315.3 0.0 copy-start.9
  315.3 0.0 copy-start.10
  315.3 0.0 copy-start.11
  315.3 0.0 copy-start.12
  315.3 0.0 copy-start.13
  315.4 0.0 copy-start.14
  315.4 0.0 copy-start.15
  315.4 0.0 copy-start.16
  315.4 0.0 copy-start.17
  315.4 64.8 %tail.1 = (bf16[3,256,1024]{2,1,0:T(8,128)(2,1)}, bf16[3,256,1024]{2,1,0:T(8,128)(2,1)}, bf16[128,2048]{1,0:T(8,128)(2,1)}, f32[4,1024]{1,0:T(4,128)}, bf16[8,128,1152]{2,1,0:T(8,128)(2,1)}) custom-call(bf16[3,4,256,1024]{3,2,1,0:T(8,128)(2,1)} %get-tuple-element.85.o_ref.dq_ref.dk_ref.dv_ref, ...), custom_call_target="tpu_custom_call" | custom-call | tf_op jit(solution)/shard_map/tail/pallas_call | solution.py:1429
  380.2 0.0 copy-done
  380.2 0.0 copy-done.1
  380.2 0.0 copy-done.2
  380.2 0.0 copy-done.3
  380.2 0.0 copy-done.4
  380.2 0.0 copy-done.5
  380.2 0.0 copy-done.6
  380.2 0.0 copy-done.7
  380.3 0.0 copy-done.9
  380.3 0.0 copy-done.10
  380.3 0.0 copy-done.11
  380.3 0.0 copy-done.12
  380.3 0.0 copy-done.13
  380.3 0.0 copy-done.14
  380.3 0.0 copy-done.15
  380.3 0.0 copy-done.16
  380.3 0.0 copy-done.17
  380.3 0.0 copy-start.8
  380.4 1.0 copy-done.8
  381.4 8.8 %update.1 = (f32[128,384]{1,0:T(8,128)}, f32[512,128]{1,0:T(8,128)}, f32[128,1024]{1,0:T(8,128)}, f32[128,128]{1,0:T(8,128)}, f32[128,384]{1,0:T(8,128)}, /*inde...) custom-call(bf16[128,2048]{1,0:T(8,128)(2,1)S(1)} %copy-done.8, ...), custom_call_target="tpu_custom_call" | custom-call | tf_op jit(solution)/shard_map/update/pallas_call | solution.py:1623
  390.2 0.0 copy-done.20
  390.2 0.6 fusion
  390.8 0.0 copy-done.19
  390.8 1.1 copy.47
  392.0 0.8 copy-done.18
  392.8 1.1 copy.48
  (5 shorter events, 0.0 us)
Async XLA Ops:
  153.8 160.9 %copy-start.21 = (bf16[1024]{0:T(1024)(128)(2,1)S(1)}, bf16[1024]{0:T(1024)(128)(2,1)}, u32[]{:S(2)}) copy-start(bf16[1024]{0:T(1024)(128)(2,1)} %param.34) | copy-start | bytes 6148
  315.2 64.9 %copy-start = (f32[128,1024]{1,0:T(8,128)S(1)}, f32[128,1024]{1,0:T(8,128)}, u32[]{:S(2)}) copy-start(f32[128,1024]{1,0:T(8,128)} %refs_8_.1) | copy-start | bytes 1572868
  315.2 65.0 %copy-start.1 = (bf16[512,1024]{1,0:T(8,128)(2,1)S(1)}, bf16[512,1024]{1,0:T(8,128)(2,1)}, u32[]{:S(2)}) copy-start(bf16[512,1024]{1,0:T(8,128)(2,1)} %wd_ref.1) | copy-start | bytes 3145732
  315.2 65.0 %copy-start.2 = (f32[128,1024]{1,0:T(8,128)S(1)}, f32[128,1024]{1,0:T(8,128)}, u32[]{:S(2)}) copy-start(f32[128,1024]{1,0:T(8,128)} %refs_9_.1) | copy-start | bytes 1572868
  315.2 65.0 %copy-start.3 = (f32[128,1024]{1,0:T(8,128)S(1)}, f32[128,1024]{1,0:T(8,128)}, u32[]{:S(2)}) copy-start(f32[128,1024]{1,0:T(8,128)} %refs_10_.1) | copy-start | bytes 1572868
  315.2 65.0 %copy-start.4 = (f32[512,128]{1,0:T(8,128)S(1)}, f32[512,128]{1,0:T(8,128)}, u32[]{:S(2)}) copy-start(f32[512,128]{1,0:T(8,128)} %refs_4_.1) | copy-start | bytes 786436
  315.3 65.0 %copy-start.5 = (f32[128,384]{1,0:T(8,128)S(1)}, f32[128,384]{1,0:T(8,128)}, u32[]{:S(2)}) copy-start(f32[128,384]{1,0:T(8,128)} %refs_0_.1) | copy-start | bytes 589828
  315.3 65.0 %copy-start.6 = (f32[128,128]{1,0:T(8,128)S(1)}, f32[128,128]{1,0:T(8,128)}, u32[]{:S(2)}) copy-start(f32[128,128]{1,0:T(8,128)} %refs_12_.1) | copy-start | bytes 196612
  315.3 65.0 %copy-start.7 = (s32[128,1024]{1,0:T(8,128)S(1)}, s32[128,1024]{1,0:T(8,128)}, u32[]{:S(2)}) copy-start(s32[128,1024]{1,0:T(8,128)} %refs_11_.1) | copy-start | bytes 1572868
  315.3 65.0 %copy-start.9 = (f32[128,128]{1,0:T(8,128)S(1)}, f32[128,128]{1,0:T(8,128)}, u32[]{:S(2)}) copy-start(f32[128,128]{1,0:T(8,128)} %refs_13_.1) | copy-start | bytes 196612
  315.3 65.0 %copy-start.10 = (f32[128,128]{1,0:T(8,128)S(1)}, f32[128,128]{1,0:T(8,128)}, u32[]{:S(2)}) copy-start(f32[128,128]{1,0:T(8,128)} %refs_14_.1) | copy-start | bytes 196612
  315.3 65.0 %copy-start.11 = (f32[512,128]{1,0:T(8,128)S(1)}, f32[512,128]{1,0:T(8,128)}, u32[]{:S(2)}) copy-start(f32[512,128]{1,0:T(8,128)} %refs_5_.1) | copy-start | bytes 786436
  315.3 65.0 %copy-start.12 = (f32[512,128]{1,0:T(8,128)S(1)}, f32[512,128]{1,0:T(8,128)}, u32[]{:S(2)}) copy-start(f32[512,128]{1,0:T(8,128)} %refs_6_.1) | copy-start | bytes 786436
  315.3 65.0 %copy-start.13 = (s32[512,128]{1,0:T(8,128)S(1)}, s32[512,128]{1,0:T(8,128)}, u32[]{:S(2)}) copy-start(s32[512,128]{1,0:T(8,128)} %refs_7_.1) | copy-start | bytes 786436
  315.4 65.0 %copy-start.14 = (f32[128,384]{1,0:T(8,128)S(1)}, f32[128,384]{1,0:T(8,128)}, u32[]{:S(2)}) copy-start(f32[128,384]{1,0:T(8,128)} %refs_1_.1) | copy-start | bytes 589828
  315.4 65.0 %copy-start.15 = (f32[128,384]{1,0:T(8,128)S(1)}, f32[128,384]{1,0:T(8,128)}, u32[]{:S(2)}) copy-start(f32[128,384]{1,0:T(8,128)} %refs_2_.1) | copy-start | bytes 589828
  315.4 65.0 %copy-start.16 = (s32[128,384]{1,0:T(8,128)S(1)}, s32[128,384]{1,0:T(8,128)}, u32[]{:S(2)}) copy-start(s32[128,384]{1,0:T(8,128)} %refs_3_.1) | copy-start | bytes 589828
  315.4 65.0 %copy-start.17 = (s32[128,128]{1,0:T(8,128)S(1)}, s32[128,128]{1,0:T(8,128)}, u32[]{:S(2)}) copy-start(s32[128,128]{1,0:T(8,128)} %refs_15_.1) | copy-start | bytes 196612
  380.3 1.0 copy-start.8
  381.4 8.8 %copy-start.20 = (f32[4,1024]{1,0:T(4,128)S(1)}, f32[4,1024]{1,0:T(4,128)}, u32[]{:S(2)}) copy-start(f32[4,1024]{1,0:T(4,128)} %get-tuple-element.97) | copy-start | bytes 49156
  381.4 9.4 %copy-start.19 = (bf16[3,256,1024]{2,1,0:T(8,128)(2,1)S(1)}, bf16[3,256,1024]{2,1,0:T(8,128)(2,1)}, u32[]{:S(2)}) copy-start(bf16[3,256,1024]{2,1,0:T(8,128)(2,1)} %get-tuple-element.134) | copy-start | bytes 4718596
  390.8 2.0 copy-start.18

commit v5 on v4

--- a/solution.py
+++ b/solution.py
@@ -382,10 +382,10 @@
     def project_near(s):
         def side(i, _):
             b = z + s * (2 * i - 1)
-            pl.when((b >= 0) & (b < n))(lambda: project_block(b))
+            pl.when((b >= 0) & (b < n) & ((s > 0) | (i == 0)))(lambda: project_block(b))
             return 0
 
-        lax.fori_loop(0, 2 if s else 1, side, 0)
+        lax.fori_loop(0, 2, side, 0)
 
     def local_products(q, _):
         part = pl.ds(pl.multiple_of(q * span, span), span)
@@ -397,19 +397,28 @@
         dmid_ff_t_ref[q] = dmid.T
         return 0
 
-    project_block(z)
-    pass_on(1)
-    start_own(2)
-    for s in range(2, n):
-        ring_wait(s)
-        if s + 1 < n:
-            ring_start(s + 1)
+    def walk(s, _):
+        @pl.when(s == 1)
+        def _():
+            pass_on(1)
+            start_own(2)
+
+        @pl.when((s > 1) & (s < n))
+        def _():
+            ring_wait(s)
+            pl.when(s + 1 < n)(lambda: ring_start(s + 1))
+
         project_near(s - 1)
-        if s == 2:
+
+        @pl.when(s == 2)
+        def _():
             close(1)
             lax.fori_loop(0, seqs, local_products, 0)
             pass_on(2)
-    project_near(n - 1)
+
+        return 0
+
+    lax.fori_loop(1, n + 1, walk, 0)
     close(2)
     arrived(1)
     arrived(2)
@@ -762,8 +771,9 @@
     step = pl.program_id(0)
     dp, z, y, x, c, core, along_x, along_y = plane()
     peers = [(dp, lax.rem(z + t, n)) for t in range(1, n)]
-    seqs, size, width = x_ref.shape
+    seqs, size, width = o_ref.shape[0], o_ref.shape[2], x_ref.shape[2]
     rows, cols = seqs * size, o_ref.shape[3]
+    blocks = width // cols
     rank = e_ref.shape[0]
     part = rank // n
     lanes = 128
@@ -883,7 +893,7 @@
         first_acc[...] = jnp.zeros_like(first_acc)
         dmid_acc[...] = jnp.zeros_like(dmid_acc)
 
-    @pl.when(step < n)
+    @pl.when(step < blocks)
     def _():
         out = o_ref[...].reshape(rows, cols)
         att_acc[...] += nn(out, wo_ref[...])
@@ -893,7 +903,7 @@
             owner = step * (cols // lanes) + i
             la[owner // 4, lax.rem(owner // 2, 2), lax.rem(owner, 2)] = ga[:, i * lanes : (i + 1) * lanes]
 
-    @pl.when(step == n - 1)
+    @pl.when(step == blocks - 1)
     def _():
         gb = None
         for q in range(seqs):
@@ -903,18 +913,18 @@
         lb[...] = (adapter_scale * gb).astype(bf16)
         late_start(0)
 
-    @pl.when(step >= n)
+    @pl.when((step >= blocks) & (step < 2 * blocks))
     def _():
         dq, dk, dv = (r[...].reshape(rows, cols) for r in (dq_ref, dk_ref, dv_ref))
         first_acc[...] += nt(dq, wq_ref[...]) + nt(dk, wk_ref[...]) + nt(dv, wv_ref[...])
         dmid_acc[...] += nt(dq, bq_ref[...]) + nt(dk, bk_ref[...]) + nt(dv, bv_ref[...])
 
-    @pl.when(step == n + 1)
+    @pl.when(step == blocks)
     def _():
         late_take(0)
         late_start(1)
 
-    @pl.when(step == 2 * n - 1)
+    @pl.when(step == 2 * blocks - 1)
     def _():
         late_take(1)
         late_start(2)
@@ -929,39 +939,43 @@
             for t in range(1, n):
                 e_back(k, t).start()
 
-    @pl.when(step == pl.num_programs(0) - 1)
+    @pl.when(step >= 2 * blocks)
     def _():
-        norm = [jnp.zeros((1, width), f32) for _ in range(4)]
-
-        def sequence(q):
-            at = slice(q * size, (q + 1) * size)
-            x_in = x_ref[q].astype(f32)
-            mid = mid_acc[at].astype(bf16)
-            att = att_acc[at] + bias_ref[...] + adapter_scale * nn(mid, b_out_ref[...])
-            ff = ff_ref[at] + bias_ff_ref[...] + adapter_scale * nn(mid_ff_ref[at], b_ff_ref[...])
-            mixed_ref[q] = (x_in + att + ff).astype(bf16)
-            dmid = (adapter_scale * dmid_acc[at]).astype(bf16)
-            grad_first = first_acc[at] + nt(dmid, a_qkv_ref[...])
-            grad_second = second_ref[at] + nt(dmid_up_ref[at], a_up_ref[...])
-            centre = x_in - jnp.mean(x_in, axis=-1, keepdims=True)
-            inv = lax.rsqrt(jnp.mean(centre * centre, axis=-1, keepdims=True) + norm_eps)
-            unit = centre * inv
-            pulled = grad_first * gain_ref[0:1] + grad_second * gain_ref[1:2]
-            back = inv * (
-                pulled
-                - jnp.mean(pulled, axis=-1, keepdims=True)
-                - unit * jnp.mean(pulled * unit, axis=-1, keepdims=True)
-            )
-            row_grad = cot_ref[q].astype(f32) * weight_ref[at]
-            tokens_ref[q] = (row_grad + back).astype(bf16)
-            for k, value in enumerate((grad_first * unit, grad_second * unit, grad_first, grad_second)):
-                norm[k] += jnp.sum(value, axis=0, keepdims=True)
-
-        sequence(0)
+        q = step - 2 * blocks
+        at = pl.ds(pl.multiple_of(q * size, size), size)
+        x_in = x_ref[0].astype(f32)
+        mid = mid_acc[at, :].astype(bf16)
+        att = att_acc[at, :] + bias_ref[...] + adapter_scale * nn(mid, b_out_ref[...])
+        ff = ff_ref[...] + bias_ff_ref[...] + adapter_scale * nn(mid_ff_ref[at, :], b_ff_ref[...])
+        mixed_ref[0] = (x_in + att + ff).astype(bf16)
+        dmid = (adapter_scale * dmid_acc[at, :]).astype(bf16)
+        grad_first = first_acc[at, :] + nt(dmid, a_qkv_ref[...])
+        grad_second = second_ref[...] + nt(dmid_up_ref[at, :], a_up_ref[...])
+        centre = x_in - jnp.mean(x_in, axis=-1, keepdims=True)
+        inv = lax.rsqrt(jnp.mean(centre * centre, axis=-1, keepdims=True) + norm_eps)
+        unit = centre * inv
+        pulled = grad_first * gain_ref[0:1] + grad_second * gain_ref[1:2]
+        back = inv * (
+            pulled
+            - jnp.mean(pulled, axis=-1, keepdims=True)
+            - unit * jnp.mean(pulled * unit, axis=-1, keepdims=True)
+        )
+        row_grad = cot_ref[0].astype(f32) * weight_ref[at, :]
+        tokens_ref[0] = (row_grad + back).astype(bf16)
+        norm = [
+            jnp.sum(value, axis=0, keepdims=True)
+            for value in (grad_first * unit, grad_second * unit, grad_first, grad_second)
+        ]
+        norm = jnp.concatenate(norm, axis=0)
+        nsum[0] = jnp.where(q == 0, norm, nsum[0] + norm)
+
+    @pl.when(step == 2 * blocks)
+    def _():
         late_take(2)
         both(late_out, lambda copy: copy.start())
-        for q in range(1, seqs - 1):
-            sequence(q)
+
+    @pl.when(step == 2 * blocks + 1)
+    def _():
         both(late_out, lambda copy: copy.wait())
         value = lj[mine, :].astype(f32)
         for t in range(1, n):
@@ -976,8 +990,9 @@
             lbt[mine, :] = value.astype(bf16)
 
         both(late_back, lambda copy: copy.start())
-        sequence(seqs - 1)
-        nsum[0] = jnp.concatenate(norm, axis=0)
+
+    @pl.when(step == pl.num_programs(0) - 1)
+    def _():
         norm_stages[0].start()
         both(late_back, lambda copy: copy.wait())
         for k in range(count):
@@ -1411,40 +1426,46 @@
         def single(shape, *at):
             return pl.BlockSpec(shape, lambda s: at, pipeline_mode=pl.Buffered(1))
 
+        wide_block = width // 2
+
         def of_out(s):
-            return jnp.minimum(s, n - 1)
+            return jnp.minimum(s, 1)
 
         def of_grad(s):
-            return jnp.maximum(s - n, 0)
+            return jnp.clip(s - 2, 0, 1)
+
+        def of_seq(s):
+            return jnp.maximum(s - 4, 0)
 
         def piece_spec(kind, at):
-            return pl.BlockSpec((seqs, 1, span, cz), lambda s: (0, kind, 0, at(s)))
+            return pl.BlockSpec((seqs, 1, span, wide_block), lambda s: (0, kind, 0, at(s)))
 
         def columns(kind, height):
-            return pl.BlockSpec((height, cz), lambda s: (0, kind * n + of_grad(s)))
-
-        full = single((seqs, span, width), 0, 0, 0)
+            return pl.BlockSpec((height, wide_block), lambda s: (0, kind * 2 + of_grad(s)))
+
+        full = pl.BlockSpec((1, span, width), lambda s: (of_seq(s), 0, 0))
+        flat = pl.BlockSpec((span, width), lambda s: (of_seq(s), 0))
         cuts = len(early_cuts)
         b_here = [adapt_b, mean_b, square_b, adapt_b_ff, mean_b_ff, square_b_ff]
         mixed, grad_tokens, reduced, norm_sum, fresh = pl.pallas_call(
             functools.partial(tail_kernel, n=n),
-            grid=(2 * n,),
+            grid=(4 + seqs,),
             in_specs=[
                 piece_spec(0, of_out), piece_spec(1, of_grad), piece_spec(2, of_grad), piece_spec(3, of_grad),
-                pl.BlockSpec((cz, width), lambda s: (of_out(s), 3)),
+                pl.BlockSpec((wide_block, width), lambda s: (of_out(s), 3)),
                 columns(0, width), columns(1, width), columns(2, width),
-                pl.BlockSpec((cz, rank), lambda s: (of_out(s), 1)),
+                pl.BlockSpec((wide_block, rank), lambda s: (of_out(s), 1)),
                 single((width, rank), 0, 0),
                 single((rank, width), 0, 3),
                 columns(0, rank), columns(1, rank), columns(2, rank),
                 single((1, width), 0, 3),
                 full, full,
                 single((rows, 1), 0, 0),
-                single((rows, width), 0, 0),
+                flat,
                 single((1, width), 0, 0),
                 single((rows, rank), 0, 0),
                 single((rank, width), 0, 0),
-                single((rows, width), 0, 0),
+                flat,
                 single((rows, rank), 0, 0),
                 single((width, rank), 0, 2),
                 single((2, width), 0, 0),

time: 401 us -> 382 us (0.953); the launches traced: 394 us -> 381 us
  Pallas kernels: 386 us -> 373 us
    pallas_call x1, Pallas kernels: 161 us -> 151 us  [body(): pl.pallas_call(functools.partial(middle_kernel, n=n, pairs=pairs, steps=s...]
where the time goes in v5:
time: 382 us; the launch traced here: 381 us
  Pallas kernels  373 us (98%)
  local copies, waits for them, and re-layouts  4.87 us (1%)
    pallas_call x1, Pallas kernels, body(): pl.pallas_call(functools.partial(front_kernel, n=n, depth=depth), in_spec...  152 us
    pallas_call x1, Pallas kernels, body(): pl.pallas_call(functools.partial(middle_kernel, n=n, pairs=pairs, steps=s...  151 us
    pallas_call x1, Pallas kernels, body(): pl.pallas_call(functools.partial(tail_kernel, n=n), grid=(4 + seqs,), in_...  61.6 us
    pallas_call x1, Pallas kernels, body(): pl.pallas_call(functools.partial(update_kernel, rank=rank, width=width),...  8.8 us

profile of v5, /device:TPU:0, one launch (start us, length us, event | category | flops | bytes accessed | tf_op | source)
XLA Modules:
  0.0 381.2 jit_solution(13729166275179583127)
XLA Ops:
  0.7 1.3 reshape.52
  2.0 151.8 %front.1 = (bf16[1024,8192]{1,0:T(8,128)(2,1)}, bf16[4096,1024]{1,0:T(8,128)(2,1)}, bf16[1024,384]{1,0:T(8,128)(2,1)}, bf16[4096,128]{1,0:T(8,128)(2,1)}, bf16[1...) custom-call(bf16[3,256,1024]{2,1,0:T(8,128)(2,1)} %x_ref.1, ...), custom_call_target="tpu_custom_call" | custom-call | tf_op jit(solution)/shard_map/front/pallas_call | solution.py:1157
  153.8 0.0 copy-start.21
  153.8 151.2 %middle.1 = (bf16[3,4,256,1024]{3,2,1,0:T(8,128)(2,1)}, f32[768,1024]{1,0:T(8,128)}, f32[768,1024]{1,0:T(8,128)}, bf16[768,128]{1,0:T(8,128)(2,1)}, bf16[768,128]{1,0:T(8,128)(2,1)}, /*index=5*/bf16[128,1920]{1,0:T(8,128)(2,1)}) custom-call(bf16[3,1024,256]{2,1,0:T(8,128)(2,1)} %get-tuple-element.66.q_ref, bf16[3,1024,256]{2,1,0:T(8,128)(2,1)} %get-tuple-element.67.k_ref, ...), custom_call_target="tpu_custom_call" | custom-call | tf_op jit(solution)/shard_map/middle/pallas_call | solution.py:1409
  305.0 0.0 copy-done.21
  305.0 0.6 reshape.54
  305.6 0.0 copy-start
  305.6 0.0 copy-start.1
  305.6 0.0 copy-start.4
  305.6 0.0 copy-start.5
  305.6 0.0 copy-start.6
  305.7 0.0 copy-start.7
  305.7 0.0 copy-start.9
  305.7 0.0 copy-start.10
  305.7 0.0 copy-start.11
  305.7 0.0 copy-start.12
  305.7 0.0 copy-start.13
  305.7 0.0 copy-start.14
  305.7 0.0 copy-start.15
  305.8 0.0 copy-start.16
  305.8 0.0 copy-start.17
  305.8 61.6 %tail.1 = (bf16[3,256,1024]{2,1,0:T(8,128)(2,1)}, bf16[3,256,1024]{2,1,0:T(8,128)(2,1)}, bf16[128,2048]{1,0:T(8,128)(2,1)}, f32[4,1024]{1,0:T(4,128)}, bf16[8,128,1152]{2,1,0:T(8,128)(2,1)}) custom-call(bf16[3,4,256,1024]{3,2,1,0:T(8,128)(2,1)} %get-tuple-element.85.o_ref.dq_ref.dk_ref.dv_ref, ...), custom_call_target="tpu_custom_call" | custom-call | tf_op jit(solution)/shard_map/tail/pallas_call | solution.py:1450
  367.4 0.0 copy-done
  367.4 0.0 copy-done.1
  367.5 0.0 copy-done.2
  367.5 0.0 copy-done.3
  367.5 0.0 copy-done.4
  367.5 0.0 copy-done.5
  367.5 0.0 copy-done.6
  367.5 0.0 copy-done.7
  367.5 0.0 copy-done.9
  367.5 0.0 copy-done.10
  367.5 0.0 copy-done.11
  367.6 0.0 copy-done.12
  367.6 0.0 copy-done.13
  367.6 0.0 copy-done.14
  367.6 0.0 copy-done.15
  367.6 0.0 copy-done.16
  367.6 0.0 copy-done.17
  367.6 0.0 copy-start.8
  367.6 1.0 copy-done.8
  368.7 8.8 %update.1 = (f32[128,384]{1,0:T(8,128)}, f32[512,128]{1,0:T(8,128)}, f32[128,1024]{1,0:T(8,128)}, f32[128,128]{1,0:T(8,128)}, f32[128,384]{1,0:T(8,128)}, /*inde...) custom-call(bf16[128,2048]{1,0:T(8,128)(2,1)S(1)} %copy-done.8, ...), custom_call_target="tpu_custom_call" | custom-call | tf_op jit(solution)/shard_map/update/pallas_call | solution.py:1644
  377.5 0.0 copy-done.20
  377.5 0.6 fusion
  378.1 0.0 copy-done.19
  378.1 1.1 copy.47
  379.2 0.8 copy-done.18
  380.1 1.1 copy.48
  (5 shorter events, 0.0 us)
Async XLA Ops:
  153.8 151.2 %copy-start.21 = (bf16[1024]{0:T(1024)(128)(2,1)S(1)}, bf16[1024]{0:T(1024)(128)(2,1)}, u32[]{:S(2)}) copy-start(bf16[1024]{0:T(1024)(128)(2,1)} %param.34) | copy-start | bytes 6148
  305.6 61.8 %copy-start = (f32[128,1024]{1,0:T(8,128)S(1)}, f32[128,1024]{1,0:T(8,128)}, u32[]{:S(2)}) copy-start(f32[128,1024]{1,0:T(8,128)} %refs_8_.1) | copy-start | bytes 1572868
  305.6 61.8 %copy-start.1 = (bf16[512,1024]{1,0:T(8,128)(2,1)S(1)}, bf16[512,1024]{1,0:T(8,128)(2,1)}, u32[]{:S(2)}) copy-start(bf16[512,1024]{1,0:T(8,128)(2,1)} %wd_ref.1) | copy-start | bytes 3145732
  305.6 61.8 %copy-start.2 = (f32[128,1024]{1,0:T(8,128)S(1)}, f32[128,1024]{1,0:T(8,128)}, u32[]{:S(2)}) copy-start(f32[128,1024]{1,0:T(8,128)} %refs_9_.1) | copy-start | bytes 1572868
  305.6 61.9 %copy-start.3 = (f32[128,1024]{1,0:T(8,128)S(1)}, f32[128,1024]{1,0:T(8,128)}, u32[]{:S(2)}) copy-start(f32[128,1024]{1,0:T(8,128)} %refs_10_.1) | copy-start | bytes 1572868
  305.6 61.9 %copy-start.4 = (f32[512,128]{1,0:T(8,128)S(1)}, f32[512,128]{1,0:T(8,128)}, u32[]{:S(2)}) copy-start(f32[512,128]{1,0:T(8,128)} %refs_4_.1) | copy-start | bytes 786436
  305.6 61.9 %copy-start.5 = (f32[128,384]{1,0:T(8,128)S(1)}, f32[128,384]{1,0:T(8,128)}, u32[]{:S(2)}) copy-start(f32[128,384]{1,0:T(8,128)} %refs_0_.1) | copy-start | bytes 589828
  305.6 61.9 %copy-start.6 = (f32[128,128]{1,0:T(8,128)S(1)}, f32[128,128]{1,0:T(8,128)}, u32[]{:S(2)}) copy-start(f32[128,128]{1,0:T(8,128)} %refs_12_.1) | copy-start | bytes 196612
  305.7 61.9 %copy-start.7 = (s32[128,1024]{1,0:T(8,128)S(1)}, s32[128,1024]{1,0:T(8,128)}, u32[]{:S(2)}) copy-start(s32[128,1024]{1,0:T(8,128)} %refs_11_.1) | copy-start | bytes 1572868
  305.7 61.8 %copy-start.9 = (f32[128,128]{1,0:T(8,128)S(1)}, f32[128,128]{1,0:T(8,128)}, u32[]{:S(2)}) copy-start(f32[128,128]{1,0:T(8,128)} %refs_13_.1) | copy-start | bytes 196612
  305.7 61.8 %copy-start.10 = (f32[128,128]{1,0:T(8,128)S(1)}, f32[128,128]{1,0:T(8,128)}, u32[]{:S(2)}) copy-start(f32[128,128]{1,0:T(8,128)} %refs_14_.1) | copy-start | bytes 196612
  305.7 61.8 %copy-start.11 = (f32[512,128]{1,0:T(8,128)S(1)}, f32[512,128]{1,0:T(8,128)}, u32[]{:S(2)}) copy-start(f32[512,128]{1,0:T(8,128)} %refs_5_.1) | copy-start | bytes 786436
  305.7 61.8 %copy-start.12 = (f32[512,128]{1,0:T(8,128)S(1)}, f32[512,128]{1,0:T(8,128)}, u32[]{:S(2)}) copy-start(f32[512,128]{1,0:T(8,128)} %refs_6_.1) | copy-start | bytes 786436
  305.7 61.8 %copy-start.13 = (s32[512,128]{1,0:T(8,128)S(1)}, s32[512,128]{1,0:T(8,128)}, u32[]{:S(2)}) copy-start(s32[512,128]{1,0:T(8,128)} %refs_7_.1) | copy-start | bytes 786436
  305.7 61.8 %copy-start.14 = (f32[128,384]{1,0:T(8,128)S(1)}, f32[128,384]{1,0:T(8,128)}, u32[]{:S(2)}) copy-start(f32[128,384]{1,0:T(8,128)} %refs_1_.1) | copy-start | bytes 589828
  305.7 61.8 %copy-start.15 = (f32[128,384]{1,0:T(8,128)S(1)}, f32[128,384]{1,0:T(8,128)}, u32[]{:S(2)}) copy-start(f32[128,384]{1,0:T(8,128)} %refs_2_.1) | copy-start | bytes 589828
  305.8 61.8 %copy-start.16 = (s32[128,384]{1,0:T(8,128)S(1)}, s32[128,384]{1,0:T(8,128)}, u32[]{:S(2)}) copy-start(s32[128,384]{1,0:T(8,128)} %refs_3_.1) | copy-start | bytes 589828
  305.8 61.8 %copy-start.17 = (s32[128,128]{1,0:T(8,128)S(1)}, s32[128,128]{1,0:T(8,128)}, u32[]{:S(2)}) copy-start(s32[128,128]{1,0:T(8,128)} %refs_15_.1) | copy-start | bytes 196612
  367.6 1.0 copy-start.8
  368.7 8.8 %copy-start.20 = (f32[4,1024]{1,0:T(4,128)S(1)}, f32[4,1024]{1,0:T(4,128)}, u32[]{:S(2)}) copy-start(f32[4,1024]{1,0:T(4,128)} %get-tuple-element.97) | copy-start | bytes 49156
  368.7 9.4 %copy-start.19 = (bf16[3,256,1024]{2,1,0:T(8,128)(2,1)S(1)}, bf16[3,256,1024]{2,1,0:T(8,128)(2,1)}, u32[]{:S(2)}) copy-start(bf16[3,256,1024]{2,1,0:T(8,128)(2,1)} %get-tuple-element.134) | copy-start | bytes 4718596
  378.1 2.0 copy-start.18

commit v6 on v5

--- a/solution.py
+++ b/solution.py
@@ -458,8 +458,8 @@
     pl.semaphore_wait(barrier, len(peers))
 
 
-early_cuts = ((0, 512), (512, 1024), (1024, 1536), (1536, 1920))
-late_end, a_ff_at, b_at_col, early_end = 256, 384, 896, 1920
+early_cuts = ((0, 512), (512, 1024), (1024, 1536), (1536, 2048))
+late_end, a_out_at, a_ff_at, b_at_col, early_end = 256, 384, 512, 1024, 2048
 
 
 class PlaneSum:
@@ -543,9 +543,11 @@
     n, pairs, steps, depth, early,
 ):
     if early:
-        first_ref, mid_qkv_ref, local_ref, ff_ref, back_ref, mid_ff_ref, dmid_up_ref, sum_ref = refs[:8]
-        buffer, dk_ref, dv_ref, mid_acc, dmid_acc, send_sem, recv_sem, own_sem = refs[8:16]
-        e_ref, dmid_seq, gb_acc, ga_acc = refs[16:20]
+        first_ref, mid_qkv_ref, a_out_ref, dmid_out_t_ref = refs[:4]
+        refs = refs[4:]
+        local_ref, ff_ref, back_ref, mid_ff_ref, dmid_up_ref, sum_ref = refs[:6]
+        buffer, dk_ref, dv_ref, mid_acc, dmid_acc, send_sem, recv_sem, own_sem = refs[6:14]
+        e_ref, dmid_seq, gb_acc, ga_acc, o_here, load_sem = refs[14:20]
         plane_refs = refs[20:]
     else:
         local_ref, own_ref, ff_ref, back_ref, mid_ff_ref, dmid_up_ref, ga_ref, gb_ref = refs[:8]
@@ -561,18 +563,30 @@
     if early:
         plane_sum = PlaneSum(e_ref, *plane_refs)
 
-    def copies(s):
+    def copies(kind, s):
         seq, pair = s // pairs, lax.rem(s, pairs)
+        what = slice(1, 4) if kind else slice(0, 1)
         at = pl.ds(pl.multiple_of((z * pairs + pair) * lanes, lanes), lanes)
-        target = local_ref.at[seq, :, :, at]
-        own = pltpu.make_async_copy(buffer.at[s, z], target, own_sem.at[s])
+        target = local_ref.at[seq, what, :, at]
+        own = pltpu.make_async_copy(buffer.at[s, z, what], target, own_sem.at[kind, s])
         away = []
         for t in range(1, n):
             peer = lax.rem(z + t, n)
             away.append(
-                remote(buffer.at[s, peer], target, send_sem.at[s, t], recv_sem.at[s, t], (dp, peer))
+                remote(
+                    buffer.at[s, peer, what], target, send_sem.at[kind, s, t], recv_sem.at[kind, s, t], (dp, peer)
+                )
             )
-        return own, away
+        return [own] + away
+
+    def send(kind, s):
+        for copy in copies(kind, s):
+            copy.start()
+
+    def receive(kind):
+        for s in range(steps):
+            for copy in copies(kind, s):
+                copy.wait()
 
     @pl.when(step == 0)
     def _():
@@ -588,10 +602,9 @@
 
         tables = keep_ref[...], above_ref[...], below_ref[...]
         attend_pair(q_ref[0], k_ref[0], v_ref[0], g_ref[0], tables, dk_ref, dv_ref, depth, n, store)
-        own, away = copies(step)
-        own.start()
-        for copy in away:
-            copy.start()
+        send(0, step)
+        pl.when(step == 0)(lambda: send(1, 0))
+        pl.when(step == steps - 2)(lambda: send(1, 1))
         if early:
             seq, pair = step // pairs, lax.rem(step, pairs)
             mid_t = mid_qkv_ref[0].T
@@ -612,6 +625,8 @@
 
     @pl.when(step == steps)
     def _():
+        for s in range(2, steps):
+            send(1, s)
         ff_ref[...] = jnp.zeros_like(ff_ref)
         back_ref[...] = jnp.zeros_like(back_ref)
         mid_acc[...] = jnp.zeros_like(mid_acc)
@@ -619,10 +634,10 @@
         if early:
             for owner in range(8):
                 place = (owner // 4, owner // 2 % 2, owner % 2)
-                e_ref[place + (slice(None), slice(late_end, a_ff_at))] = ga_acc[
+                e_ref[place + (slice(None), slice(late_end, a_out_at))] = ga_acc[
                     :, owner * lanes : (owner + 1) * lanes
                 ].astype(bf16)
-                if owner < 4:
+                if owner < 3:
                     e_ref[place + (slice(None), slice(b_at_col, early_end))] = jnp.zeros((lanes, 1024), bf16)
             for t in range(3):
                 for pair in range(pairs):
@@ -658,14 +673,31 @@
             e_ref[j // 4, lax.rem(j // 2, 2), lax.rem(j, 2), :, a_ff_at:b_at_col] = ga.astype(bf16)
             at = pl.ds(pl.multiple_of(b_at_col + lax.rem(j, 2) * inner_block, lanes), inner_block)
             e_ref[1, j // 4, lax.rem(j // 2, 2), :, at] = (adapter_scale * gb).astype(bf16)
-            for m in range(3):
-
-                @pl.when(j == 2 * m + 3)
-                def _(m=m):
-                    plane_sum.take_first(m)
-
-            for m in range(4):
-                pl.when(j == 2 * m + 1)(lambda m=m: plane_sum.first(m).start())
+
+            @pl.when(j == 2)
+            def _():
+                receive(0)
+                load = pltpu.make_async_copy(local_ref.at[:, 0], o_here, load_sem.at[0])
+                load.start()
+                load.wait()
+                ga_out, gb_out = None, None
+                for q in range(count):
+                    rows = slice(q * size, (q + 1) * size)
+                    out = o_here[q]
+                    mid = nn(out, a_out_ref[...]).astype(bf16)
+                    ga_part = nn(dmid_out_t_ref[q], out)
+                    gb_part = nn(mid.T, low_ref[rows])
+                    ga_out = ga_part if ga_out is None else ga_out + ga_part
+                    gb_out = gb_part if gb_out is None else gb_out + gb_part
+                e_ref[0, 1, 1, :, b_at_col:early_end] = (adapter_scale * gb_out).astype(bf16)
+                for owner in range(8):
+                    at = slice(owner * lanes, (owner + 1) * lanes)
+                    e_ref[owner // 4, owner // 2 % 2, owner % 2, :, a_out_at:a_ff_at] = ga_out[:, at].astype(bf16)
+
+            for m, (begin, take) in enumerate(((3, 5), (4, 6), (5, 7))):
+                pl.when(j == begin)(lambda m=m: plane_sum.first(m).start())
+                pl.when(j == take)(lambda m=m: plane_sum.take_first(m))
+            pl.when(j == 7)(lambda: plane_sum.first(3).start())
         else:
             ga_ref[...] = ga
             gb_ref[...] = gb
@@ -692,11 +724,9 @@
             plane_sum.take_first(3)
             plane_sum.take_first(4)
             plane_sum.finish(sum_ref)
-        for s in range(steps):
-            own, away = copies(s)
-            own.wait()
-            for copy in away:
-                copy.wait()
+        if not early:
+            receive(0)
+        receive(1)
 
 
 def finish_kernel(
@@ -760,12 +790,12 @@
 def tail_kernel(
     o_ref, dq_ref, dk_ref, dv_ref, wo_ref, wq_ref, wk_ref, wv_ref, a_out_ref, a_qkv_ref, b_out_ref,
     bq_ref, bk_ref, bv_ref, bias_ref, x_ref, cot_ref, weight_ref, ff_ref, bias_ff_ref, mid_ff_ref, b_ff_ref,
-    second_ref, dmid_up_ref, a_up_ref, gain_ref, dmid_out_t_ref, low_ref,
+    second_ref, dmid_up_ref, a_up_ref, gain_ref,
     e_ref, b_ref, mean_ref, square_ref, bf_ref, mean_f_ref, square_f_ref,
     mixed_ref, tokens_ref, out_hbm, norm_ref, fresh_hbm,
     out_ref, fresh_ref, att_acc, mid_acc, first_acc, dmid_acc,
-    r4, la, lb, lr1, lr2, lr3, lbr, lj, lr4, lbr4, lbt, nr, nsum,
-    s4, q4, s5, q5, sl, ql, sl4, ql4, sl5, ql5, sn, qn, sg, qg, done_sem,
+    r4, nr, nsum,
+    s4, q4, s5, q5, sf, qf, sn, qn, sg, qg, done_sem,
     *, n,
 ):
     step = pl.program_id(0)
@@ -773,12 +803,13 @@
     peers = [(dp, lax.rem(z + t, n)) for t in range(1, n)]
     seqs, size, width = o_ref.shape[0], o_ref.shape[2], x_ref.shape[2]
     rows, cols = seqs * size, o_ref.shape[3]
-    blocks = width // cols
+    outs = width // cols
+    grads = width // dq_ref.shape[3]
+    first_seq = outs + grads
     rank = e_ref.shape[0]
     part = rank // n
     lanes = 128
     mine = pl.ds(pl.multiple_of(z * part, part), part)
-    late = slice(early_end, early_end + lanes)
 
     def to_part(t):
         return pl.ds(pl.multiple_of(lax.rem(z + t, n) * part, part), part)
@@ -793,60 +824,8 @@
 
     count = len(early_cuts)
 
-    has_b = (c == 1, (c == 1) & (x == 1), dp == 3)
-    gives_b = (c == 0, (c == 1) & (x == 0), (c == 1) & (x == 1) & (y == 1))
-
-    def late_a(i):
-        src, dst, peer = [
-            (la.at[:, :, 1 - c], lr1, core),
-            (la.at[:, 1 - x, c], lr2, along_x),
-            (la.at[1 - y, x, c], lr3, along_y),
-        ][i]
-        return remote(src, dst, sl.at[0, i], ql.at[0, i], peer)
-
-    def late_b(i):
-        return remote(lb, lbr.at[i], sl.at[1, i], ql.at[1, i], (core, along_x, along_y)[i])
-
-    def late_start(i):
-        late_a(i).start()
-        pl.when(gives_b[i])(lambda: late_b(i).start())
-
-    def late_take(i):
-        late_a(i).wait()
-        pl.when(gives_b[i])(lambda: late_b(i).wait_send())
-
-        @pl.when(has_b[i])
-        def _():
-            late_b(i).wait_recv()
-            lb[...] = add_low(lb[...], lbr[i])
-
-        if i == 0:
-            for yy in range(2):
-                for xx in range(2):
-                    la[yy, xx, c] = add_low(la[yy, xx, c], lr1[yy, xx])
-        elif i == 1:
-            for yy in range(2):
-                la[yy, x, c] = add_low(la[yy, x, c], lr2[yy])
-        else:
-            lj[...] = add_low(la[y, x, c], lr3[...])
-
-    def late_out(t):
-        return (
-            remote(lj.at[to_part(t), :], lr4.at[t], sl4.at[0, t], ql4.at[0, t], peers[t - 1]),
-            remote(lb.at[to_part(t), :], lbr4.at[t], sl4.at[1, t], ql4.at[1, t], peers[t - 1]),
-        )
-
-    def late_back(t):
-        return (
-            remote(out_ref.at[mine, late], out_ref.at[mine, late], sl5.at[0, t], ql5.at[0, t], peers[t - 1]),
-            remote(lbt.at[mine, :], lbt.at[mine, :], sl5.at[1, t], ql5.at[1, t], peers[t - 1]),
-        )
-
-    def both(make, act):
-        for t in range(1, n):
-            a, b = make(t)
-            act(a)
-            pl.when(dp == 3)(lambda b=b: act(b))
+    def fresh_back(t):
+        return remote(fresh_ref.at[dp, mine, :], fresh_ref.at[dp, mine, :], sf.at[t], qf.at[t], peers[t - 1])
 
     from_x, from_y, from_c = along_x[0], along_y[0], core[0]
     across = from_x + from_y - dp
@@ -858,17 +837,19 @@
         (from_x, from_x + other, core), (from_y, from_y + other, core), (across, across + other, core),
     ]
 
-    def gather(kind):
+    middle_row = rank // 2
+    parts = (slice(0, middle_row), slice(middle_row, rank))
+
+    def gather(kind, p):
         slot, _, peer = hops[kind]
-        return remote(fresh_ref.at[slot], fresh_ref.at[slot], sg.at[kind], qg.at[kind], peer)
-
-    def make_fresh():
+        there = fresh_ref.at[slot, parts[p], :]
+        return remote(there, there, sg.at[p, kind], qg.at[p, kind], peer)
+
+    def fresh_rows(value, grad_b):
         cut = b_ref.shape[1]
-        grads = out_ref[:, b_at_col:early_end].astype(f32)
-        new_b = adam_fresh(b_ref[...], grads, mean_ref[...], square_ref[...])
-        grads = out_ref[:, lanes:late_end].astype(f32)
-        new_f = adam_fresh(bf_ref[...], grads, mean_f_ref[...], square_f_ref[...])
-        fresh_ref[dp] = jnp.concatenate([new_b, new_f], axis=1).astype(bf16)
+        new_b = adam_fresh(b_ref[mine, :], grad_b, mean_ref[mine, :], square_ref[mine, :])
+        new_f = adam_fresh(bf_ref[mine, :], value, mean_f_ref[mine, :], square_f_ref[mine, :])
+        fresh_ref[dp, mine, :] = jnp.concatenate([new_b, new_f], axis=1).astype(bf16)
 
     def norm_copy(i, peer):
         return remote(nsum.at[i], nr.at[i], sn.at[i], qn.at[i], peer)
@@ -893,41 +874,20 @@
         first_acc[...] = jnp.zeros_like(first_acc)
         dmid_acc[...] = jnp.zeros_like(dmid_acc)
 
-    @pl.when(step < blocks)
+    @pl.when(step < outs)
     def _():
         out = o_ref[...].reshape(rows, cols)
         att_acc[...] += nn(out, wo_ref[...])
         mid_acc[...] += nn(out, a_out_ref[...])
-        ga = sum(nn(dmid_out_t_ref[q], out[q * size : (q + 1) * size]) for q in range(seqs)).astype(bf16)
-        for i in range(cols // lanes):
-            owner = step * (cols // lanes) + i
-            la[owner // 4, lax.rem(owner // 2, 2), lax.rem(owner, 2)] = ga[:, i * lanes : (i + 1) * lanes]
-
-    @pl.when(step == blocks - 1)
+
+    @pl.when((step >= outs) & (step < first_seq))
     def _():
-        gb = None
-        for q in range(seqs):
-            at = slice(q * size, (q + 1) * size)
-            product = nn(mid_acc[at].astype(bf16).T, low_ref[at])
-            gb = product if gb is None else gb + product
-        lb[...] = (adapter_scale * gb).astype(bf16)
-        late_start(0)
-
-    @pl.when((step >= blocks) & (step < 2 * blocks))
-    def _():
-        dq, dk, dv = (r[...].reshape(rows, cols) for r in (dq_ref, dk_ref, dv_ref))
+        dq, dk, dv = (r[...].reshape(rows, r.shape[3]) for r in (dq_ref, dk_ref, dv_ref))
         first_acc[...] += nt(dq, wq_ref[...]) + nt(dk, wk_ref[...]) + nt(dv, wv_ref[...])
         dmid_acc[...] += nt(dq, bq_ref[...]) + nt(dk, bk_ref[...]) + nt(dv, bv_ref[...])
 
-    @pl.when(step == blocks)
+    @pl.when(step == outs)
     def _():
-        late_take(0)
-        late_start(1)
-
-    @pl.when(step == 2 * blocks - 1)
-    def _():
-        late_take(1)
-        late_start(2)
         for k in range(count):
             cut = slice(*early_cuts[k])
             for t in range(1, n):
@@ -936,12 +896,24 @@
             for t in range(1, n):
                 value += r4[t, :, cut].astype(f32)
             out_ref[mine, cut] = value.astype(bf16)
+        fresh_rows(out_ref[mine, lanes:late_end].astype(f32), out_ref[mine, b_at_col:early_end].astype(f32))
+        for t in range(1, n):
+            fresh_back(t).start()
+
+    @pl.when(step == first_seq - 1)
+    def _():
+        for t in range(1, n):
+            fresh_back(t).wait()
+        for p in range(2):
+            for kind in (0, 1, 2):
+                gather(kind, p).start()
+        for k in range(count):
             for t in range(1, n):
                 e_back(k, t).start()
 
-    @pl.when(step >= 2 * blocks)
+    @pl.when(step >= first_seq)
     def _():
-        q = step - 2 * blocks
+        q = step - first_seq
         at = pl.ds(pl.multiple_of(q * size, size), size)
         x_in = x_ref[0].astype(f32)
         mid = mid_acc[at, :].astype(bf16)
@@ -969,64 +941,36 @@
         norm = jnp.concatenate(norm, axis=0)
         nsum[0] = jnp.where(q == 0, norm, nsum[0] + norm)
 
-    @pl.when(step == 2 * blocks)
-    def _():
-        late_take(2)
-        both(late_out, lambda copy: copy.start())
-
-    @pl.when(step == 2 * blocks + 1)
-    def _():
-        both(late_out, lambda copy: copy.wait())
-        value = lj[mine, :].astype(f32)
-        for t in range(1, n):
-            value += lr4[t].astype(f32)
-        out_ref[mine, late] = value.astype(bf16)
-
-        @pl.when(dp == 3)
-        def _():
-            value = lb[mine, :].astype(f32)
-            for t in range(1, n):
-                value += lbr4[t].astype(f32)
-            lbt[mine, :] = value.astype(bf16)
-
-        both(late_back, lambda copy: copy.start())
-
     @pl.when(step == pl.num_programs(0) - 1)
     def _():
         norm_stages[0].start()
-        both(late_back, lambda copy: copy.wait())
+        for p in range(2):
+            gather(0, p).wait_recv()
+            gather(1, p).wait_recv()
+            for kind in (3, 4, 5):
+                gather(kind, p).start()
+            norm_take(p)
+            norm_stages[p + 1].start()
+        for p in range(2):
+            gather(3, p).wait_recv()
+            gather(6, p).start()
+        norm_take(2)
+        for copy in norm_last:
+            copy.start()
         for k in range(count):
             for t in range(1, n):
                 e_back(k, t).wait()
 
-        @pl.when(dp == 3)
-        def _():
-            out_ref[:, b_at_col:early_end] = lbt[...]
-
-        make_fresh()
-        for kind in (0, 1, 2):
-            gather(kind).start()
         keep_out = pltpu.make_async_copy(out_ref, out_hbm, done_sem.at[0])
         keep_out.start()
-        norm_take(0)
-        norm_stages[1].start()
-        gather(0).wait_recv()
-        gather(1).wait_recv()
-        for kind in (3, 4, 5):
-            gather(kind).start()
-        norm_take(1)
-        norm_stages[2].start()
-        gather(3).wait_recv()
-        gather(6).start()
-        norm_take(2)
-        for copy in norm_last:
-            copy.start()
-        for kind in (2, 4, 5, 6):
-            gather(kind).wait_recv()
+        for p in range(2):
+            for kind in (2, 4, 5, 6):
+                gather(kind, p).wait_recv()
         keep_fresh = pltpu.make_async_copy(fresh_ref, fresh_hbm, done_sem.at[1])
         keep_fresh.start()
-        for kind in range(7):
-            gather(kind).wait_send()
+        for p in range(2):
+            for kind in range(7):
+                gather(kind, p).wait_send()
         for copy in norm_last:
             copy.wait()
         keep_out.wait()
@@ -1053,8 +997,8 @@
         cut, cut_f = params[8].shape[1], params[12].shape[1]
         up = got[:, :rows]
         qkv = got[:, rows + cut_f : 2 * rows + cut_f]
-        out = got[:, 2 * rows + cut_f + inner + cut :]
-        at = 2 * rows + cut_f
+        out = got[:, 2 * rows + cut_f : 3 * rows + cut_f]
+        at = 3 * rows + cut_f
         grads = [
             jnp.concatenate([part.T for part in (qkv, out, up)], axis=1),
             got[:, at : at + inner].T,
@@ -1077,10 +1021,14 @@
                 else:
                     aff_new[...] = fresh.astype(bf16)
 
-    block = jnp.where(j * cols < 3 * width, 0, jnp.where(j * cols < 4 * width, 1, 2))
     cut = params[8].shape[1]
     fresh = [fresh_ref[i] for i in range(fresh_ref.shape[0])]
-    update = nn(a_new[block], jnp.concatenate([f[:, :cut] for f in fresh], axis=1))
+    update = []
+    for i, part in enumerate(fresh):
+        at = j * cols + i * cut
+        block = jnp.where(at < 3 * width, 0, jnp.where(at < 4 * width, 1, 2))
+        update.append(nn(a_new[block], part[:, :cut]))
+    update = jnp.concatenate(update, axis=1)
     outs[12][...] = (w_ref[...].astype(f32) + adapter_scale * update).astype(bf16)
     update = nn(aff_new[...], jnp.concatenate([f[:, cut:] for f in fresh], axis=1))
     outs[13][...] = (wd_ref[...].astype(f32) + adapter_scale * update).astype(bf16)
@@ -1372,16 +1320,20 @@
         pltpu.VMEM((length, lanes), f32),
         pltpu.VMEM((rows, rank), f32),
         pltpu.VMEM((rows, rank), f32),
-        dma((steps, n)),
-        dma((steps, n)),
-        dma((steps,)),
+        dma((2, steps, n)),
+        dma((2, steps, n)),
+        dma((2, steps)),
     ]
     if early:
         in_specs += [
             pl.BlockSpec((1, length, width), lambda s: (seq_pair(s)[0], 0, 0)),
             pl.BlockSpec((1, length, rank), lambda s: (seq_pair(s)[0], 0, 0)),
         ]
-        operands += [first_pos, mid_pos]
+        in_specs += [
+            pl.BlockSpec((width, rank), lambda s: (0, 1), pipeline_mode=pl.Buffered(1)),
+            one_buffer((seqs, rank, span)),
+        ]
+        operands += [first_pos, mid_pos, a_all, dmid_out_t]
         out_specs = [local_spec] + partial_specs + [one_buffer((rank, early_end))]
         out_shapes = [local_shape] + partial_shapes + [wide(rank, early_end)]
         cuts = len(early_cuts)
@@ -1390,6 +1342,8 @@
             pltpu.VMEM((length, rank), f32),
             pltpu.VMEM((3, pairs, rank, lanes), f32),
             pltpu.VMEM((rank, width), f32),
+            pltpu.VMEM((seqs, span, width), bf16),
+            dma((1,)),
             pltpu.VMEM((2, 2, rank, early_end), bf16),
             pltpu.VMEM((2, half_rank, early_end), bf16),
             pltpu.VMEM((2, half_rank, early_end), bf16),
@@ -1432,16 +1386,16 @@
             return jnp.minimum(s, 1)
 
         def of_grad(s):
-            return jnp.clip(s - 2, 0, 1)
+            return jnp.clip(s - 2, 0, n - 1)
 
         def of_seq(s):
-            return jnp.maximum(s - 4, 0)
-
-        def piece_spec(kind, at):
-            return pl.BlockSpec((seqs, 1, span, wide_block), lambda s: (0, kind, 0, at(s)))
+            return jnp.maximum(s - 2 - n, 0)
+
+        def piece_spec(kind):
+            return pl.BlockSpec((seqs, 1, span, cz), lambda s: (0, kind, 0, of_grad(s)))
 
         def columns(kind, height):
-            return pl.BlockSpec((height, wide_block), lambda s: (0, kind * 2 + of_grad(s)))
+            return pl.BlockSpec((height, cz), lambda s: (0, kind * n + of_grad(s)))
 
         full = pl.BlockSpec((1, span, width), lambda s: (of_seq(s), 0, 0))
         flat = pl.BlockSpec((span, width), lambda s: (of_seq(s), 0))
@@ -1449,9 +1403,10 @@
         b_here = [adapt_b, mean_b, square_b, adapt_b_ff, mean_b_ff, square_b_ff]
         mixed, grad_tokens, reduced, norm_sum, fresh = pl.pallas_call(
             functools.partial(tail_kernel, n=n),
-            grid=(4 + seqs,),
+            grid=(2 + n + seqs,),
             in_specs=[
-                piece_spec(0, of_out), piece_spec(1, of_grad), piece_spec(2, of_grad), piece_spec(3, of_grad),
+                pl.BlockSpec((seqs, 1, span, wide_block), lambda s: (0, 0, 0, of_out(s))),
+                piece_spec(1), piece_spec(2), piece_spec(3),
                 pl.BlockSpec((wide_block, width), lambda s: (of_out(s), 3)),
                 columns(0, width), columns(1, width), columns(2, width),
                 pl.BlockSpec((wide_block, rank), lambda s: (of_out(s), 1)),
@@ -1469,8 +1424,6 @@
                 single((rows, rank), 0, 0),
                 single((width, rank), 0, 2),
                 single((2, width), 0, 0),
-                single((seqs, rank, span), 0, 0, 0),
-                single((rows, width), 0, 0),
                 single((rank, early_end), 0, 0),
             ]
             + [single(v.shape, 0, 0) for v in b_here],
@@ -1490,21 +1443,10 @@
                 pltpu.VMEM((rows, width), f32),
                 pltpu.VMEM((rows, rank), f32),
                 pltpu.VMEM((n, part, early_end), bf16),
-                pltpu.VMEM((2, 2, 2, rank, lanes), bf16),
-                pltpu.VMEM((rank, width), bf16),
-                pltpu.VMEM((2, 2, rank, lanes), bf16),
-                pltpu.VMEM((2, rank, lanes), bf16),
-                pltpu.VMEM((rank, lanes), bf16),
-                pltpu.VMEM((3, rank, width), bf16),
-                pltpu.VMEM((rank, lanes), bf16),
-                pltpu.VMEM((n, part, lanes), bf16),
-                pltpu.VMEM((n, part, width), bf16),
-                pltpu.VMEM((rank, width), bf16),
                 pltpu.VMEM((2 + n, 4, width), f32),
                 pltpu.VMEM((4, 4, width), f32),
-                dma((n, cuts)), dma((n, cuts)), dma((n, cuts)), dma((n, cuts)),
-                dma((2, 3)), dma((2, 3)), dma((2, n)), dma((2, n)), dma((2, n)), dma((2, n)),
-                dma((2 + n,)), dma((2 + n,)), dma((7,)), dma((7,)), dma((2,)),
+                dma((n, cuts)), dma((n, cuts)), dma((n, cuts)), dma((n, cuts)), dma((n,)), dma((n,)),
+                dma((2 + n,)), dma((2 + n,)), dma((2, 7)), dma((2, 7)), dma((2,)),
             ],
             compiler_params=pltpu.CompilerParams(
                 collective_id=1, has_side_effects=True, vmem_limit_bytes=58 << 20
@@ -1513,7 +1455,7 @@
         )(
             local, local, local, local, w_in, w_in, w_in, w_in, a_all, a_all, b_in, b_in, b_in, b_in,
             bias32.reshape(1, -1), tokens, cotangent, row_weight, ff, bias_ff.astype(f32).reshape(1, -1), mid_ff, b_ff,
-            grad_second, dmid_up, a_all, norm_gain, dmid_out_t, grad_low, summed, *b_here,
+            grad_second, dmid_up, a_all, norm_gain, summed, *b_here,
         )
     else:
         local, own, ff, grad_second, mid_ff, dmid_up, grad_a_ff_t, grad_b_up = middle
@@ -1603,12 +1545,12 @@
             return values.reshape(rank, dp_n, -1)
 
         parts = [
-            by_owner(grad_a_up_t), by_owner(grad_b_ffp), by_owner(grad_a_qkv_t), by_owner(grad_a_ff_t),
-            by_owner(jnp.concatenate([grad_b_qkv, grad_b_out, grad_b_up], axis=1)), by_owner(grad_a_out_t),
+            by_owner(grad_a_up_t), by_owner(grad_b_ffp), by_owner(grad_a_qkv_t), by_owner(grad_a_out_t),
+            by_owner(grad_a_ff_t), by_owner(jnp.concatenate([grad_b_qkv, grad_b_out, grad_b_up], axis=1)),
         ]
         widths = [p.shape[2] for p in parts]
         owned = jnp.transpose(jnp.concatenate([p.astype(bf16) for p in parts], axis=2), (1, 0, 2))
-        b_at = sum(widths[:4])
+        b_at = sum(widths[:5])
         reduced = lax.psum_scatter(owned.astype(f32), "dp", scatter_dimension=0, tiled=True)
         reduced = lax.psum(reduced[0], "blk").astype(bf16)
         norm_sum = lax.psum(norm_part, ("dp", "blk"))
@@ -1638,7 +1580,7 @@
     four = [adapt_a, adapt_a_ff, adapt_b, adapt_b_ff]
     results = [v for v in four] + [v for v in four for _ in range(2)]
     b_w, f_w = adapt_b.shape[1], adapt_b_ff.shape[1]
-    owners = max(1, lanes // f_w)
+    owners = max(4, lanes // f_w)
     w_spec = pl.BlockSpec((kr, owners * b_w), lambda j: (0, j))
     wd_spec = pl.BlockSpec((down_rows, owners * f_w), lambda j: (0, j))
     updated = pl.pallas_call(

time: 382 us -> 375 us (0.982)
  Pallas kernels: 373 us -> 367 us
    pallas_call x1, Pallas kernels: 61.6 us -> 54.7 us  [body(): pl.pallas_call(functools.partial(tail_kernel, n=n), grid=(2 + n + seqs,),...]
    pallas_call x1, Pallas kernels: 151 us -> 155 us  [body(): pl.pallas_call(functools.partial(middle_kernel, n=n, pairs=pairs, steps=s...]
where the time goes in v6:
time: 375 us
  Pallas kernels  367 us (98%)
  local copies, waits for them, and re-layouts  4.87 us (1%)
    pallas_call x1, Pallas kernels, body(): pl.pallas_call(functools.partial(middle_kernel, n=n, pairs=pairs, steps=s...  155 us
    pallas_call x1, Pallas kernels, body(): pl.pallas_call(functools.partial(front_kernel, n=n, depth=depth), in_spec...  152 us
    pallas_call x1, Pallas kernels, body(): pl.pallas_call(functools.partial(tail_kernel, n=n), grid=(2 + n + seqs,),...  54.7 us

profile of v6, /device:TPU:0, one launch (start us, length us, event | category | flops | bytes accessed | tf_op | source)
XLA Modules:
  0.0 375.1 jit_solution(5694658543856296445)
XLA Ops:
  0.7 1.3 reshape.52
  2.0 151.9 %front.1 = (bf16[1024,8192]{1,0:T(8,128)(2,1)}, bf16[4096,1024]{1,0:T(8,128)(2,1)}, bf16[1024,384]{1,0:T(8,128)(2,1)}, bf16[4096,128]{1,0:T(8,128)(2,1)}, bf16[1...) custom-call(bf16[3,256,1024]{2,1,0:T(8,128)(2,1)} %x_ref.1, ...), custom_call_target="tpu_custom_call" | custom-call | tf_op jit(solution)/shard_map/front/pallas_call | solution.py:1105
  153.9 0.0 copy-start.21
  153.9 155.1 %middle.1 = (bf16[3,4,256,1024]{3,2,1,0:T(8,128)(2,1)}, f32[768,1024]{1,0:T(8,128)}, f32[768,1024]{1,0:T(8,128)}, bf16[768,128]{1,0:T(8,128)(2,1)}, bf16[768,128]{1,0:T(8,128)(2,1)}, /*index=5*/bf16[128,2048]{1,0:T(8,128)(2,1)}) custom-call(bf16[3,1024,256]{2,1,0:T(8,128)(2,1)} %get-tuple-element.66.q_ref, bf16[3,1024,256]{2,1,0:T(8,128)(2,1)} %get-tuple-element.67.k_ref, ...), custom_call_target="tpu_custom_call" | custom-call | tf_op jit(solution)/shard_map/middle/pallas_call | solution.py:1363
  308.9 0.0 copy-done.21
  309.0 0.6 reshape.54
  309.6 0.0 copy-start
  309.6 0.0 copy-start.1
  309.6 0.0 copy-start.4
  309.6 0.0 copy-start.5
  309.6 0.0 copy-start.6
  309.6 0.0 copy-start.7
  309.6 0.0 copy-start.9
  309.6 0.0 copy-start.10
  309.6 0.0 copy-start.11
  309.6 0.0 copy-start.12
  309.7 0.0 copy-start.13
  309.7 0.0 copy-start.14
  309.7 0.0 copy-start.15
  309.7 0.0 copy-start.16
  309.7 0.0 copy-start.17
  309.7 54.7 %tail.1 = (bf16[3,256,1024]{2,1,0:T(8,128)(2,1)}, bf16[3,256,1024]{2,1,0:T(8,128)(2,1)}, bf16[128,2048]{1,0:T(8,128)(2,1)}, f32[4,1024]{1,0:T(4,128)}, bf16[8,128,1152]{2,1,0:T(8,128)(2,1)}) custom-call(bf16[3,4,256,1024]{3,2,1,0:T(8,128)(2,1)} %get-tuple-element.87.o_ref.dq_ref.dk_ref.dv_ref, ...), custom_call_target="tpu_custom_call" | custom-call | tf_op jit(solution)/shard_map/tail/pallas_call | solution.py:1404
  364.4 0.0 copy-done
  364.4 0.0 copy-done.1
  364.4 0.0 copy-done.2
  364.4 0.0 copy-done.3
  364.4 0.0 copy-done.4
  364.5 0.0 copy-done.5
  364.5 0.0 copy-done.6
  364.5 0.0 copy-done.7
  364.5 0.0 copy-done.9
  364.5 0.0 copy-done.10
  364.5 0.0 copy-done.11
  364.5 0.0 copy-done.12
  364.5 0.0 copy-done.13
  364.5 0.0 copy-done.14
  364.6 0.0 copy-done.15
  364.6 0.0 copy-done.16
  364.6 0.0 copy-done.17
  364.6 0.0 copy-start.8
  364.6 1.0 copy-done.8
  365.6 5.8 %update.1 = (f32[128,384]{1,0:T(8,128)}, f32[512,128]{1,0:T(8,128)}, f32[128,1024]{1,0:T(8,128)}, f32[128,128]{1,0:T(8,128)}, f32[128,384]{1,0:T(8,128)}, /*inde...) custom-call(bf16[128,2048]{1,0:T(8,128)(2,1)S(1)} %copy-done.8, ...), custom_call_target="tpu_custom_call" | custom-call | tf_op jit(solution)/shard_map/update/pallas_call | solution.py:1586
  371.4 0.0 copy-done.20
  371.4 0.6 fusion
  372.0 0.0 copy-done.19
  372.0 1.1 copy.47
  373.1 0.8 copy-done.18
  374.0 1.1 copy.48
  (5 shorter events, 0.0 us)
Async XLA Ops:
  153.9 155.1 %copy-start.21 = (bf16[1024]{0:T(1024)(128)(2,1)S(1)}, bf16[1024]{0:T(1024)(128)(2,1)}, u32[]{:S(2)}) copy-start(bf16[1024]{0:T(1024)(128)(2,1)} %param.34) | copy-start | bytes 6148
  309.6 54.9 %copy-start = (f32[128,1024]{1,0:T(8,128)S(1)}, f32[128,1024]{1,0:T(8,128)}, u32[]{:S(2)}) copy-start(f32[128,1024]{1,0:T(8,128)} %refs_8_.1) | copy-start | bytes 1572868
  309.6 54.9 %copy-start.1 = (bf16[512,1024]{1,0:T(8,128)(2,1)S(1)}, bf16[512,1024]{1,0:T(8,128)(2,1)}, u32[]{:S(2)}) copy-start(bf16[512,1024]{1,0:T(8,128)(2,1)} %wd_ref.1) | copy-start | bytes 3145732
  309.6 54.9 %copy-start.2 = (f32[128,1024]{1,0:T(8,128)S(1)}, f32[128,1024]{1,0:T(8,128)}, u32[]{:S(2)}) copy-start(f32[128,1024]{1,0:T(8,128)} %refs_9_.1) | copy-start | bytes 1572868
  309.6 54.9 %copy-start.3 = (f32[128,1024]{1,0:T(8,128)S(1)}, f32[128,1024]{1,0:T(8,128)}, u32[]{:S(2)}) copy-start(f32[128,1024]{1,0:T(8,128)} %refs_10_.1) | copy-start | bytes 1572868
  309.6 54.9 %copy-start.4 = (f32[512,128]{1,0:T(8,128)S(1)}, f32[512,128]{1,0:T(8,128)}, u32[]{:S(2)}) copy-start(f32[512,128]{1,0:T(8,128)} %refs_4_.1) | copy-start | bytes 786436
  309.6 54.9 %copy-start.5 = (f32[128,384]{1,0:T(8,128)S(1)}, f32[128,384]{1,0:T(8,128)}, u32[]{:S(2)}) copy-start(f32[128,384]{1,0:T(8,128)} %refs_0_.1) | copy-start | bytes 589828
  309.6 54.9 %copy-start.6 = (f32[128,128]{1,0:T(8,128)S(1)}, f32[128,128]{1,0:T(8,128)}, u32[]{:S(2)}) copy-start(f32[128,128]{1,0:T(8,128)} %refs_12_.1) | copy-start | bytes 196612
  309.6 54.9 %copy-start.7 = (s32[128,1024]{1,0:T(8,128)S(1)}, s32[128,1024]{1,0:T(8,128)}, u32[]{:S(2)}) copy-start(s32[128,1024]{1,0:T(8,128)} %refs_11_.1) | copy-start | bytes 1572868
  309.6 54.9 %copy-start.9 = (f32[128,128]{1,0:T(8,128)S(1)}, f32[128,128]{1,0:T(8,128)}, u32[]{:S(2)}) copy-start(f32[128,128]{1,0:T(8,128)} %refs_13_.1) | copy-start | bytes 196612
  309.6 54.9 %copy-start.10 = (f32[128,128]{1,0:T(8,128)S(1)}, f32[128,128]{1,0:T(8,128)}, u32[]{:S(2)}) copy-start(f32[128,128]{1,0:T(8,128)} %refs_14_.1) | copy-start | bytes 196612
  309.6 54.9 %copy-start.11 = (f32[512,128]{1,0:T(8,128)S(1)}, f32[512,128]{1,0:T(8,128)}, u32[]{:S(2)}) copy-start(f32[512,128]{1,0:T(8,128)} %refs_5_.1) | copy-start | bytes 786436
  309.6 54.9 %copy-start.12 = (f32[512,128]{1,0:T(8,128)S(1)}, f32[512,128]{1,0:T(8,128)}, u32[]{:S(2)}) copy-start(f32[512,128]{1,0:T(8,128)} %refs_6_.1) | copy-start | bytes 786436
  309.7 54.9 %copy-start.13 = (s32[512,128]{1,0:T(8,128)S(1)}, s32[512,128]{1,0:T(8,128)}, u32[]{:S(2)}) copy-start(s32[512,128]{1,0:T(8,128)} %refs_7_.1) | copy-start | bytes 786436
  309.7 54.9 %copy-start.14 = (f32[128,384]{1,0:T(8,128)S(1)}, f32[128,384]{1,0:T(8,128)}, u32[]{:S(2)}) copy-start(f32[128,384]{1,0:T(8,128)} %refs_1_.1) | copy-start | bytes 589828
  309.7 54.9 %copy-start.15 = (f32[128,384]{1,0:T(8,128)S(1)}, f32[128,384]{1,0:T(8,128)}, u32[]{:S(2)}) copy-start(f32[128,384]{1,0:T(8,128)} %refs_2_.1) | copy-start | bytes 589828
  309.7 54.9 %copy-start.16 = (s32[128,384]{1,0:T(8,128)S(1)}, s32[128,384]{1,0:T(8,128)}, u32[]{:S(2)}) copy-start(s32[128,384]{1,0:T(8,128)} %refs_3_.1) | copy-start | bytes 589828
  309.7 54.9 %copy-start.17 = (s32[128,128]{1,0:T(8,128)S(1)}, s32[128,128]{1,0:T(8,128)}, u32[]{:S(2)}) copy-start(s32[128,128]{1,0:T(8,128)} %refs_15_.1) | copy-start | bytes 196612
  364.6 1.0 copy-start.8
  365.6 5.8 %copy-start.20 = (f32[4,1024]{1,0:T(4,128)S(1)}, f32[4,1024]{1,0:T(4,128)}, u32[]{:S(2)}) copy-start(f32[4,1024]{1,0:T(4,128)} %get-tuple-element.97) | copy-start | bytes 49156
  365.6 6.4 %copy-start.19 = (bf16[3,256,1024]{2,1,0:T(8,128)(2,1)S(1)}, bf16[3,256,1024]{2,1,0:T(8,128)(2,1)}, u32[]{:S(2)}) copy-start(bf16[3,256,1024]{2,1,0:T(8,128)(2,1)} %get-tuple-element.134) | copy-start | bytes 4718596
  372.0 2.0 copy-start.18

commit v7 on v6

--- a/solution.py
+++ b/solution.py
@@ -87,7 +87,7 @@
 MESH = pl.DeviceIdType.MESH
 
 
-def attend_pair(query, keys, values, grad, tables, dk_ref, dv_ref, depth, blocks, store):
+def attend_pair(query, keys, values, grad, tables, dk_ref, dv_ref, depth, blocks, store, block_done):
     lanes = keys.shape[1]
     span = keys.shape[0] // blocks
     scale = 1.0 / math.sqrt(depth)
@@ -141,6 +141,7 @@
         store(i, 0, jnp.concatenate(outs, axis=0).T.astype(bf16))
         dq = jnp.concatenate(grads, axis=0).T * scale
         store(i, 1, turn(dq, *[t[rows] for t in tables], -1.0).astype(bf16))
+        block_done(i)
     for i in range(blocks):
         rows = slice(i * span, (i + 1) * span)
         store(i, 2, turn(dk_ref[rows], *[t[rows] for t in tables], -1.0).astype(bf16))
@@ -341,8 +342,6 @@
 
     grad_own = pltpu.make_async_copy(ga.at[z], g_out.at[:, place_own, :], token_sem.at[1])
     grad_own.start()
-    for t in range(1, n):
-        grad_send(t).start()
 
     def stores(b):
         rows = pl.ds(pl.multiple_of(b * span, span), span)
@@ -407,6 +406,11 @@
         def _():
             ring_wait(s)
             pl.when(s + 1 < n)(lambda: ring_start(s + 1))
+
+        @pl.when(s == 2)
+        def _():
+            for t in range(1, n):
+                grad_send(t).start()
 
         project_near(s - 1)
 
@@ -563,25 +567,23 @@
     if early:
         plane_sum = PlaneSum(e_ref, *plane_refs)
 
+    def pair_place(kind, s):
+        seq, pair = s // pairs, lax.rem(s, pairs)
+        what = slice(2, 4) if kind else slice(0, 2)
+        at = pl.ds(pl.multiple_of((z * pairs + pair) * lanes, lanes), lanes)
+        return what, local_ref.at[seq, what, :, at]
+
+    def own_copy(kind, s):
+        what, target = pair_place(kind, s)
+        return pltpu.make_async_copy(buffer.at[s, z, what], target, own_sem.at[kind, s])
+
+    def away_copy(kind, s, t):
+        what, target = pair_place(kind, s)
+        peer = lax.rem(z + t, n)
+        return remote(buffer.at[s, peer, what], target, send_sem.at[kind, s, t], recv_sem.at[kind, s, t], (dp, peer))
+
     def copies(kind, s):
-        seq, pair = s // pairs, lax.rem(s, pairs)
-        what = slice(1, 4) if kind else slice(0, 1)
-        at = pl.ds(pl.multiple_of((z * pairs + pair) * lanes, lanes), lanes)
-        target = local_ref.at[seq, what, :, at]
-        own = pltpu.make_async_copy(buffer.at[s, z, what], target, own_sem.at[kind, s])
-        away = []
-        for t in range(1, n):
-            peer = lax.rem(z + t, n)
-            away.append(
-                remote(
-                    buffer.at[s, peer, what], target, send_sem.at[kind, s, t], recv_sem.at[kind, s, t], (dp, peer)
-                )
-            )
-        return [own] + away
-
-    def send(kind, s):
-        for copy in copies(kind, s):
-            copy.start()
+        return [own_copy(kind, s)] + [away_copy(kind, s, t) for t in range(1, n)]
 
     def receive(kind):
         for s in range(steps):
@@ -601,10 +603,14 @@
                 own_ref[0, kind - 1, i * value.shape[0] : (i + 1) * value.shape[0], :] = value
 
         tables = keep_ref[...], above_ref[...], below_ref[...]
-        attend_pair(q_ref[0], k_ref[0], v_ref[0], g_ref[0], tables, dk_ref, dv_ref, depth, n, store)
-        send(0, step)
-        pl.when(step == 0)(lambda: send(1, 0))
-        pl.when(step == steps - 2)(lambda: send(1, 1))
+
+        def block_done(i):
+            pl.when(i == z)(lambda: own_copy(0, step).start())
+            pl.when(i != z)(lambda: away_copy(0, step, lax.rem(i - z + n, n)).start())
+
+        attend_pair(
+            q_ref[0], k_ref[0], v_ref[0], g_ref[0], tables, dk_ref, dv_ref, depth, n, store, block_done
+        )
         if early:
             seq, pair = step // pairs, lax.rem(step, pairs)
             mid_t = mid_qkv_ref[0].T
@@ -625,8 +631,10 @@
 
     @pl.when(step == steps)
     def _():
-        for s in range(2, steps):
-            send(1, s)
+        for s in range(steps):
+            own_copy(1, s).start()
+            for t in range(1, n) if s % 2 else range(n - 1, 0, -1):
+                away_copy(1, s, t).start()
         ff_ref[...] = jnp.zeros_like(ff_ref)
         back_ref[...] = jnp.zeros_like(back_ref)
         mid_acc[...] = jnp.zeros_like(mid_acc)

time: 375 us -> 365 us (0.973)
  Pallas kernels: 367 us -> 357 us
    pallas_call x1, Pallas kernels: 155 us -> 148 us  [body(): pl.pallas_call(functools.partial(middle_kernel, n=n, pairs=pairs, steps=s...]
where the time goes in v7:
time: 365 us
  Pallas kernels  357 us (98%)
  local copies, waits for them, and re-layouts  4.87 us (1%)
    pallas_call x1, Pallas kernels, body(): pl.pallas_call(functools.partial(front_kernel, n=n, depth=depth), in_spec...  151 us
    pallas_call x1, Pallas kernels, body(): pl.pallas_call(functools.partial(middle_kernel, n=n, pairs=pairs, steps=s...  148 us
    pallas_call x1, Pallas kernels, body(): pl.pallas_call(functools.partial(tail_kernel, n=n), grid=(2 + n + seqs,),...  52.6 us

profile of v7, /device:TPU:0, one launch (start us, length us, event | category | flops | bytes accessed | tf_op | source)
XLA Modules:
  0.0 364.6 jit_solution(2993614487016359814)
XLA Ops:
  0.7 1.3 reshape.52
  2.0 150.6 %front.1 = (bf16[1024,8192]{1,0:T(8,128)(2,1)}, bf16[4096,1024]{1,0:T(8,128)(2,1)}, bf16[1024,384]{1,0:T(8,128)(2,1)}, bf16[4096,128]{1,0:T(8,128)(2,1)}, bf16[1...) custom-call(bf16[3,256,1024]{2,1,0:T(8,128)(2,1)} %x_ref.1, ...), custom_call_target="tpu_custom_call" | custom-call | tf_op jit(solution)/shard_map/front/pallas_call | solution.py:1113
  152.6 0.0 copy-start.21
  152.6 148.0 %middle.1 = (bf16[3,4,256,1024]{3,2,1,0:T(8,128)(2,1)}, f32[768,1024]{1,0:T(8,128)}, f32[768,1024]{1,0:T(8,128)}, bf16[768,128]{1,0:T(8,128)(2,1)}, bf16[768,128]{1,0:T(8,128)(2,1)}, /*index=5*/bf16[128,2048]{1,0:T(8,128)(2,1)}) custom-call(bf16[3,1024,256]{2,1,0:T(8,128)(2,1)} %get-tuple-element.66.q_ref, bf16[3,1024,256]{2,1,0:T(8,128)(2,1)} %get-tuple-element.67.k_ref, ...), custom_call_target="tpu_custom_call" | custom-call | tf_op jit(solution)/shard_map/middle/pallas_call | solution.py:1371
  300.6 0.0 copy-done.21
  300.6 0.6 reshape.54
  301.2 0.0 copy-start
  301.2 0.0 copy-start.1
  301.2 0.0 copy-start.4
  301.2 0.0 copy-start.5
  301.2 0.0 copy-start.6
  301.2 0.0 copy-start.7
  301.2 0.0 copy-start.9
  301.2 0.0 copy-start.10
  301.3 0.0 copy-start.11
  301.3 0.0 copy-start.12
  301.3 0.0 copy-start.13
  301.3 0.0 copy-start.14
  301.3 0.0 copy-start.15
  301.3 0.0 copy-start.16
  301.3 0.0 copy-start.17
  301.3 52.6 %tail.1 = (bf16[3,256,1024]{2,1,0:T(8,128)(2,1)}, bf16[3,256,1024]{2,1,0:T(8,128)(2,1)}, bf16[128,2048]{1,0:T(8,128)(2,1)}, f32[4,1024]{1,0:T(4,128)}, bf16[8,128,1152]{2,1,0:T(8,128)(2,1)}) custom-call(bf16[3,4,256,1024]{3,2,1,0:T(8,128)(2,1)} %get-tuple-element.87.o_ref.dq_ref.dk_ref.dv_ref, ...), custom_call_target="tpu_custom_call" | custom-call | tf_op jit(solution)/shard_map/tail/pallas_call | solution.py:1412
  353.9 0.0 copy-done
  353.9 0.0 copy-done.1
  354.0 0.0 copy-done.2
  354.0 0.0 copy-done.3
  354.0 0.0 copy-done.4
  354.0 0.0 copy-done.5
  354.0 0.0 copy-done.6
  354.0 0.0 copy-done.7
  354.0 0.0 copy-done.9
  354.0 0.0 copy-done.10
  354.0 0.0 copy-done.11
  354.0 0.0 copy-done.12
  354.1 0.0 copy-done.13
  354.1 0.0 copy-done.14
  354.1 0.0 copy-done.15
  354.1 0.0 copy-done.16
  354.1 0.0 copy-done.17
  354.1 0.0 copy-start.8
  354.1 1.0 copy-done.8
  355.2 5.8 %update.1 = (f32[128,384]{1,0:T(8,128)}, f32[512,128]{1,0:T(8,128)}, f32[128,1024]{1,0:T(8,128)}, f32[128,128]{1,0:T(8,128)}, f32[128,384]{1,0:T(8,128)}, /*inde...) custom-call(bf16[128,2048]{1,0:T(8,128)(2,1)S(1)} %copy-done.8, ...), custom_call_target="tpu_custom_call" | custom-call | tf_op jit(solution)/shard_map/update/pallas_call | solution.py:1594
  360.9 0.0 copy-done.20
  360.9 0.6 fusion
  361.5 0.0 copy-done.19
  361.5 1.1 copy.47
  362.7 0.8 copy-done.18
  363.5 1.1 copy.48
  (5 shorter events, 0.0 us)
Async XLA Ops:
  152.6 148.0 %copy-start.21 = (bf16[1024]{0:T(1024)(128)(2,1)S(1)}, bf16[1024]{0:T(1024)(128)(2,1)}, u32[]{:S(2)}) copy-start(bf16[1024]{0:T(1024)(128)(2,1)} %param.34) | copy-start | bytes 6148
  301.2 52.8 %copy-start = (f32[128,1024]{1,0:T(8,128)S(1)}, f32[128,1024]{1,0:T(8,128)}, u32[]{:S(2)}) copy-start(f32[128,1024]{1,0:T(8,128)} %refs_8_.1) | copy-start | bytes 1572868
  301.2 52.8 %copy-start.1 = (bf16[512,1024]{1,0:T(8,128)(2,1)S(1)}, bf16[512,1024]{1,0:T(8,128)(2,1)}, u32[]{:S(2)}) copy-start(bf16[512,1024]{1,0:T(8,128)(2,1)} %wd_ref.1) | copy-start | bytes 3145732
  301.2 52.8 %copy-start.2 = (f32[128,1024]{1,0:T(8,128)S(1)}, f32[128,1024]{1,0:T(8,128)}, u32[]{:S(2)}) copy-start(f32[128,1024]{1,0:T(8,128)} %refs_9_.1) | copy-start | bytes 1572868
  301.2 52.8 %copy-start.3 = (f32[128,1024]{1,0:T(8,128)S(1)}, f32[128,1024]{1,0:T(8,128)}, u32[]{:S(2)}) copy-start(f32[128,1024]{1,0:T(8,128)} %refs_10_.1) | copy-start | bytes 1572868
  301.2 52.8 %copy-start.4 = (f32[512,128]{1,0:T(8,128)S(1)}, f32[512,128]{1,0:T(8,128)}, u32[]{:S(2)}) copy-start(f32[512,128]{1,0:T(8,128)} %refs_4_.1) | copy-start | bytes 786436
  301.2 52.8 %copy-start.5 = (f32[128,384]{1,0:T(8,128)S(1)}, f32[128,384]{1,0:T(8,128)}, u32[]{:S(2)}) copy-start(f32[128,384]{1,0:T(8,128)} %refs_0_.1) | copy-start | bytes 589828
  301.2 52.8 %copy-start.6 = (f32[128,128]{1,0:T(8,128)S(1)}, f32[128,128]{1,0:T(8,128)}, u32[]{:S(2)}) copy-start(f32[128,128]{1,0:T(8,128)} %refs_12_.1) | copy-start | bytes 196612
  301.2 52.8 %copy-start.7 = (s32[128,1024]{1,0:T(8,128)S(1)}, s32[128,1024]{1,0:T(8,128)}, u32[]{:S(2)}) copy-start(s32[128,1024]{1,0:T(8,128)} %refs_11_.1) | copy-start | bytes 1572868
  301.2 52.8 %copy-start.9 = (f32[128,128]{1,0:T(8,128)S(1)}, f32[128,128]{1,0:T(8,128)}, u32[]{:S(2)}) copy-start(f32[128,128]{1,0:T(8,128)} %refs_13_.1) | copy-start | bytes 196612
  301.2 52.8 %copy-start.10 = (f32[128,128]{1,0:T(8,128)S(1)}, f32[128,128]{1,0:T(8,128)}, u32[]{:S(2)}) copy-start(f32[128,128]{1,0:T(8,128)} %refs_14_.1) | copy-start | bytes 196612
  301.3 52.8 %copy-start.11 = (f32[512,128]{1,0:T(8,128)S(1)}, f32[512,128]{1,0:T(8,128)}, u32[]{:S(2)}) copy-start(f32[512,128]{1,0:T(8,128)} %refs_5_.1) | copy-start | bytes 786436
  301.3 52.8 %copy-start.12 = (f32[512,128]{1,0:T(8,128)S(1)}, f32[512,128]{1,0:T(8,128)}, u32[]{:S(2)}) copy-start(f32[512,128]{1,0:T(8,128)} %refs_6_.1) | copy-start | bytes 786436
  301.3 52.8 %copy-start.13 = (s32[512,128]{1,0:T(8,128)S(1)}, s32[512,128]{1,0:T(8,128)}, u32[]{:S(2)}) copy-start(s32[512,128]{1,0:T(8,128)} %refs_7_.1) | copy-start | bytes 786436
  301.3 52.8 %copy-start.14 = (f32[128,384]{1,0:T(8,128)S(1)}, f32[128,384]{1,0:T(8,128)}, u32[]{:S(2)}) copy-start(f32[128,384]{1,0:T(8,128)} %refs_1_.1) | copy-start | bytes 589828
  301.3 52.8 %copy-start.15 = (f32[128,384]{1,0:T(8,128)S(1)}, f32[128,384]{1,0:T(8,128)}, u32[]{:S(2)}) copy-start(f32[128,384]{1,0:T(8,128)} %refs_2_.1) | copy-start | bytes 589828
  301.3 52.8 %copy-start.16 = (s32[128,384]{1,0:T(8,128)S(1)}, s32[128,384]{1,0:T(8,128)}, u32[]{:S(2)}) copy-start(s32[128,384]{1,0:T(8,128)} %refs_3_.1) | copy-start | bytes 589828
  301.3 52.8 %copy-start.17 = (s32[128,128]{1,0:T(8,128)S(1)}, s32[128,128]{1,0:T(8,128)}, u32[]{:S(2)}) copy-start(s32[128,128]{1,0:T(8,128)} %refs_15_.1) | copy-start | bytes 196612
  354.1 1.0 copy-start.8
  355.1 5.8 %copy-start.20 = (f32[4,1024]{1,0:T(4,128)S(1)}, f32[4,1024]{1,0:T(4,128)}, u32[]{:S(2)}) copy-start(f32[4,1024]{1,0:T(4,128)} %get-tuple-element.97) | copy-start | bytes 49156
  355.1 6.4 %copy-start.19 = (bf16[3,256,1024]{2,1,0:T(8,128)(2,1)S(1)}, bf16[3,256,1024]{2,1,0:T(8,128)(2,1)}, u32[]{:S(2)}) copy-start(bf16[3,256,1024]{2,1,0:T(8,128)(2,1)} %get-tuple-element.134) | copy-start | bytes 4718596
  361.5 2.0 copy-start.18

commit v8 on v7

--- a/solution.py
+++ b/solution.py
@@ -245,29 +245,35 @@
             for kind in (2, 4, 5, 6):
                 hop(i, kind).wait_recv()
 
-    def rightward(s):
-        return remote(x_all.at[z - s + 1], x_all.at[z - s + 1], sr.at[s], qr.at[s], (dp, z + 1))
-
-    def leftward(s):
-        return remote(x_all.at[z + s - 1], x_all.at[z + s - 1], sl.at[s], ql.at[s], (dp, z - 1))
-
-    def from_left(s):
-        return remote(x_all.at[z - s], x_all.at[z - s], sr.at[s], qr.at[s], (dp, z - 1))
-
-    def from_right(s):
-        return remote(x_all.at[z + s], x_all.at[z + s], sl.at[s], ql.at[s], (dp, z + 1))
+    def token_hop(block, q, send, recv, s, to):
+        return remote(x_all.at[block, q], x_all.at[block, q], send.at[s, q], recv.at[s, q], (dp, to))
+
+    def rightward(s, q):
+        return token_hop(z - s + 1, q, sr, qr, s, z + 1)
+
+    def leftward(s, q):
+        return token_hop(z + s - 1, q, sl, ql, s, z - 1)
+
+    def from_left(s, q):
+        return token_hop(z - s, q, sr, qr, s, z - 1)
+
+    def from_right(s, q):
+        return token_hop(z + s, q, sl, ql, s, z + 1)
 
     def ring_start(s):
-        pl.when((z < n - 1) & (z - s + 1 >= 0))(lambda: rightward(s).start())
-        pl.when((z > 0) & (z + s - 1 < n))(lambda: leftward(s).start())
+        for q in range(seqs):
+            pl.when((z < n - 1) & (z - s + 1 >= 0))(lambda q=q: rightward(s, q).start())
+            pl.when((z > 0) & (z + s - 1 < n))(lambda q=q: leftward(s, q).start())
 
     def ring_wait(s):
-        pl.when(z - s >= 0)(lambda: from_left(s).wait_recv())
-        pl.when(z + s < n)(lambda: from_right(s).wait_recv())
+        for q in range(seqs):
+            pl.when(z - s >= 0)(lambda q=q: from_left(s, q).wait_recv())
+            pl.when(z + s < n)(lambda q=q: from_right(s, q).wait_recv())
 
     def ring_end(s):
-        pl.when((z < n - 1) & (z - s + 1 >= 0))(lambda: rightward(s).wait_send())
-        pl.when((z > 0) & (z + s - 1 < n))(lambda: leftward(s).wait_send())
+        for q in range(seqs):
+            pl.when((z < n - 1) & (z - s + 1 >= 0))(lambda q=q: rightward(s, q).wait_send())
+            pl.when((z > 0) & (z + s - 1 < n))(lambda q=q: leftward(s, q).wait_send())
 
     for low, values in ((a_ref, a_wide), (aff_ref, aff_wide), (b_ref, b_wide), (bff_ref, bff_wide)):
         low[...] = values[...].astype(bf16)
@@ -356,6 +362,8 @@
         rows = pl.ds(pl.multiple_of(b * span, span), span)
 
         def one(q, _):
+            pl.when(b == z - n + 1)(lambda: from_left(n - 1, q).wait_recv())
+            pl.when(b == z + n - 1)(lambda: from_right(n - 1, q).wait_recv())
             first = (normal(x_all[b, q].astype(f32)) * gain_ref[0:1] + shift_ref[0:1]).astype(bf16)
             mid = nn(first, a_v[:, 0:rank]).astype(bf16)
             first_s[q, rows, :] = first
@@ -402,10 +410,10 @@
             pass_on(1)
             start_own(2)
 
-        @pl.when((s > 1) & (s < n))
+        @pl.when((s > 1) & (s < n - 1))
         def _():
             ring_wait(s)
-            pl.when(s + 1 < n)(lambda: ring_start(s + 1))
+            ring_start(s + 1)
 
         @pl.when(s == 2)
         def _():
@@ -1143,7 +1151,7 @@
                 pltpu.VMEM((rank, 8 * width), bf16),
                 pltpu.VMEM((rank, width), bf16),
                 dma((7, 7)), dma((7, 7)), dma((7,)),
-                dma((n,)), dma((n,)), dma((n,)), dma((n,)), dma((n,)), dma((n,)),
+                dma((n, seqs)), dma((n, seqs)), dma((n, seqs)), dma((n, seqs)), dma((n,)), dma((n,)),
                 dma((7,)), dma((5, n)), dma((2,)),
             ],
             compiler_params=pltpu.CompilerParams(

time: 365 us -> 371 us (1.016)
  Pallas kernels: 357 us -> 362 us
    pallas_call x1, Pallas kernels: 52.6 us -> 60.2 us  [body(): pl.pallas_call(functools.partial(tail_kernel, n=n), grid=(2 + n + seqs,),...]
where the time goes in v8:
time: 371 us; the launch traced here: 370 us
  Pallas kernels  362 us (98%)
  local copies, waits for them, and re-layouts  4.87 us (1%)
    pallas_call x1, Pallas kernels, body(): pl.pallas_call(functools.partial(front_kernel, n=n, depth=depth), in_spec...  149 us
    pallas_call x1, Pallas kernels, body(): pl.pallas_call(functools.partial(middle_kernel, n=n, pairs=pairs, steps=s...  148 us
    pallas_call x1, Pallas kernels, body(): pl.pallas_call(functools.partial(tail_kernel, n=n), grid=(2 + n + seqs,),...  60.2 us

profile of v8, /device:TPU:0, one launch (start us, length us, event | category | flops | bytes accessed | tf_op | source)
XLA Modules:
  0.0 370.2 jit_solution(1260121433038098017)
XLA Ops:
  0.7 1.3 reshape.52
  2.0 148.6 %front.1 = (bf16[1024,8192]{1,0:T(8,128)(2,1)}, bf16[4096,1024]{1,0:T(8,128)(2,1)}, bf16[1024,384]{1,0:T(8,128)(2,1)}, bf16[4096,128]{1,0:T(8,128)(2,1)}, bf16[1...) custom-call(bf16[3,256,1024]{2,1,0:T(8,128)(2,1)} %x_ref.1, ...), custom_call_target="tpu_custom_call" | custom-call | tf_op jit(solution)/shard_map/front/pallas_call | solution.py:1121
  150.6 0.0 copy-start.21
  150.6 147.9 %middle.1 = (bf16[3,4,256,1024]{3,2,1,0:T(8,128)(2,1)}, f32[768,1024]{1,0:T(8,128)}, f32[768,1024]{1,0:T(8,128)}, bf16[768,128]{1,0:T(8,128)(2,1)}, bf16[768,128]{1,0:T(8,128)(2,1)}, /*index=5*/bf16[128,2048]{1,0:T(8,128)(2,1)}) custom-call(bf16[3,1024,256]{2,1,0:T(8,128)(2,1)} %get-tuple-element.66.q_ref, bf16[3,1024,256]{2,1,0:T(8,128)(2,1)} %get-tuple-element.67.k_ref, ...), custom_call_target="tpu_custom_call" | custom-call | tf_op jit(solution)/shard_map/middle/pallas_call | solution.py:1379
  298.5 0.0 copy-done.21
  298.5 0.6 reshape.54
  299.1 0.0 copy-start.1
  299.1 0.0 copy-start.2
  299.1 0.0 copy-start.4
  299.1 0.0 copy-start.5
  299.1 0.0 copy-start.6
  299.1 0.0 copy-start.7
  299.2 0.0 copy-start.9
  299.2 0.0 copy-start.10
  299.2 0.0 copy-start.11
  299.2 0.0 copy-start.12
  299.2 0.0 copy-start.13
  299.2 0.0 copy-start.14
  299.2 0.0 copy-start.15
  299.2 0.0 copy-start.16
  299.2 0.0 copy-start.17
  299.3 60.2 %tail.1 = (bf16[3,256,1024]{2,1,0:T(8,128)(2,1)}, bf16[3,256,1024]{2,1,0:T(8,128)(2,1)}, bf16[128,2048]{1,0:T(8,128)(2,1)}, f32[4,1024]{1,0:T(4,128)}, bf16[8,128,1152]{2,1,0:T(8,128)(2,1)}) custom-call(bf16[3,4,256,1024]{3,2,1,0:T(8,128)(2,1)} %get-tuple-element.87.o_ref.dq_ref.dk_ref.dv_ref, ...), custom_call_target="tpu_custom_call" | custom-call | tf_op jit(solution)/shard_map/tail/pallas_call | solution.py:1420
  359.5 0.0 copy-done
  359.5 0.0 copy-done.1
  359.5 0.0 copy-done.2
  359.5 0.0 copy-done.3
  359.5 0.0 copy-done.4
  359.5 0.0 copy-done.5
  359.5 0.0 copy-done.6
  359.5 0.0 copy-done.7
  359.5 0.0 copy-done.9
  359.6 0.0 copy-done.10
  359.6 0.0 copy-done.11
  359.6 0.0 copy-done.12
  359.6 0.0 copy-done.13
  359.6 0.0 copy-done.14
  359.6 0.0 copy-done.15
  359.6 0.0 copy-done.16
  359.6 0.0 copy-done.17
  359.6 0.0 copy-start.8
  359.6 1.0 copy-done.8
  360.7 5.8 %update.1 = (f32[128,384]{1,0:T(8,128)}, f32[512,128]{1,0:T(8,128)}, f32[128,1024]{1,0:T(8,128)}, f32[128,128]{1,0:T(8,128)}, f32[128,384]{1,0:T(8,128)}, /*inde...) custom-call(bf16[128,2048]{1,0:T(8,128)(2,1)S(1)} %copy-done.8, ...), custom_call_target="tpu_custom_call" | custom-call | tf_op jit(solution)/shard_map/update/pallas_call | solution.py:1602
  366.4 0.0 copy-done.20
  366.4 0.6 fusion
  367.1 0.0 copy-done.19
  367.1 1.1 copy.47
  368.2 0.8 copy-done.18
  369.0 1.1 copy.48
  (5 shorter events, 0.0 us)
Async XLA Ops:
  150.6 147.9 %copy-start.21 = (bf16[1024]{0:T(1024)(128)(2,1)S(1)}, bf16[1024]{0:T(1024)(128)(2,1)}, u32[]{:S(2)}) copy-start(bf16[1024]{0:T(1024)(128)(2,1)} %param.34) | copy-start | bytes 6148
  299.1 60.4 %copy-start = (f32[128,1024]{1,0:T(8,128)S(1)}, f32[128,1024]{1,0:T(8,128)}, u32[]{:S(2)}) copy-start(f32[128,1024]{1,0:T(8,128)} %refs_8_.1) | copy-start | bytes 1572868
  299.1 60.4 %copy-start.1 = (bf16[512,1024]{1,0:T(8,128)(2,1)S(1)}, bf16[512,1024]{1,0:T(8,128)(2,1)}, u32[]{:S(2)}) copy-start(bf16[512,1024]{1,0:T(8,128)(2,1)} %wd_ref.1) | copy-start | bytes 3145732
  299.1 60.4 %copy-start.2 = (f32[128,1024]{1,0:T(8,128)S(1)}, f32[128,1024]{1,0:T(8,128)}, u32[]{:S(2)}) copy-start(f32[128,1024]{1,0:T(8,128)} %refs_9_.1) | copy-start | bytes 1572868
  299.1 60.4 %copy-start.3 = (f32[128,1024]{1,0:T(8,128)S(1)}, f32[128,1024]{1,0:T(8,128)}, u32[]{:S(2)}) copy-start(f32[128,1024]{1,0:T(8,128)} %refs_10_.1) | copy-start | bytes 1572868
  299.1 60.4 %copy-start.4 = (f32[512,128]{1,0:T(8,128)S(1)}, f32[512,128]{1,0:T(8,128)}, u32[]{:S(2)}) copy-start(f32[512,128]{1,0:T(8,128)} %refs_4_.1) | copy-start | bytes 786436
  299.1 60.4 %copy-start.5 = (f32[128,384]{1,0:T(8,128)S(1)}, f32[128,384]{1,0:T(8,128)}, u32[]{:S(2)}) copy-start(f32[128,384]{1,0:T(8,128)} %refs_0_.1) | copy-start | bytes 589828
  299.1 60.4 %copy-start.6 = (f32[128,128]{1,0:T(8,128)S(1)}, f32[128,128]{1,0:T(8,128)}, u32[]{:S(2)}) copy-start(f32[128,128]{1,0:T(8,128)} %refs_12_.1) | copy-start | bytes 196612
  299.1 60.4 %copy-start.7 = (s32[128,1024]{1,0:T(8,128)S(1)}, s32[128,1024]{1,0:T(8,128)}, u32[]{:S(2)}) copy-start(s32[128,1024]{1,0:T(8,128)} %refs_11_.1) | copy-start | bytes 1572868
  299.2 60.4 %copy-start.9 = (f32[128,128]{1,0:T(8,128)S(1)}, f32[128,128]{1,0:T(8,128)}, u32[]{:S(2)}) copy-start(f32[128,128]{1,0:T(8,128)} %refs_13_.1) | copy-start | bytes 196612
  299.2 60.4 %copy-start.10 = (f32[128,128]{1,0:T(8,128)S(1)}, f32[128,128]{1,0:T(8,128)}, u32[]{:S(2)}) copy-start(f32[128,128]{1,0:T(8,128)} %refs_14_.1) | copy-start | bytes 196612
  299.2 60.4 %copy-start.11 = (f32[512,128]{1,0:T(8,128)S(1)}, f32[512,128]{1,0:T(8,128)}, u32[]{:S(2)}) copy-start(f32[512,128]{1,0:T(8,128)} %refs_5_.1) | copy-start | bytes 786436
  299.2 60.4 %copy-start.12 = (f32[512,128]{1,0:T(8,128)S(1)}, f32[512,128]{1,0:T(8,128)}, u32[]{:S(2)}) copy-start(f32[512,128]{1,0:T(8,128)} %refs_6_.1) | copy-start | bytes 786436
  299.2 60.4 %copy-start.13 = (s32[512,128]{1,0:T(8,128)S(1)}, s32[512,128]{1,0:T(8,128)}, u32[]{:S(2)}) copy-start(s32[512,128]{1,0:T(8,128)} %refs_7_.1) | copy-start | bytes 786436
  299.2 60.4 %copy-start.14 = (f32[128,384]{1,0:T(8,128)S(1)}, f32[128,384]{1,0:T(8,128)}, u32[]{:S(2)}) copy-start(f32[128,384]{1,0:T(8,128)} %refs_1_.1) | copy-start | bytes 589828
  299.2 60.4 %copy-start.15 = (f32[128,384]{1,0:T(8,128)S(1)}, f32[128,384]{1,0:T(8,128)}, u32[]{:S(2)}) copy-start(f32[128,384]{1,0:T(8,128)} %refs_2_.1) | copy-start | bytes 589828
  299.2 60.4 %copy-start.16 = (s32[128,384]{1,0:T(8,128)S(1)}, s32[128,384]{1,0:T(8,128)}, u32[]{:S(2)}) copy-start(s32[128,384]{1,0:T(8,128)} %refs_3_.1) | copy-start | bytes 589828
  299.2 60.4 %copy-start.17 = (s32[128,128]{1,0:T(8,128)S(1)}, s32[128,128]{1,0:T(8,128)}, u32[]{:S(2)}) copy-start(s32[128,128]{1,0:T(8,128)} %refs_15_.1) | copy-start | bytes 196612
  359.6 1.0 copy-start.8
  360.7 5.8 %copy-start.20 = (f32[4,1024]{1,0:T(4,128)S(1)}, f32[4,1024]{1,0:T(4,128)}, u32[]{:S(2)}) copy-start(f32[4,1024]{1,0:T(4,128)} %get-tuple-element.97) | copy-start | bytes 49156
  360.7 6.4 %copy-start.19 = (bf16[3,256,1024]{2,1,0:T(8,128)(2,1)S(1)}, bf16[3,256,1024]{2,1,0:T(8,128)(2,1)}, u32[]{:S(2)}) copy-start(bf16[3,256,1024]{2,1,0:T(8,128)(2,1)} %get-tuple-element.134) | copy-start | bytes 4718596
  367.1 2.0 copy-start.18
